TPU v7x, 512 devices: a whole 4x8x8 slice. The times are simulated.
512 devices in a mesh: ctx: 128 (over z, y, core), head: 4 (over x).
Axes of the slice: x: 4, y: 8, z: 8, core: 2. Of those that a mesh axis runs over, the one named last changes fastest.
Arguments:
- query_rows: bfloat16 [65536, 1536], P(('ctx', 'head')), may hold values from -51 to 51
- key_rows: bfloat16 [65536, 1536], P(('ctx', 'head')), may hold values from -6 to 6
- value_rows: bfloat16 [65536, 1536], P(('ctx', 'head')), may hold values from -12 to 12
- residual: bfloat16 [65536, 1536], P(('ctx', 'head')), may hold values from -6 to 6
- levels: int32 [128], P('ctx'), may hold values from 0 to 49
- gate_table: float32 [50, 1536], replicated, may hold values from -4 to 4
- block_mask: int32 [128, 7, 4, 4], P('ctx'), may hold values from 0 to 1, as said below
- out_weight: bfloat16 [1536, 1536], P('head'), may hold values from -0.15625 to 0.15625
Outputs:
- mixed: bfloat16 [65536, 1536], P(('ctx', 'head'))
Inputs may be any that keep to these rules, and one draw needn't show every extreme that they name: block_mask[f, s, a, b] = 1 lets query block a of frame f attend key block b of frame f + offset(s); slot 0 is all ones; entries whose frame f + offset(s) lies outside the clip are 0.
All inputs are finite; a program needn't handle non-finite values.
Results may differ from a plain program's by a relative error of at most 0.0065.
Values may be sent and summed in bfloat16 or wider, within the bound.
No kernel may reach another device: no remote copies, remote signals or barrier semaphores. Data moves between devices by JAX's collectives and lax.ppermute only.
A program may use at most 64 MiB of HBM per device.

v0:
```python
import math

import jax
import jax.numpy as jnp
from jax import lax
from jax.sharding import PartitionSpec as P

HEAD_DIM = 128
BLOCK = 128
LOGR = 3


def in_one_piece(arrays, axis, split_dim, concat_dim, along):
    both = jnp.concatenate(arrays, axis=along)
    filled, at, done = (
        lax.all_to_all(both, axis, split_axis=split_dim, concat_axis=concat_dim, tiled=True),
        0,
        [],
    )
    for a in arrays:
        done.append(lax.slice_in_dim(filled, at, at + a.shape[along], axis=along))
        at += a.shape[along]
    return tuple(done)


def from_behind(shard, axis, by):
    length = lax.axis_size(axis)
    pairs = [(i, i + by) for i in range(length) if 0 <= i + by < length]
    return lax.ppermute(shard, axis, pairs)


def cut_along(shard, dim, length):
    dims = shard.shape
    tiles = shard.reshape(*dims[:dim], length, dims[dim] // length, *dims[dim + 1 :])
    return jnp.moveaxis(tiles, dim, 0)


def sum_at_owner(shard, axis, dim):
    length = lax.axis_size(axis)
    tiles = lax.all_to_all(cut_along(shard, dim, length), axis, 0, 0, tiled=True)
    return jnp.sum(tiles.astype(jnp.float32), axis=0)


def expand_blocks(block_rows):
    blocks = block_rows.shape[0]
    broadened = jnp.broadcast_to(block_rows[:, None, :, None], (blocks, BLOCK, blocks, BLOCK))
    return broadened.reshape(blocks * BLOCK, blocks * BLOCK) > 0


def fold_slot(running, queries, key_values, allowed):
    run_max, run_total, run_acc = running
    scores = jnp.einsum("qhd,khd->hqk", queries, key_values[0], preferred_element_type=jnp.float32)
    scores = jnp.where(allowed[None], scores * (1.0 / math.sqrt(HEAD_DIM)), -jnp.inf)
    new_max = jnp.maximum(run_max, jnp.max(scores, axis=2))
    rescale = jnp.exp(run_max - new_max)
    exp_scores = jnp.exp(scores - new_max[:, :, None])
    run_total = run_total * rescale + jnp.sum(exp_scores, axis=2)
    weighted = jnp.einsum(
        "hqk,khd->qhd",
        exp_scores.astype(jnp.bfloat16),
        key_values[1],
        preferred_element_type=jnp.float32,
    )
    run_acc = run_acc * jnp.transpose(rescale)[:, :, None] + weighted
    return (new_max, run_total, run_acc)


def body(query_rows, key_rows, value_rows, residual, levels, gate_table, block_mask, out_weight):
    tok_count = query_rows.shape[0]
    heads_here = query_rows.shape[1] // HEAD_DIM
    shaped = [
        rows.reshape(tok_count, heads_here, HEAD_DIM) for rows in (query_rows, key_rows, value_rows)
    ]
    queries, keys_frame, values_frame = in_one_piece(
        (shaped[0], shaped[1], shaped[2]), "head", 1, 0, 2
    )
    key_values = jnp.stack([keys_frame, values_frame])
    pieces = [key_values] + [None] * (2 * LOGR)
    carried = [key_values, key_values]
    for octave in range(LOGR):
        for polarity in (0, 1):
            stride = 1 if octave == 0 else 2 ** (octave - 1)
            shift_by = stride if polarity == 0 else -stride
            carried[polarity] = from_behind(carried[polarity], "ctx", shift_by)
            pieces[1 + 2 * octave + polarity] = carried[polarity]
    frame_len = queries.shape[0]
    group_heads = queries.shape[1]
    running = (
        jnp.full((group_heads, frame_len), -jnp.inf, jnp.float32),
        jnp.zeros((group_heads, frame_len), jnp.float32),
        jnp.zeros((frame_len, group_heads, HEAD_DIM), jnp.float32),
    )
    for slot_idx in range(2 * LOGR + 1):
        running = fold_slot(
            running, queries, pieces[slot_idx], expand_blocks(block_mask[0, slot_idx])
        )
    attention = (running[2] / jnp.transpose(running[1])[:, :, None]).astype(jnp.bfloat16)
    gate_row = lax.dynamic_index_in_dim(gate_table, levels[0], 0, keepdims=False)
    own_heads = attention.reshape(frame_len, -1)
    projected = sum_at_owner(
        jnp.dot(own_heads, out_weight, preferred_element_type=jnp.float32).astype(jnp.bfloat16),
        "head",
        0,
    )
    return (residual.astype(jnp.float32) + gate_row[None, :] * projected).astype(jnp.bfloat16)


def solution(mesh):
    return jax.shard_map(
        body,
        mesh=mesh,
        in_specs=(
            P(("ctx", "head"), None),
            P(("ctx", "head"), None),
            P(("ctx", "head"), None),
            P(("ctx", "head"), None),
            P("ctx"),
            P(),
            P("ctx", None, None, None),
            P("head", None),
        ),
        out_specs=P(("ctx", "head"), None),
        check_vma=False,
    )
```

profile of v0, /device:TPU:256, one launch (start us, length us, event | category | flops | bytes accessed | tf_op | source)
XLA Modules:
  0.0 128.8 jit_solution(9817615884317277093)
XLA Ops:
  0.0 1.3 %copy.33 = bf16[128,1536]{0,1:T(8,128)(2,1)S(1)} copy(bf16[128,1536]{1,0:T(8,128)(2,1)} %param.10) | data formatting | bytes 786432 | tf_op args[2]
  1.3 1.2 copy.32
  2.5 1.2 copy.31
  3.9 20.6 %all_to_all.23 = bf16[128,12,384]{0,2,1:T(8,128)(2,1)S(1)} all-to-all(bf16[128,12,384]{0,2,1:T(8,128)(2,1)S(1)} %pad_maximum_fusion), channel_id=1, replica_groups=mesh['ctx'=128,'head'=4] {'head'}, dimensions={1} | all-to-all | bytes 2359296 | tf_op jit(solution)/shard_map/all_to_all | solution.py:16
  25.3 1.0 pad_maximum_fusion.1
  26.3 2.8 %collective-permute-start.1 = (bf16[2,512,3,128]{3,1,2,0:T(8,128)(2,1)}, bf16[2,512,3,128]{3,1,2,0:T(8,128)(2,1)}, u32[]{:S(2)}, u32[]{:S(2)}) collective-permute-start(bf16[2,512,3,128]{3,1,2,0:T(8,128)(2,1)} %pad_maximum_fusion.1), channel_id=1, source_target_pairs={{4,0},{8,4},{12,8},{16,12},{20,16},{24,20},{28,24},{32,28},{36,32}... | collective-permute-start | bytes 2359304 | tf_op jit(solution)/shard_map/ppermute | solution.py:29
  29.1 1.9 %collective-permute-start = (bf16[2,512,3,128]{3,1,2,0:T(8,128)(2,1)}, bf16[2,512,3,128]{3,1,2,0:T(8,128)(2,1)}, u32[]{:S(2)}, u32[]{:S(2)}) collective-permute-start(bf16[2,512,3,128]{3,1,2,0:T(8,128)(2,1)} %pad_maximum_fusion.1), channel_id=1, source_target_pairs={{0,4},{4,8},{8,12},{12,16},{16,20},{20,24},{24,28},{28,32},{32,36}... | collective-permute-start | bytes 2359304 | tf_op jit(solution)/shard_map/ppermute | solution.py:29
  38.0 0.9 collective-permute-done.1
  38.9 7.1 %collective-permute-start.3 = (bf16[2,512,3,128]{3,1,2,0:T(8,128)(2,1)}, bf16[2,512,3,128]{3,1,2,0:T(8,128)(2,1)S(1)}, u32[]{:S(2)}, u32[]{:S(2)}) collective-permute-start(bf16[2,512,3,128]{3,1,2,0:T(8,128)(2,1)} %collective-permute-done.1), channel_id=1, source_target_pairs={{4,0},{8,4},{12,8},{16,12},{20,16},{24,20},{28,24},{32,28},{36,32}... | collective-permute-start | bytes 2359304 | tf_op jit(solution)/shard_map/ppermute | solution.py:29
  46.7 1.9 %collective-permute-start.2 = (bf16[2,512,3,128]{3,1,2,0:T(8,128)(2,1)}, bf16[2,512,3,128]{3,1,2,0:T(8,128)(2,1)S(1)}, u32[]{:S(2)}, u32[]{:S(2)}) collective-permute-start(bf16[2,512,3,128]{3,1,2,0:T(8,128)(2,1)} %collective-permute-done), channel_id=1, source_target_pairs={{0,4},{4,8},{8,12},{12,16},{16,20},{20,24},{24,28},{28,32},{32,36}... | collective-permute-start | bytes 2359304 | tf_op jit(solution)/shard_map/ppermute | solution.py:29
  48.7 1.7 %fusion.2 = (f32[3,512]{1,0:T(4,128)S(1)}, f32[3,512,512]{1,2,0:T(8,128)S(1)}) fusion(pred[512,512]{0,1:T(8,128)(4,1)S(1)} %bitcast.316, bf16[2,512,3,128]{3,1,2,0:T(8,128)(2,1)} %collective-permute-done.1, bf16[512,3,384]{2,0,1:T(8,128)(2,1)S(1)} %bitcast.281), kind=kOutput, calls=%fused_computation.18 | convolution fusion | flops 203684352 | bytes 4200448 | tf_op jit(solution)/shard_map/qhd,khd->hqk/dot_general | solution.py:52
  50.4 1.7 %fusion.1 = (f32[3,512]{1,0:T(4,128)S(1)}, f32[3,512,512]{1,2,0:T(8,128)S(1)}) fusion(pred[512,512]{0,1:T(8,128)(4,1)S(1)} %bitcast.291, bf16[2,512,3,128]{3,1,2,0:T(8,128)(2,1)} %collective-permute-done, bf16[512,3,384]{2,0,1:T(8,128)(2,1)S(1)} %bitcast.282), kind=kOutput, calls=%fused_computation.17 | convolution fusion | flops 203684352 | bytes 4200448 | tf_op jit(solution)/shard_map/qhd,khd->hqk/dot_general | solution.py:52
  52.1 3.7 %collective-permute-done.3 = bf16[2,512,3,128]{3,1,2,0:T(8,128)(2,1)S(1)} collective-permute-done((bf16[2,512,3,128]{3,1,2,0:T(8,128)(2,1)}, bf16[2,512,3,128]{3,1,2,0:T(8,128)(2,1)S(1)}, u32[]{:S(2)}, u32[]{:S(2)}) %collective-permute-start.3) | collective-permute-done | bytes 786464 | tf_op jit(solution)/shard_map/ppermute | solution.py:29
  55.8 1.9 %collective-permute-start.5 = (bf16[2,512,3,128]{3,1,2,0:T(8,128)(2,1)S(1)}, bf16[2,512,3,128]{3,1,2,0:T(8,128)(2,1)S(1)}, u32[]{:S(2)}, u32[]{:S(2)}) collective-permute-start(bf16[2,512,3,128]{3,1,2,0:T(8,128)(2,1)S(1)} %collective-permute-done.3), channel_id=1, source_target_pairs={{8,0},{12,4},{16,8},{20,12},{24,16},{28,20},{32,24},{36,28},{40,32... | collective-permute-start | bytes 2359304 | tf_op jit(solution)/shard_map/ppermute | solution.py:29
  57.7 5.8 %collective-permute-done.2 = bf16[2,512,3,128]{3,1,2,0:T(8,128)(2,1)S(1)} collective-permute-done((bf16[2,512,3,128]{3,1,2,0:T(8,128)(2,1)}, bf16[2,512,3,128]{3,1,2,0:T(8,128)(2,1)S(1)}, u32[]{:S(2)}, u32[]{:S(2)}) %collective-permute-start.2) | collective-permute-done | bytes 786464 | tf_op jit(solution)/shard_map/ppermute | solution.py:29
  63.6 2.1 %collective-permute-start.4 = (bf16[2,512,3,128]{3,1,2,0:T(8,128)(2,1)S(1)}, bf16[2,512,3,128]{3,1,2,0:T(8,128)(2,1)S(1)}, u32[]{:S(2)}, u32[]{:S(2)}) collective-permute-start(bf16[2,512,3,128]{3,1,2,0:T(8,128)(2,1)S(1)} %collective-permute-done.2), channel_id=1, source_target_pairs={{0,8},{4,12},{8,16},{12,20},{16,24},{20,28},{24,32},{28,36},{32,40... | collective-permute-start | bytes 2359304 | tf_op jit(solution)/shard_map/ppermute | solution.py:29
  67.1 8.0 %collective-permute-done.5 = bf16[2,512,3,128]{3,1,2,0:T(8,128)(2,1)S(1)} collective-permute-done((bf16[2,512,3,128]{3,1,2,0:T(8,128)(2,1)S(1)}, bf16[2,512,3,128]{3,1,2,0:T(8,128)(2,1)S(1)}, u32[]{:S(2)}, u32[]{:S(2)}) %collective-permute-start.5) | collective-permute-done | bytes 786464 | tf_op jit(solution)/shard_map/ppermute | solution.py:29
  75.8 11.8 %collective-permute-done.4 = bf16[2,512,3,128]{3,1,2,0:T(8,128)(2,1)S(1)} collective-permute-done((bf16[2,512,3,128]{3,1,2,0:T(8,128)(2,1)S(1)}, bf16[2,512,3,128]{3,1,2,0:T(8,128)(2,1)S(1)}, u32[]{:S(2)}, u32[]{:S(2)}) %collective-permute-start.4) | collective-permute-done | bytes 786464 | tf_op jit(solution)/shard_map/ppermute | solution.py:29
  88.4 1.4 %fusion.17 = (f32[3,512]{1,0:T(4,128)S(1)}, f32[3,512]{1,0:T(4,128)S(1)}) fusion(f32[3,512,512]{1,2,0:T(8,128)S(1)} %get-tuple-element.32, f32[3,512]{1,0:T(4,128)S(1)} %get-tuple-element.13, pred[512,512]{0,1:T(8,128)(4,1)S(1)} %bitcast.308, f32[3,512]{1,0:T(4,128)S(1)} %get-tuple-element.12, f32[3,512,512]{1,2,0:T(8,128)S(1)} %get-tuple-element.30, ...), kind=kLoop, calls=%fused_computation.33 | loop fusion | flops 6288384 | bytes 6840320 | tf_op jit(solution)/shard_map/reduce_sum | solution.py:57
  89.8 1.4 %fusion.13 = (f32[3,512]{1,0:T(4,128)S(1)}, f32[3,512]{1,0:T(4,128)S(1)}) fusion(f32[3,512,512]{1,2,0:T(8,128)S(1)} %get-tuple-element.36, f32[3,512]{1,0:T(4,128)S(1)} %get-tuple-element.15, pred[512,512]{0,1:T(8,128)(4,1)S(1)} %bitcast.289, f32[3,512]{1,0:T(4,128)S(1)} %get-tuple-element.14, f32[3,512,512]{1,2,0:T(8,128)S(1)} %get-tuple-element.34, ...), kind=kLoop, calls=%fused_computation.29 | loop fusion | flops 6288384 | bytes 6840320 | tf_op jit(solution)/shard_map/reduce_sum | solution.py:57
  91.2 1.4 %fusion.9 = (f32[3,512]{1,0:T(4,128)S(1)}, f32[3,512]{1,0:T(4,128)S(1)}) fusion(f32[3,512,512]{1,2,0:T(8,128)S(1)} %get-tuple-element.42, f32[3,512]{1,0:T(4,128)S(1)} %get-tuple-element.17, pred[512,512]{0,1:T(8,128)(4,1)S(1)} %bitcast.292, f32[3,512]{1,0:T(4,128)S(1)} %get-tuple-element.16, f32[3,512,512]{1,2,0:T(8,128)S(1)} %get-tuple-element.38, ...), kind=kLoop, calls=%fused_computation.25 | loop fusion | flops 6288384 | bytes 6840320 | tf_op jit(solution)/shard_map/reduce_sum | solution.py:57
  92.6 1.0 fusion.105
  93.7 1.0 fusion.93
  94.7 1.0 fusion.84
  95.7 2.0 %fusion.75 = f32[512,3,128]{0,2,1:T(8,128)S(1)} fusion(f32[3,512,512]{1,2,0:T(8,128)S(1)} %get-tuple-element.38, f32[3,512]{1,0:T(4,128)S(1)} %get-tuple-element.16, pred[512,512]{0,1:T(8,128)(4,1)S(1)} %bitcast.318, bf16[2,512,3,128]{3,1,2,0:T(8,128)(2,1)} %collective-permute-done.1), kind=kOutput, calls=%fused_computation.76 | convolution fusion | flops 204472320 | bytes 4593664 | tf_op jit(solution)/shard_map/hqk,khd->qhd/dot_general | solution.py:58
  97.7 2.1 %fusion.111 = f32[512,3,128]{0,2,1:T(8,128)S(1)} fusion(f32[512,3,128]{0,2,1:T(8,128)S(1)} %fusion.75, f32[512,3,128]{0,2,1:T(8,128)S(1)} %fusion.105, f32[3,512,512]{1,2,0:T(8,128)S(1)} %get-tuple-element.42, f32[3,512]{1,0:T(4,128)S(1)} %get-tuple-element.17, pred[512,512]{0,1:T(8,128)(4,1)S(1)} %bitcast.293, ...), kind=kOutput, calls=%fused_computation.88 | convolution fusion | flops 205258752 | bytes 6178816 | tf_op jit(solution)/shard_map/hqk,khd->qhd/dot_general | solution.py:58
  99.8 1.3 fusion.117
  101.1 1.1 fusion.126
  102.2 2.2 %convolution_convert_fusion = bf16[512,1536]{1,0:T(8,128)(2,1)} fusion(bf16[512,384]{0,1:T(8,128)(2,1)S(1)} %bitcast.319, bf16[384,1536]{1,0:T(8,128)(2,1)S(1)} %copy-done), kind=kOutput, calls=%fused_computation.15 | convolution fusion | flops 604766208 | bytes 3145728 | tf_op jit(solution)/shard_map/dot_general | solution.py:101
  104.3 3.7 %all-to-all-start.1 = ((bf16[4,128,1536]{2,1,0:T(8,128)(2,1)}), bf16[4,128,1536]{2,1,0:T(8,128)(2,1)S(1)}, u32[]{:S(2)}, u32[]{:S(2)}) async-start(bf16[4,128,1536]{2,1,0:T(8,128)(2,1)} %bitcast.277), calls=%async_computation.1 | async-start | bytes 3145728 | tf_op jit(solution)/shard_map/all_to_all | solution.py:40
  109.5 18.2 %all-to-all-done.1 = bf16[4,128,1536]{2,1,0:T(8,128)(2,1)S(1)} async-done(((bf16[4,128,1536]{2,1,0:T(8,128)(2,1)}), bf16[4,128,1536]{2,1,0:T(8,128)(2,1)S(1)}, u32[]{:S(2)}, u32[]{:S(2)}) %all-to-all-start.1) | async-done | bytes 1572896 | tf_op jit(solution)/shard_map/all_to_all | solution.py:40
  127.9 0.9 add_convert_fusion
  (51 shorter events, 12.5 us)
Async XLA Ops:
  0.0 102.1 %copy-start = (bf16[384,1536]{1,0:T(8,128)(2,1)S(1)}, bf16[384,1536]{1,0:T(8,128)(2,1)}, u32[]{:S(2)}) copy-start(bf16[384,1536]{1,0:T(8,128)(2,1)} %param.15) | copy-start | bytes 3538948
  24.4 6.5 %copy-start.5 = (s32[1,7,4,4]{1,3,2,0:T(4,128)S(1)}, s32[1,7,4,4]{1,3,2,0:T(4,128)}, u32[]{:S(2)}) copy-start(s32[1,7,4,4]{1,3,2,0:T(4,128)} %param.14) | copy-start | bytes 1348
  26.3 12.6 %collective-permute-start.1 = (bf16[2,512,3,128]{3,1,2,0:T(8,128)(2,1)}, bf16[2,512,3,128]{3,1,2,0:T(8,128)(2,1)}, u32[]{:S(2)}, u32[]{:S(2)}) collective-permute-start(bf16[2,512,3,128]{3,1,2,0:T(8,128)(2,1)} %pad_maximum_fusion.1), channel_id=1, source_target_pairs={{4,0},{8,4},{12,8},{16,12},{20,16},{24,20},{28,24},{32,28},{36,32}... | collective-permute-start | bytes 2359304 | tf_op jit(solution)/shard_map/ppermute | solution.py:29
  29.1 17.7 %collective-permute-start = (bf16[2,512,3,128]{3,1,2,0:T(8,128)(2,1)}, bf16[2,512,3,128]{3,1,2,0:T(8,128)(2,1)}, u32[]{:S(2)}, u32[]{:S(2)}) collective-permute-start(bf16[2,512,3,128]{3,1,2,0:T(8,128)(2,1)} %pad_maximum_fusion.1), channel_id=1, source_target_pairs={{0,4},{4,8},{8,12},{12,16},{16,20},{20,24},{24,28},{28,32},{32,36}... | collective-permute-start | bytes 2359304 | tf_op jit(solution)/shard_map/ppermute | solution.py:29
  37.3 11.4 %copy-start.4 = (pred[64,8,4,128]{3,1,2,0:T(8,128)(4,1)S(1)}, pred[64,8,4,128]{3,1,2,0:T(8,128)(4,1)}, u32[]{:S(2)}) copy-start(pred[64,8,4,128]{3,1,2,0:T(8,128)(4,1)} %copy.96) | copy-start | bytes 786436
  38.9 16.9 %collective-permute-start.3 = (bf16[2,512,3,128]{3,1,2,0:T(8,128)(2,1)}, bf16[2,512,3,128]{3,1,2,0:T(8,128)(2,1)S(1)}, u32[]{:S(2)}, u32[]{:S(2)}) collective-permute-start(bf16[2,512,3,128]{3,1,2,0:T(8,128)(2,1)} %collective-permute-done.1), channel_id=1, source_target_pairs={{4,0},{8,4},{12,8},{16,12},{20,16},{24,20},{28,24},{32,28},{36,32}... | collective-permute-start | bytes 2359304 | tf_op jit(solution)/shard_map/ppermute | solution.py:29
  46.7 16.8 %collective-permute-start.2 = (bf16[2,512,3,128]{3,1,2,0:T(8,128)(2,1)}, bf16[2,512,3,128]{3,1,2,0:T(8,128)(2,1)S(1)}, u32[]{:S(2)}, u32[]{:S(2)}) collective-permute-start(bf16[2,512,3,128]{3,1,2,0:T(8,128)(2,1)} %collective-permute-done), channel_id=1, source_target_pairs={{0,4},{4,8},{8,12},{12,16},{16,20},{20,24},{24,28},{28,32},{32,36}... | collective-permute-start | bytes 2359304 | tf_op jit(solution)/shard_map/ppermute | solution.py:29
  50.4 15.3 %copy-start.3 = (pred[64,8,4,128]{3,1,2,0:T(8,128)(4,1)S(1)}, pred[64,8,4,128]{3,1,2,0:T(8,128)(4,1)}, u32[]{:S(2)}) copy-start(pred[64,8,4,128]{3,1,2,0:T(8,128)(4,1)} %copy.94) | copy-start | bytes 786436
  55.8 19.3 %collective-permute-start.5 = (bf16[2,512,3,128]{3,1,2,0:T(8,128)(2,1)S(1)}, bf16[2,512,3,128]{3,1,2,0:T(8,128)(2,1)S(1)}, u32[]{:S(2)}, u32[]{:S(2)}) collective-permute-start(bf16[2,512,3,128]{3,1,2,0:T(8,128)(2,1)S(1)} %collective-permute-done.3), channel_id=1, source_target_pairs={{8,0},{12,4},{16,8},{20,12},{24,16},{28,20},{32,24},{36,28},{40,32... | collective-permute-start | bytes 2359304 | tf_op jit(solution)/shard_map/ppermute | solution.py:29
  63.6 24.1 %collective-permute-start.4 = (bf16[2,512,3,128]{3,1,2,0:T(8,128)(2,1)S(1)}, bf16[2,512,3,128]{3,1,2,0:T(8,128)(2,1)S(1)}, u32[]{:S(2)}, u32[]{:S(2)}) collective-permute-start(bf16[2,512,3,128]{3,1,2,0:T(8,128)(2,1)S(1)} %collective-permute-done.2), channel_id=1, source_target_pairs={{0,8},{4,12},{8,16},{12,20},{16,24},{20,28},{24,32},{28,36},{32,40... | collective-permute-start | bytes 2359304 | tf_op jit(solution)/shard_map/ppermute | solution.py:29
  66.4 8.8 %copy-start.2 = (pred[64,8,4,128]{3,1,2,0:T(8,128)(4,1)S(1)}, pred[64,8,4,128]{3,1,2,0:T(8,128)(4,1)}, u32[]{:S(2)}) copy-start(pred[64,8,4,128]{3,1,2,0:T(8,128)(4,1)} %copy.92) | copy-start | bytes 786436
  67.1 20.5 %copy-start.1 = (pred[64,8,4,128]{3,1,2,0:T(8,128)(4,1)S(1)}, pred[64,8,4,128]{3,1,2,0:T(8,128)(4,1)}, u32[]{:S(2)}) copy-start(pred[64,8,4,128]{3,1,2,0:T(8,128)(4,1)} %copy.93) | copy-start | bytes 786436
  104.3 23.6 %copy-start.6 = (bf16[128,1536]{1,0:T(8,128)(2,1)S(1)}, bf16[128,1536]{1,0:T(8,128)(2,1)}, u32[]{:S(2)}) copy-start(bf16[128,1536]{1,0:T(8,128)(2,1)} %param.11) | copy-start | bytes 1179652
  104.3 23.4 %all-to-all-start.1 = ((bf16[4,128,1536]{2,1,0:T(8,128)(2,1)}), bf16[4,128,1536]{2,1,0:T(8,128)(2,1)S(1)}, u32[]{:S(2)}, u32[]{:S(2)}) async-start(bf16[4,128,1536]{2,1,0:T(8,128)(2,1)} %bitcast.277), calls=%async_computation.1 | async-start | bytes 3145728 | tf_op jit(solution)/shard_map/all_to_all | solution.py:40
where the time goes:
time: 129 us
  waiting for transfers between devices  48.4 us (38%)
  starting transfers between devices  21.4 us (17%)
  blocking collectives  20.6 us (16%)
  matrix products  18.6 us (14%)
  local copies, waits for them, and re-layouts  11.6 us (9%)
  other arithmetic  7.23 us (6%)
    ppermute x6, waiting for transfers between devices, from_behind(): return lax.ppermute(shard, axis, pairs)  30.2 us
    all_to_all x1, blocking collectives, in_one_piece(): lax.all_to_all(both, axis, split_axis=split_dim, concat_axis=concat_dim,...  20.6 us
    all_to_all x1, waiting for transfers between devices, sum_at_owner(): lax.all_to_all(cut_along(shard, dim, length), axis, 0, 0, tiled=True)  18.2 us
    ppermute x6, starting transfers between devices, from_behind(): return lax.ppermute(shard, axis, pairs)  17.7 us
    dot_general x7, matrix products, fold_slot(): jnp.einsum('hqk,khd->qhd', exp_scores.astype(jnp.bfloat16), key_values[1]...  9.45 us
    unnamed x24, local copies, waits for them, and re-layouts  7.52 us
    dot_general x7, matrix products, fold_slot(): jnp.einsum('qhd,khd->hqk', queries, key_values[0], preferred_element_type...  6.93 us
    reduce_sum x4, other arithmetic, fold_slot(): run_total = run_total * rescale + jnp.sum(exp_scores, axis=2)  4.94 us
  transfers between devices with their start and end apart: 7, of which 6 were waited for; matrix products, arithmetic and copies ran while one was open for 11% of the time, Pallas kernels for 0%

commit v1 on v0

v1 whole, which is shorter than its diff:
```python
import math

import jax
import jax.numpy as jnp
from jax import lax
from jax.experimental import pallas as pl
from jax.experimental.pallas import tpu as pltpu
from jax.sharding import PartitionSpec as P


HEAD_DIM = 128
BLOCK = 128
EXP2_SCALE = math.log2(math.e) / math.sqrt(HEAD_DIM)
SMEM = pl.BlockSpec(memory_space=pltpu.SMEM)
VMEM = pl.BlockSpec(memory_space=pltpu.VMEM)


def to_frame(x, source_of):
    count = lax.axis_size("ctx")
    pairs = [(source_of(f), f) for f in range(count) if 0 <= source_of(f) < count]
    return lax.ppermute(x, "ctx", pairs)


def partner(f):
    return f ^ 1


def outward(f):
    return f + 2 if f % 2 == 0 else f - 2


def inward(f):
    return f - 2 if f % 2 == 0 else f + 2


def along_head(x, by):
    size = lax.axis_size("head")
    return lax.ppermute(x, "head", [(i, (i + by) % size) for i in range(size)])


def exchange(pieces):
    return lax.all_to_all(pieces, "head", 0, 0, tiled=True)


def pack_kernel(*refs):
    row_refs, out_ref = refs[:-1], refs[-1]
    for i, rows in enumerate(row_refs):
        for h in range(out_ref.shape[2]):
            out_ref[0, i, h] = rows[:, h * HEAD_DIM : (h + 1) * HEAD_DIM]


def pack(arrays, groups):
    tokens, width = arrays[0].shape
    heads = width // HEAD_DIM // groups
    shape = (groups, len(arrays), heads, tokens, HEAD_DIM)
    return pl.pallas_call(
        pack_kernel,
        grid=(groups,),
        in_specs=[pl.BlockSpec((tokens, width // groups), lambda g: (0, g))] * len(arrays),
        out_specs=pl.BlockSpec((1, *shape[1:]), lambda g: (g, 0, 0, 0, 0)),
        out_shape=jax.ShapeDtypeStruct(shape, arrays[0].dtype),
        name="pack",
    )(*arrays)


def deal_kernel(place_ref, rows_ref, *out_refs):
    groups, heads = len(out_refs), out_refs[0].shape[0]
    for r, out_ref in enumerate(out_refs):
        group = (place_ref[1] + r) % groups
        for h in range(heads):
            at = pl.multiple_of((group * heads + h) * HEAD_DIM, HEAD_DIM)
            out_ref[h] = rows_ref[:, pl.ds(at, HEAD_DIM)]


def deal(place, rows, groups):
    tokens, width = rows.shape
    shape = (width // HEAD_DIM // groups, tokens, HEAD_DIM)
    return pl.pallas_call(
        deal_kernel,
        in_specs=[SMEM, VMEM],
        out_specs=[VMEM] * groups,
        out_shape=[jax.ShapeDtypeStruct(shape, rows.dtype)] * groups,
        name="deal",
    )(place, rows)


def attend_kernel(slots, groups, first, last, place_ref, mask_ref, *refs):
    count = len(slots)
    q_refs, kv_refs, refs = refs[:groups], refs[groups : groups + count], refs[groups + count :]
    rows = groups * BLOCK
    core, x = place_ref[0], place_ref[1]
    queries = jnp.concatenate([q[0] for q in q_refs], axis=0)
    if first:
        outs = refs
    else:
        acc_in, stat_in = refs[:2]
        outs = refs[2:]
    scores = [
        lax.dot_general(
            queries,
            kv[:, 0, 0].reshape(rows, HEAD_DIM),
            (((1,), (1,)), ((), ())),
            preferred_element_type=jnp.float32,
        )
        for kv in kv_refs
    ]
    slot_at = [jnp.where(core == 0, even, odd) * groups * groups for even, odd in slots]
    weights, maxima, totals, rescales = [], [], [], []
    for r in range(groups):
        own = slice(r * BLOCK, (r + 1) * BLOCK)
        q_block = (x + groups - r) % groups
        tiles = []
        for s in range(count):
            for b in range(groups):
                keep = mask_ref[slot_at[s] + q_block * groups + b] > 0
                tile = scores[s][own, b * BLOCK : (b + 1) * BLOCK]
                tiles.append(jnp.where(keep, tile, -jnp.inf))
        peak = tiles[0]
        for tile in tiles[1:]:
            peak = jnp.maximum(peak, tile)
        peak = jnp.max(peak, axis=1, keepdims=True)
        if not first:
            before = stat_in[0, own, 0:1]
            peak = jnp.maximum(peak, before)
            rescale = jnp.exp2((before - peak) * EXP2_SCALE)
        tiles = [jnp.exp2((tile - peak) * EXP2_SCALE) for tile in tiles]
        total = tiles[0]
        for tile in tiles[1:]:
            total = total + tile
        total = jnp.sum(total, axis=1, keepdims=True)
        if not first:
            total = total + stat_in[0, own, 1:2] * rescale
            rescales.append(rescale)
        maxima.append(peak)
        totals.append(total)
        weights.append(jnp.concatenate([t.astype(jnp.bfloat16) for t in tiles], axis=1))
    weights = jnp.concatenate(weights, axis=0)
    values = jnp.concatenate([kv[:, 1, 0].reshape(rows, HEAD_DIM) for kv in kv_refs], axis=0)
    weighted = jnp.dot(weights, values, preferred_element_type=jnp.float32)
    total = jnp.concatenate(totals, axis=0)
    if not first:
        weighted = weighted + acc_in[0] * jnp.concatenate(rescales, axis=0)
    if last:
        attention = (weighted / total).astype(jnp.bfloat16)
        for r in range(groups):
            outs[0][(x + groups - r) % groups, 0] = attention[r * BLOCK : (r + 1) * BLOCK]
    else:
        acc_out, stat_out = outs
        acc_out[0] = weighted
        lane = lax.broadcasted_iota(jnp.int32, (rows, HEAD_DIM), 1)
        stat_out[0] = jnp.where(lane == 0, jnp.concatenate(maxima, axis=0), total)


def attend(slots, place, mask, queries, kvs, state, last):
    groups, (heads, tokens, _) = len(queries), queries[0].shape
    rows = groups * tokens
    q_spec = pl.BlockSpec((1, tokens, HEAD_DIM), lambda h: (h, 0, 0))
    kv_spec = pl.BlockSpec((groups, 2, 1, tokens, HEAD_DIM), lambda h: (0, 0, h, 0, 0))
    state_spec = pl.BlockSpec((1, rows, HEAD_DIM), lambda h: (h, 0, 0))
    state_shape = jax.ShapeDtypeStruct((heads, rows, HEAD_DIM), jnp.float32)
    extra = () if state is None else state
    if last:
        out_shape = jax.ShapeDtypeStruct((groups, heads, tokens, HEAD_DIM), jnp.bfloat16)
        out_specs = pl.BlockSpec((groups, 1, tokens, HEAD_DIM), lambda h: (0, h, 0, 0))
    else:
        out_shape, out_specs = (state_shape, state_shape), (state_spec, state_spec)

    def kernel(*refs):
        attend_kernel(slots, groups, state is None, last, *refs)

    return pl.pallas_call(
        kernel,
        grid=(heads,),
        in_specs=[SMEM, SMEM]
        + [q_spec] * groups
        + [kv_spec] * len(kvs)
        + [state_spec] * len(extra),
        out_specs=out_specs,
        out_shape=out_shape,
    )(place, mask, *queries, *kvs, *extra)


def project_kernel(place_ref, o_ref, w_ref, m1, m2, m3, other_ref, gate_ref, residual_ref, out_ref):
    groups, heads = o_ref.shape[0], o_ref.shape[1]
    core, x = place_ref[0], place_ref[1]
    half = m1.shape[1]
    features = []
    for r in range(groups):
        group = (x + groups - r) % groups
        features.append(jnp.concatenate([o_ref[group, h] for h in range(heads)], axis=1))
    mine = [m1[...], m2[...], m3[...]]
    other = [other_ref[i] for i in range(groups - 1)]
    for column, far in ((core, mine), (1 - core, other)):
        at = pl.ds(pl.multiple_of(column * half, 128), half)
        projected = jnp.dot(features[0], w_ref[:, at], preferred_element_type=jnp.float32)
        for rows, weight in zip(features[1:], far, strict=True):
            projected += jnp.dot(rows, weight, preferred_element_type=jnp.float32)
        mixed = residual_ref[:, at].astype(jnp.float32) + gate_ref[:, at] * projected
        out_ref[:, at] = mixed.astype(jnp.bfloat16)


def project(place, gathered, weight, mine, other, gate, residual):
    return pl.pallas_call(
        project_kernel,
        in_specs=[SMEM] + [VMEM] * 8,
        out_specs=VMEM,
        out_shape=jax.ShapeDtypeStruct(residual.shape, jnp.bfloat16),
        name="project",
    )(place, gathered, weight, *mine, other, gate, residual)


def after(value, *others):
    return lax.optimization_barrier((value, *others))[0]


def body(query_rows, key_rows, value_rows, residual, levels, gate_table, block_mask, out_weight):
    groups = lax.axis_size("head")
    core = lax.axis_index("ctx") % 2
    place = jnp.stack([core, lax.axis_index("head")])
    mask = block_mask.reshape(-1)
    half = out_weight.shape[1] // 2

    kv_send = pack((key_rows, value_rows), groups)
    own = exchange(kv_send)
    dealt = deal(place, after(query_rows, kv_send), groups)
    queries = [dealt[0], None, None, None]
    for r in (1, 3, 2):
        queries[r] = along_head(dealt[r], r)
    gate = lax.dynamic_slice_in_dim(gate_table, levels[0], 1, axis=0)
    weight_half = after(lax.dynamic_slice_in_dim(out_weight, core * half, half, axis=1), kv_send)
    mine = [None, None, None]
    for r in (1, 3, 2):
        mine[r - 1] = along_head(weight_half, r)

    first = to_frame(own, outward)
    swapped = to_frame(own, partner)
    second = to_frame(own, inward)
    far_first = to_frame(first, outward)
    swapped_first = to_frame(first, partner)
    far_second = to_frame(second, inward)

    state = attend(((0, 0), (2, 1)), place, mask, queries, [own, swapped], None, False)
    state = attend(
        ((4, 3), (1, 2), (3, 4)),
        place,
        mask,
        queries,
        [first, swapped_first, second],
        state,
        False,
    )
    other = to_frame(jnp.stack([after(m, state[0]) for m in mine]), partner)
    state = attend(((6, 5),), place, mask, queries, [far_first], state, False)
    attention = attend(((5, 6),), place, mask, queries, [far_second], state, True)
    gathered = exchange(attention)
    return project(place, gathered, out_weight, mine, other, gate, residual)


def solution(mesh):
    return jax.shard_map(
        body,
        mesh=mesh,
        in_specs=(
            P(("ctx", "head"), None),
            P(("ctx", "head"), None),
            P(("ctx", "head"), None),
            P(("ctx", "head"), None),
            P("ctx"),
            P(),
            P("ctx", None, None, None),
            P("head", None),
        ),
        out_specs=P(("ctx", "head"), None),
        check_vma=False,
    )
```

time: 129 us -> 144 us (1.12)
  the two profiles are of different devices: /device:TPU:256 before, /device:TPU:248 now
where the time goes in v1:
time: 144 us; the launch traced here: 143 us
  starting transfers between devices  46.3 us (32%)
  Pallas kernels  41.4 us (29%)
  waiting for transfers between devices  30.8 us (21%)
  blocking collectives  16.7 us (12%)
  local copies, waits for them, and re-layouts  4.85 us (3%)
  other arithmetic  2 us (1%)
    pallas_call x4, Pallas kernels, attend(): pl.pallas_call(kernel, grid=(heads,), in_specs=[SMEM, SMEM] + [q_spec] *...  31.9 us
    ppermute x7, starting transfers between devices, to_frame(): return lax.ppermute(x, 'ctx', pairs)  24.1 us
    ppermute x6, starting transfers between devices, along_head(): return lax.ppermute(x, 'head', [(i, (i + by) % size) for i in range(size)])  18.8 us
    all_to_all x1, blocking collectives, exchange(): return lax.all_to_all(pieces, 'head', 0, 0, tiled=True)  16.7 us
    ppermute x7, waiting for transfers between devices, to_frame(): return lax.ppermute(x, 'ctx', pairs)  16.4 us
    ppermute x6, waiting for transfers between devices, along_head(): return lax.ppermute(x, 'head', [(i, (i + by) % size) for i in range(size)])  8.32 us
    all_to_all x1, waiting for transfers between devices, exchange(): return lax.all_to_all(pieces, 'head', 0, 0, tiled=True)  6.09 us
    pallas_call x1, Pallas kernels, project(): pl.pallas_call(project_kernel, in_specs=[SMEM] + [VMEM] * 8, out_specs=VM...  4.29 us
  transfers between devices with their start and end apart: 14, of which 5 were waited for; matrix products, arithmetic and copies ran while one was open for 2% of the time, Pallas kernels for 24%

profile of v1, /device:TPU:248, one launch (start us, length us, event | category | flops | bytes accessed | tf_op | source)
XLA Modules:
  0.0 143.0 jit_solution(17910070759519506298)
XLA Ops:
  0.0 3.4 %pack.1 = bf16[4,2,3,128,128]{4,3,2,1,0:T(8,128)(2,1)} custom-call(bf16[128,1536]{1,0:T(8,128)(2,1)} %refs_0_.1, bf16[128,1536]{1,0:T(8,128)(2,1)} %refs_1_.1), custom_call_target="tpu_custom_call" | custom-call | tf_op jit(solution)/shard_map/pack/pallas_call | solution.py:56
  3.5 16.7 %all_to_all.10.refs_6_ = bf16[4,2,3,128,128]{4,3,2,1,0:T(8,128)(2,1)S(1)} all-to-all(bf16[4,2,3,128,128]{4,3,2,1,0:T(8,128)(2,1)} %pack.1), channel_id=1, replica_groups=mesh['ctx'=128,'head'=4] {'head'}, dimensions={0} | all-to-all | bytes 1572864 | tf_op jit(solution)/shard_map/all_to_all | solution.py:42
  20.2 3.2 %collective-permute-start.5 = (bf16[4,2,3,128,128]{4,3,2,1,0:T(8,128)(2,1)S(1)}, bf16[4,2,3,128,128]{4,3,2,1,0:T(8,128)(2,1)}, u32[]{:S(2)}, u32[]{:S(2)}) collective-permute-start(bf16[4,2,3,128,128]{4,3,2,1,0:T(8,128)(2,1)S(1)} %all_to_all.10.refs_6_), channel_id=1, source_target_pairs={{8,0},{16,8},{4,12},{24,16},{12,20},{32,24},{20,28},{40,32},{28,36... | collective-permute-start | bytes 2359304 | tf_op jit(solution)/shard_map/ppermute | solution.py:21
  23.4 1.9 %collective-permute-start.8 = (bf16[4,2,3,128,128]{4,3,2,1,0:T(8,128)(2,1)S(1)}, bf16[4,2,3,128,128]{4,3,2,1,0:T(8,128)(2,1)}, u32[]{:S(2)}, u32[]{:S(2)}) collective-permute-start(bf16[4,2,3,128,128]{4,3,2,1,0:T(8,128)(2,1)S(1)} %all_to_all.10.refs_6_), channel_id=1, source_target_pairs={{4,0},{0,4},{12,8},{8,12},{20,16},{16,20},{28,24},{24,28},{36,32},... | collective-permute-start | bytes 2359304 | tf_op jit(solution)/shard_map/ppermute | solution.py:21
  26.0 1.8 %deal.1 = (bf16[3,128,128]{2,1,0:T(8,128)(2,1)}, bf16[3,128,128]{2,1,0:T(8,128)(2,1)}, bf16[3,128,128]{2,1,0:T(8,128)(2,1)}, bf16[3,128,128]{2,1,0:T(8,128)(2,1)}) custom-call(s32[2]{0:T(128)} %pad_add_fusion.place_ref.refs_0_, bf16[128,1536]{1,0:T(8,128)(2,1)} %rows_ref), custom_call_target="tpu_custom_call" | custom-call | tf_op jit(solution)/shard_map/deal/pallas_call | solution.py:78
  27.8 2.5 %collective-permute-start = (bf16[3,128,128]{2,1,0:T(8,128)(2,1)}, bf16[3,128,128]{2,1,0:T(8,128)(2,1)S(1)}, u32[]{:S(2)}, u32[]{:S(2)}) collective-permute-start(bf16[3,128,128]{2,1,0:T(8,128)(2,1)} %get-tuple-element.22), channel_id=1, source_target_pairs={{0,1},{1,2},{2,3},{3,0},{4,5},{5,6},{6,7},{7,4},{8,9},{9,10},{10,1... | collective-permute-start | bytes 294920 | tf_op jit(solution)/shard_map/ppermute | solution.py:38
  30.2 5.9 %collective-permute-start.3 = (bf16[4,2,3,128,128]{4,3,2,1,0:T(8,128)(2,1)S(1)}, bf16[4,2,3,128,128]{4,3,2,1,0:T(8,128)(2,1)}, u32[]{:S(2)}, u32[]{:S(2)}) collective-permute-start(bf16[4,2,3,128,128]{4,3,2,1,0:T(8,128)(2,1)S(1)} %all_to_all.10.refs_6_), channel_id=1, source_target_pairs={{12,4},{0,8},{20,12},{8,16},{28,20},{16,24},{36,28},{24,32},{44,36... | collective-permute-start | bytes 2359304 | tf_op jit(solution)/shard_map/ppermute | solution.py:21
  36.1 1.3 collective-permute-done.5.refs_6_
  37.5 1.9 %collective-permute-start.7 = (bf16[4,2,3,128,128]{4,3,2,1,0:T(8,128)(2,1)}, bf16[4,2,3,128,128]{4,3,2,1,0:T(8,128)(2,1)}, u32[]{:S(2)}, u32[]{:S(2)}) collective-permute-start(bf16[4,2,3,128,128]{4,3,2,1,0:T(8,128)(2,1)} %collective-permute-done.5.refs_6_), channel_id=1, source_target_pairs={{4,0},{0,4},{12,8},{8,12},{20,16},{16,20},{28,24},{24,28},{36,32},... | collective-permute-start | bytes 2359304 | tf_op jit(solution)/shard_map/ppermute | solution.py:21
  39.4 2.7 %collective-permute-start.1 = (bf16[3,128,128]{2,1,0:T(8,128)(2,1)}, bf16[3,128,128]{2,1,0:T(8,128)(2,1)S(1)}, u32[]{:S(2)}, u32[]{:S(2)}) collective-permute-start(bf16[3,128,128]{2,1,0:T(8,128)(2,1)} %get-tuple-element.23), channel_id=1, source_target_pairs={{0,2},{1,3},{2,0},{3,1},{4,6},{5,7},{6,4},{7,5},{8,10},{9,11},{10,... | collective-permute-start | bytes 294920 | tf_op jit(solution)/shard_map/ppermute | solution.py:38
  42.1 4.3 %collective-permute-start.2 = (bf16[3,128,128]{2,1,0:T(8,128)(2,1)}, bf16[3,128,128]{2,1,0:T(8,128)(2,1)S(1)}, u32[]{:S(2)}, u32[]{:S(2)}) collective-permute-start(bf16[3,128,128]{2,1,0:T(8,128)(2,1)} %get-tuple-element.24), channel_id=1, source_target_pairs={{0,3},{1,0},{2,1},{3,2},{4,7},{5,4},{6,5},{7,6},{8,11},{9,8},{10,9... | collective-permute-start | bytes 294920 | tf_op jit(solution)/shard_map/ppermute | solution.py:38
  46.5 0.9 constant_dynamic-slice_fusion.1
  47.4 0.8 collective-permute-done.1.refs_4_
  48.2 3.3 %collective-permute-start.11 = (bf16[384,768]{1,0:T(8,128)(2,1)}, bf16[384,768]{1,0:T(8,128)(2,1)S(1)}, u32[]{:S(2)}, u32[]{:S(2)}) collective-permute-start(bf16[384,768]{1,0:T(8,128)(2,1)} %constant_dynamic-slice_fusion.1), channel_id=1, source_target_pairs={{0,3},{1,0},{2,1},{3,2},{4,7},{5,4},{6,5},{7,6},{8,11},{9,8},{10,9... | collective-permute-start | bytes 1769480 | tf_op jit(solution)/shard_map/ppermute | solution.py:38
  51.5 3.2 %collective-permute-start.10 = (bf16[384,768]{1,0:T(8,128)(2,1)}, bf16[384,768]{1,0:T(8,128)(2,1)S(1)}, u32[]{:S(2)}, u32[]{:S(2)}) collective-permute-start(bf16[384,768]{1,0:T(8,128)(2,1)} %constant_dynamic-slice_fusion.1), channel_id=1, source_target_pairs={{0,2},{1,3},{2,0},{3,1},{4,6},{5,7},{6,4},{7,5},{8,10},{9,11},{10,... | collective-permute-start | bytes 1769480 | tf_op jit(solution)/shard_map/ppermute | solution.py:38
  54.7 2.8 %collective-permute-start.9 = (bf16[384,768]{1,0:T(8,128)(2,1)}, bf16[384,768]{1,0:T(8,128)(2,1)S(1)}, u32[]{:S(2)}, u32[]{:S(2)}) collective-permute-start(bf16[384,768]{1,0:T(8,128)(2,1)} %constant_dynamic-slice_fusion.1), channel_id=1, source_target_pairs={{0,1},{1,2},{2,3},{3,0},{4,5},{5,6},{6,7},{7,4},{8,9},{9,10},{10,1... | collective-permute-start | bytes 1769480 | tf_op jit(solution)/shard_map/ppermute | solution.py:38
  58.2 7.3 %shard_map.82 = (f32[3,512,128]{2,1,0:T(8,128)}, f32[3,512,128]{2,1,0:T(8,128)}) custom-call(s32[2]{0:T(128)} %pad_add_fusion.place_ref.refs_0_, s32[112]{0:T(128)} %reshape.3.refs_1_, bf16[3,128,128]{2,1,0:T(8,128)(2,1)} %get-tuple-element.21.refs_2_, bf16[3,128,128]{2,1,0:T(8,128)(2,1)} %copy-done.6, bf16[3,128,128]{2,1,0:T(8,128)(2,1)} %copy-done.7, ...), custom_call_target="tpu_custom_call" | custom-call | tf_op jit(solution)/shard_map/pallas_call | solution.py:171
  65.6 9.2 %shard_map.83 = (f32[3,512,128]{2,1,0:T(8,128)}, f32[3,512,128]{2,1,0:T(8,128)}) custom-call(s32[2]{0:T(128)} %pad_add_fusion.place_ref.refs_0_, s32[112]{0:T(128)} %reshape.3.refs_1_, bf16[3,128,128]{2,1,0:T(8,128)(2,1)} %get-tuple-element.21.refs_2_, bf16[3,128,128]{2,1,0:T(8,128)(2,1)} %copy-done.6, bf16[3,128,128]{2,1,0:T(8,128)(2,1)} %copy-done.7, ...), custom_call_target="tpu_custom_call" | custom-call | tf_op jit(solution)/shard_map/pallas_call | solution.py:171
  74.8 7.5 %collective-permute-done.9.m1 = bf16[384,768]{1,0:T(8,128)(2,1)S(1)} collective-permute-done((bf16[384,768]{1,0:T(8,128)(2,1)}, bf16[384,768]{1,0:T(8,128)(2,1)S(1)}, u32[]{:S(2)}, u32[]{:S(2)}) %collective-permute-start.9) | collective-permute-done | bytes 589856 | tf_op jit(solution)/shard_map/ppermute | solution.py:38
  82.3 1.4 pad_maximum_fusion
  83.7 1.9 %collective-permute-start.12 = (bf16[3,384,768]{2,1,0:T(8,128)(2,1)}, bf16[3,384,768]{2,1,0:T(8,128)(2,1)}, u32[]{:S(2)}, u32[]{:S(2)}) collective-permute-start(bf16[3,384,768]{2,1,0:T(8,128)(2,1)} %pad_maximum_fusion), channel_id=1, source_target_pairs={{4,0},{0,4},{12,8},{8,12},{20,16},{16,20},{28,24},{24,28},{36,32},... | collective-permute-start | bytes 5308424 | tf_op jit(solution)/shard_map/ppermute | solution.py:21
  85.7 1.9 %collective-permute-start.6 = (bf16[4,2,3,128,128]{4,3,2,1,0:T(8,128)(2,1)}, bf16[4,2,3,128,128]{4,3,2,1,0:T(8,128)(2,1)S(1)}, u32[]{:S(2)}, u32[]{:S(2)}) collective-permute-start(bf16[4,2,3,128,128]{4,3,2,1,0:T(8,128)(2,1)} %collective-permute-done.5.refs_6_), channel_id=1, source_target_pairs={{8,0},{16,8},{4,12},{24,16},{12,20},{32,24},{20,28},{40,32},{28,36... | collective-permute-start | bytes 2359304 | tf_op jit(solution)/shard_map/ppermute | solution.py:21
  87.6 7.2 %collective-permute-start.4 = (bf16[4,2,3,128,128]{4,3,2,1,0:T(8,128)(2,1)}, bf16[4,2,3,128,128]{4,3,2,1,0:T(8,128)(2,1)S(1)}, u32[]{:S(2)}, u32[]{:S(2)}) collective-permute-start(bf16[4,2,3,128,128]{4,3,2,1,0:T(8,128)(2,1)} %collective-permute-done.3.refs_8_), channel_id=1, source_target_pairs={{12,4},{0,8},{20,12},{8,16},{28,20},{16,24},{36,28},{24,32},{44,36... | collective-permute-start | bytes 2359304 | tf_op jit(solution)/shard_map/ppermute | solution.py:21
  94.8 15.1 %collective-permute-done.6.refs_6_ = bf16[4,2,3,128,128]{4,3,2,1,0:T(8,128)(2,1)S(1)} collective-permute-done((bf16[4,2,3,128,128]{4,3,2,1,0:T(8,128)(2,1)}, bf16[4,2,3,128,128]{4,3,2,1,0:T(8,128)(2,1)S(1)}, u32[]{:S(2)}, u32[]{:S(2)}) %collective-permute-start.6) | collective-permute-done | bytes 786464 | tf_op jit(solution)/shard_map/ppermute | solution.py:21
  109.9 1.0 copy-done.11
  110.9 7.7 %shard_map.84 = (f32[3,512,128]{2,1,0:T(8,128)}, f32[3,512,128]{2,1,0:T(8,128)}) custom-call(s32[2]{0:T(128)} %pad_add_fusion.place_ref.refs_0_, s32[112]{0:T(128)} %reshape.3.refs_1_, bf16[3,128,128]{2,1,0:T(8,128)(2,1)} %get-tuple-element.21.refs_2_, bf16[3,128,128]{2,1,0:T(8,128)(2,1)} %copy-done.6, bf16[3,128,128]{2,1,0:T(8,128)(2,1)} %copy-done.7, ...), custom_call_target="tpu_custom_call" | custom-call | tf_op jit(solution)/shard_map/pallas_call | solution.py:171
  118.6 0.9 copy-done.10
  119.5 7.7 %shard_map.85 = bf16[4,3,128,128]{3,2,1,0:T(8,128)(2,1)} custom-call(s32[2]{0:T(128)} %pad_add_fusion.place_ref.refs_0_, s32[112]{0:T(128)} %reshape.3.refs_1_, bf16[3,128,128]{2,1,0:T(8,128)(2,1)} %get-tuple-element.21.refs_2_, bf16[3,128,128]{2,1,0:T(8,128)(2,1)} %copy-done.6, bf16[3,128,128]{2,1,0:T(8,128)(2,1)} %copy-done.7, ...), custom_call_target="tpu_custom_call" | custom-call | tf_op jit(solution)/shard_map/pallas_call | solution.py:171
  127.2 3.5 %all-to-all-start.1 = ((bf16[4,3,128,128]{3,2,1,0:T(8,128)(2,1)}), bf16[4,3,128,128]{3,2,1,0:T(8,128)(2,1)S(1)}, u32[]{:S(2)}, u32[]{:S(2)}) async-start(bf16[4,3,128,128]{3,2,1,0:T(8,128)(2,1)} %shard_map.85), calls=%async_computation.1 | async-start | bytes 786432 | tf_op jit(solution)/shard_map/all_to_all | solution.py:42
  131.9 6.1 %all-to-all-done.1.o_ref = bf16[4,3,128,128]{3,2,1,0:T(8,128)(2,1)S(1)} async-done(((bf16[4,3,128,128]{3,2,1,0:T(8,128)(2,1)}), bf16[4,3,128,128]{3,2,1,0:T(8,128)(2,1)S(1)}, u32[]{:S(2)}, u32[]{:S(2)}) %all-to-all-start.1) | async-done | bytes 393248 | tf_op jit(solution)/shard_map/all_to_all | solution.py:42
  138.0 0.7 copy-done.9
  138.7 4.3 %project.1 = bf16[128,1536]{1,0:T(8,128)(2,1)} custom-call(s32[2]{0:T(128)} %pad_add_fusion.place_ref.refs_0_, bf16[4,3,128,128]{3,2,1,0:T(8,128)(2,1)} %copy-done.9, bf16[384,1536]{1,0:T(8,128)(2,1)} %w_ref.1, bf16[384,768]{1,0:T(8,128)(2,1)} %copy-done.5, bf16[384,768]{1,0:T(8,128)(2,1)} %copy-done.4, bf16[384,768]{1,0:T(8,128)(2,1)} %copy-done.3, ...), custom_call_target="tpu_custom_call" | custom-call | tf_op jit(solution)/shard_map/project/pallas_call | solution.py:203
  (36 shorter events, 2.0 us)
Async XLA Ops:
  0.0 131.3 %copy-start = (f32[50,1536]{1,0:T(8,128)S(1)}, f32[50,1536]{1,0:T(8,128)}, u32[]{:S(2)}) copy-start(f32[50,1536]{1,0:T(8,128)} %param.13) | copy-start | bytes 921604
  0.0 46.5 %copy-start.2 = (bf16[384,1536]{1,0:T(8,128)(2,1)S(1)}, bf16[384,1536]{1,0:T(8,128)(2,1)}, u32[]{:S(2)}) copy-start(bf16[384,1536]{1,0:T(8,128)(2,1)} %w_ref.1) | copy-start | bytes 3538948
  3.5 54.0 %copy-start.12 = (s32[1,7,4,4]{1,3,2,0:T(4,128)S(1)}, s32[1,7,4,4]{1,3,2,0:T(4,128)}, u32[]{:S(2)}) copy-start(s32[1,7,4,4]{1,3,2,0:T(4,128)} %param.14) | copy-start | bytes 1348
  20.2 38.0 %copy-start.1 = (bf16[4,2,3,128,128]{4,3,2,1,0:T(8,128)(2,1)}, bf16[4,2,3,128,128]{4,3,2,1,0:T(8,128)(2,1)S(1)}, u32[]{:S(2)}) copy-start(bf16[4,2,3,128,128]{4,3,2,1,0:T(8,128)(2,1)S(1)} %all_to_all.10.refs_6_) | copy-start | bytes 2359300
  20.2 17.3 %collective-permute-start.5 = (bf16[4,2,3,128,128]{4,3,2,1,0:T(8,128)(2,1)S(1)}, bf16[4,2,3,128,128]{4,3,2,1,0:T(8,128)(2,1)}, u32[]{:S(2)}, u32[]{:S(2)}) collective-permute-start(bf16[4,2,3,128,128]{4,3,2,1,0:T(8,128)(2,1)S(1)} %all_to_all.10.refs_6_), channel_id=1, source_target_pairs={{8,0},{16,8},{4,12},{24,16},{12,20},{32,24},{20,28},{40,32},{28,36... | collective-permute-start | bytes 2359304 | tf_op jit(solution)/shard_map/ppermute | solution.py:21
  23.4 31.3 %collective-permute-start.8 = (bf16[4,2,3,128,128]{4,3,2,1,0:T(8,128)(2,1)S(1)}, bf16[4,2,3,128,128]{4,3,2,1,0:T(8,128)(2,1)}, u32[]{:S(2)}, u32[]{:S(2)}) collective-permute-start(bf16[4,2,3,128,128]{4,3,2,1,0:T(8,128)(2,1)S(1)} %all_to_all.10.refs_6_), channel_id=1, source_target_pairs={{4,0},{0,4},{12,8},{8,12},{20,16},{16,20},{28,24},{24,28},{36,32},... | collective-permute-start | bytes 2359304 | tf_op jit(solution)/shard_map/ppermute | solution.py:21
  27.8 14.4 %collective-permute-start = (bf16[3,128,128]{2,1,0:T(8,128)(2,1)}, bf16[3,128,128]{2,1,0:T(8,128)(2,1)S(1)}, u32[]{:S(2)}, u32[]{:S(2)}) collective-permute-start(bf16[3,128,128]{2,1,0:T(8,128)(2,1)} %get-tuple-element.22), channel_id=1, source_target_pairs={{0,1},{1,2},{2,3},{3,0},{4,5},{5,6},{6,7},{7,4},{8,9},{9,10},{10,1... | collective-permute-start | bytes 294920 | tf_op jit(solution)/shard_map/ppermute | solution.py:38
  30.2 35.3 %collective-permute-start.3 = (bf16[4,2,3,128,128]{4,3,2,1,0:T(8,128)(2,1)S(1)}, bf16[4,2,3,128,128]{4,3,2,1,0:T(8,128)(2,1)}, u32[]{:S(2)}, u32[]{:S(2)}) collective-permute-start(bf16[4,2,3,128,128]{4,3,2,1,0:T(8,128)(2,1)S(1)} %all_to_all.10.refs_6_), channel_id=1, source_target_pairs={{12,4},{0,8},{20,12},{8,16},{28,20},{16,24},{36,28},{24,32},{44,36... | collective-permute-start | bytes 2359304 | tf_op jit(solution)/shard_map/ppermute | solution.py:21
  37.5 28.1 %collective-permute-start.7 = (bf16[4,2,3,128,128]{4,3,2,1,0:T(8,128)(2,1)}, bf16[4,2,3,128,128]{4,3,2,1,0:T(8,128)(2,1)}, u32[]{:S(2)}, u32[]{:S(2)}) collective-permute-start(bf16[4,2,3,128,128]{4,3,2,1,0:T(8,128)(2,1)} %collective-permute-done.5.refs_6_), channel_id=1, source_target_pairs={{4,0},{0,4},{12,8},{8,12},{20,16},{16,20},{28,24},{24,28},{36,32},... | collective-permute-start | bytes 2359304 | tf_op jit(solution)/shard_map/ppermute | solution.py:21
  39.4 8.8 %collective-permute-start.1 = (bf16[3,128,128]{2,1,0:T(8,128)(2,1)}, bf16[3,128,128]{2,1,0:T(8,128)(2,1)S(1)}, u32[]{:S(2)}, u32[]{:S(2)}) collective-permute-start(bf16[3,128,128]{2,1,0:T(8,128)(2,1)} %get-tuple-element.23), channel_id=1, source_target_pairs={{0,2},{1,3},{2,0},{3,1},{4,6},{5,7},{6,4},{7,5},{8,10},{9,11},{10,... | collective-permute-start | bytes 294920 | tf_op jit(solution)/shard_map/ppermute | solution.py:38
  42.1 16.1 %copy-start.6 = (bf16[3,128,128]{2,1,0:T(8,128)(2,1)}, bf16[3,128,128]{2,1,0:T(8,128)(2,1)S(1)}, u32[]{:S(2)}) copy-start(bf16[3,128,128]{2,1,0:T(8,128)(2,1)S(1)} %collective-permute-done.refs_3_) | copy-start | bytes 294916
  42.1 9.3 %collective-permute-start.2 = (bf16[3,128,128]{2,1,0:T(8,128)(2,1)}, bf16[3,128,128]{2,1,0:T(8,128)(2,1)S(1)}, u32[]{:S(2)}, u32[]{:S(2)}) collective-permute-start(bf16[3,128,128]{2,1,0:T(8,128)(2,1)} %get-tuple-element.24), channel_id=1, source_target_pairs={{0,3},{1,0},{2,1},{3,2},{4,7},{5,4},{6,5},{7,6},{8,11},{9,8},{10,9... | collective-permute-start | bytes 294920 | tf_op jit(solution)/shard_map/ppermute | solution.py:38
  48.2 10.0 %copy-start.7 = (bf16[3,128,128]{2,1,0:T(8,128)(2,1)}, bf16[3,128,128]{2,1,0:T(8,128)(2,1)S(1)}, u32[]{:S(2)}) copy-start(bf16[3,128,128]{2,1,0:T(8,128)(2,1)S(1)} %collective-permute-done.1.refs_4_) | copy-start | bytes 294916
  48.2 26.6 %collective-permute-start.11 = (bf16[384,768]{1,0:T(8,128)(2,1)}, bf16[384,768]{1,0:T(8,128)(2,1)S(1)}, u32[]{:S(2)}, u32[]{:S(2)}) collective-permute-start(bf16[384,768]{1,0:T(8,128)(2,1)} %constant_dynamic-slice_fusion.1), channel_id=1, source_target_pairs={{0,3},{1,0},{2,1},{3,2},{4,7},{5,4},{6,5},{7,6},{8,11},{9,8},{10,9... | collective-permute-start | bytes 1769480 | tf_op jit(solution)/shard_map/ppermute | solution.py:38
  51.5 6.7 %copy-start.8 = (bf16[3,128,128]{2,1,0:T(8,128)(2,1)}, bf16[3,128,128]{2,1,0:T(8,128)(2,1)S(1)}, u32[]{:S(2)}) copy-start(bf16[3,128,128]{2,1,0:T(8,128)(2,1)S(1)} %collective-permute-done.2.refs_5_) | copy-start | bytes 294916
  51.5 23.3 %collective-permute-start.10 = (bf16[384,768]{1,0:T(8,128)(2,1)}, bf16[384,768]{1,0:T(8,128)(2,1)S(1)}, u32[]{:S(2)}, u32[]{:S(2)}) collective-permute-start(bf16[384,768]{1,0:T(8,128)(2,1)} %constant_dynamic-slice_fusion.1), channel_id=1, source_target_pairs={{0,2},{1,3},{2,0},{3,1},{4,6},{5,7},{6,4},{7,5},{8,10},{9,11},{10,... | collective-permute-start | bytes 1769480 | tf_op jit(solution)/shard_map/ppermute | solution.py:38
  54.7 27.6 %collective-permute-start.9 = (bf16[384,768]{1,0:T(8,128)(2,1)}, bf16[384,768]{1,0:T(8,128)(2,1)S(1)}, u32[]{:S(2)}, u32[]{:S(2)}) collective-permute-start(bf16[384,768]{1,0:T(8,128)(2,1)} %constant_dynamic-slice_fusion.1), channel_id=1, source_target_pairs={{0,1},{1,2},{2,3},{3,0},{4,5},{5,6},{6,7},{7,4},{8,9},{9,10},{10,1... | collective-permute-start | bytes 1769480 | tf_op jit(solution)/shard_map/ppermute | solution.py:38
  74.8 9.0 %copy-start.3 = (bf16[384,768]{1,0:T(8,128)(2,1)}, bf16[384,768]{1,0:T(8,128)(2,1)S(1)}, u32[]{:S(2)}) copy-start(bf16[384,768]{1,0:T(8,128)(2,1)S(1)} %collective-permute-done.11.m3) | copy-start | bytes 1769476
  74.8 9.0 %copy-start.4 = (bf16[384,768]{1,0:T(8,128)(2,1)}, bf16[384,768]{1,0:T(8,128)(2,1)S(1)}, u32[]{:S(2)}) copy-start(bf16[384,768]{1,0:T(8,128)(2,1)S(1)} %collective-permute-done.10.m2) | copy-start | bytes 1769476
  82.3 1.4 copy-start.5
  83.7 54.3 %collective-permute-start.12 = (bf16[3,384,768]{2,1,0:T(8,128)(2,1)}, bf16[3,384,768]{2,1,0:T(8,128)(2,1)}, u32[]{:S(2)}, u32[]{:S(2)}) collective-permute-start(bf16[3,384,768]{2,1,0:T(8,128)(2,1)} %pad_maximum_fusion), channel_id=1, source_target_pairs={{4,0},{0,4},{12,8},{8,12},{20,16},{16,20},{28,24},{24,28},{36,32},... | collective-permute-start | bytes 5308424 | tf_op jit(solution)/shard_map/ppermute | solution.py:21
  85.7 24.3 %collective-permute-start.6 = (bf16[4,2,3,128,128]{4,3,2,1,0:T(8,128)(2,1)}, bf16[4,2,3,128,128]{4,3,2,1,0:T(8,128)(2,1)S(1)}, u32[]{:S(2)}, u32[]{:S(2)}) collective-permute-start(bf16[4,2,3,128,128]{4,3,2,1,0:T(8,128)(2,1)} %collective-permute-done.5.refs_6_), channel_id=1, source_target_pairs={{8,0},{16,8},{4,12},{24,16},{12,20},{32,24},{20,28},{40,32},{28,36... | collective-permute-start | bytes 2359304 | tf_op jit(solution)/shard_map/ppermute | solution.py:21
  87.6 31.0 %collective-permute-start.4 = (bf16[4,2,3,128,128]{4,3,2,1,0:T(8,128)(2,1)}, bf16[4,2,3,128,128]{4,3,2,1,0:T(8,128)(2,1)S(1)}, u32[]{:S(2)}, u32[]{:S(2)}) collective-permute-start(bf16[4,2,3,128,128]{4,3,2,1,0:T(8,128)(2,1)} %collective-permute-done.3.refs_8_), channel_id=1, source_target_pairs={{12,4},{0,8},{20,12},{8,16},{28,20},{16,24},{36,28},{24,32},{44,36... | collective-permute-start | bytes 2359304 | tf_op jit(solution)/shard_map/ppermute | solution.py:21
  109.9 1.0 copy-start.11
  118.6 0.9 copy-start.10
  127.2 10.8 %all-to-all-start.1 = ((bf16[4,3,128,128]{3,2,1,0:T(8,128)(2,1)}), bf16[4,3,128,128]{3,2,1,0:T(8,128)(2,1)S(1)}, u32[]{:S(2)}, u32[]{:S(2)}) async-start(bf16[4,3,128,128]{3,2,1,0:T(8,128)(2,1)} %shard_map.85), calls=%async_computation.1 | async-start | bytes 786432 | tf_op jit(solution)/shard_map/all_to_all | solution.py:42
  138.0 0.7 copy-start.9

commit v2 on v0

v2 whole, which is shorter than its diff:
```python
import math

import jax
import jax.numpy as jnp
from jax import lax
from jax.experimental import pallas as pl
from jax.experimental.pallas import tpu as pltpu
from jax.sharding import PartitionSpec as P


HEAD_DIM = 128
BLOCK = 128
EXP2_SCALE = math.log2(math.e) / math.sqrt(HEAD_DIM)
SMEM = pl.BlockSpec(memory_space=pltpu.SMEM)
VMEM = pl.BlockSpec(memory_space=pltpu.VMEM)


def to_frame(x, source_of):
    count = lax.axis_size("ctx")
    pairs = [(source_of(f), f) for f in range(count) if 0 <= source_of(f) < count]
    return lax.ppermute(x, "ctx", pairs)


def partner(f):
    return f ^ 1


def outward(f):
    return f + 2 if f % 2 == 0 else f - 2


def inward(f):
    return f - 2 if f % 2 == 0 else f + 2


def beside(x):
    frames, size = lax.axis_size("ctx"), lax.axis_size("head")
    pairs = [
        (f * size + (i + 1 - 2 * (f % 2)) % size, f * size + i)
        for f in range(frames)
        for i in range(size)
    ]
    return lax.ppermute(x, ("ctx", "head"), pairs)


def exchange(pieces):
    return lax.all_to_all(pieces, "head", 0, 0, tiled=True)


def call(kernel, args, out_shape):
    specs = [SMEM if a.dtype == jnp.int32 else VMEM for a in args]
    args = [
        a if a.dtype == jnp.int32 else pltpu.with_memory_space_constraint(a, pltpu.VMEM)
        for a in args
    ]
    return pl.pallas_call(
        kernel,
        in_specs=specs,
        out_specs=jax.tree.map(lambda _: VMEM, out_shape),
        out_shape=out_shape,
        compiler_params=pltpu.CompilerParams(vmem_limit_bytes=24 << 20),
    )(*args)


def pack_kv_kernel(key_ref, value_ref, out_ref):
    groups, _, heads = out_ref.shape[:3]
    for g in range(groups):
        for h in range(heads):
            at = slice((g * heads + h) * HEAD_DIM, (g * heads + h + 1) * HEAD_DIM)
            out_ref[g, 0, h] = key_ref[:, at]
            out_ref[g, 1, h] = jnp.transpose(value_ref[:, at])


def pack_q_kernel(query_ref, out_ref):
    groups, heads = out_ref.shape[:2]
    for g in range(groups):
        for h in range(heads):
            out_ref[g, h] = query_ref[:, (g * heads + h) * HEAD_DIM : (g * heads + h + 1) * HEAD_DIM]


def attend_kernel(slots, first, last, place_ref, mask_ref, q_ref, *refs):
    count = len(slots)
    kv_refs, refs = refs[:count], refs[count:]
    groups, heads = q_ref.shape[:2]
    rows = groups * BLOCK
    core = place_ref[0]
    if first:
        outs = refs
    else:
        peak_in, total_in, acc_in = refs[:3]
        outs = refs[3:]
    slot_at = [jnp.where(core == 0, even, odd) * groups * groups for even, odd in slots]
    keep = [
        [[mask_ref[slot_at[s] + a * groups + b] > 0 for a in range(groups)] for b in range(groups)]
        for s in range(count)
    ]
    for h in range(heads):
        queries = q_ref[:, h].reshape(rows, HEAD_DIM)
        tiles, peak = [], None
        for s in range(count):
            for b in range(groups):
                tile = lax.dot_general(
                    kv_refs[s][b, 0, h],
                    queries,
                    (((1,), (1,)), ((), ())),
                    preferred_element_type=jnp.float32,
                )
                tile = jnp.concatenate(
                    [
                        jnp.where(keep[s][b][a], tile[:, a * BLOCK : (a + 1) * BLOCK], -jnp.inf)
                        for a in range(groups)
                    ],
                    axis=1,
                )
                top = jnp.max(tile.reshape(BLOCK // 8, 8, rows), axis=0)
                peak = top if peak is None else jnp.maximum(peak, top)
                tiles.append(tile)
        peak = jnp.max(peak, axis=0, keepdims=True)
        if not first:
            before = peak_in[h, 0:1]
            peak = jnp.maximum(peak, before)
            rescale = jnp.exp2((before - peak) * EXP2_SCALE)
        total, weights = None, []
        for tile in tiles:
            tile = jnp.exp2((tile - peak) * EXP2_SCALE)
            part = jnp.sum(tile.reshape(BLOCK // 8, 8, rows), axis=0)
            total = part if total is None else total + part
            weights.append(tile.astype(jnp.bfloat16))
        values = jnp.concatenate(
            [kv_refs[s][b, 1, h] for s in range(count) for b in range(groups)], axis=1
        )
        weighted = jnp.dot(
            values, jnp.concatenate(weights, axis=0), preferred_element_type=jnp.float32
        )
        if not first:
            total = total + total_in[h] * rescale
            weighted = weighted + acc_in[h] * rescale
        if last:
            total = jnp.sum(total, axis=0, keepdims=True)
            attention = (weighted / total).astype(jnp.bfloat16)
            for a in range(groups):
                outs[0][a, h] = jnp.transpose(attention[:, a * BLOCK : (a + 1) * BLOCK])
        else:
            outs[0][h] = jnp.broadcast_to(peak, (8, rows))
            outs[1][h] = total
            outs[2][h] = weighted


def attend(slots, place, mask, queries, kvs, state, last):
    groups, heads, tokens = queries.shape[:3]
    rows = groups * tokens
    if last:
        out_shape = jax.ShapeDtypeStruct(queries.shape, jnp.bfloat16)
    else:
        stat = jax.ShapeDtypeStruct((heads, 8, rows), jnp.float32)
        out_shape = [stat, stat, jax.ShapeDtypeStruct((heads, HEAD_DIM, rows), jnp.float32)]

    def kernel(*refs):
        attend_kernel(slots, state is None, last, *refs)

    return call(kernel, (place, mask, queries, *kvs, *(state or ())), out_shape)


def project_kernel(
    place_ref, o_ref, own_ref, near_ref, far_ref, mine_ref, other_ref, gate_ref, residual_ref, out_ref
):
    groups, heads = o_ref.shape[:2]
    core, x = place_ref[0], place_ref[1]
    half = mine_ref.shape[1]

    def features(up):
        group = (x + up) % groups
        return jnp.concatenate([o_ref[group, h] for h in range(heads)], axis=1)

    step = 1 + 2 * core
    own, near, far, opposite = features(0), features(step), features(4 - step), features(2)
    for column, opposite_ref in ((core, mine_ref), (1 - core, other_ref)):
        at = pl.ds(pl.multiple_of(column * half, 128), half)
        projected = jnp.dot(own, own_ref[:, at], preferred_element_type=jnp.float32)
        projected += jnp.dot(near, near_ref[:, at], preferred_element_type=jnp.float32)
        projected += jnp.dot(far, far_ref[:, at], preferred_element_type=jnp.float32)
        projected += jnp.dot(opposite, opposite_ref[...], preferred_element_type=jnp.float32)
        mixed = residual_ref[:, at].astype(jnp.float32) + gate_ref[:, at] * projected
        out_ref[:, at] = mixed.astype(jnp.bfloat16)


def after(value, *others):
    return lax.optimization_barrier((value, *others))[0]


def body(query_rows, key_rows, value_rows, residual, levels, gate_table, block_mask, out_weight):
    groups = lax.axis_size("head")
    tokens, width = query_rows.shape
    heads = width // HEAD_DIM // groups
    core = lax.axis_index("ctx") % 2
    place = jnp.stack([core, lax.axis_index("head")])
    mask = block_mask.reshape(-1)
    half = width // 2

    kv_shape = jax.ShapeDtypeStruct((groups, 2, heads, tokens, HEAD_DIM), jnp.bfloat16)
    q_shape = jax.ShapeDtypeStruct((groups, heads, tokens, HEAD_DIM), jnp.bfloat16)
    kv_send = call(pack_kv_kernel, (key_rows, value_rows), kv_shape)
    own = exchange(kv_send)
    q_send = call(pack_q_kernel, (after(query_rows, kv_send),), q_shape)
    gate = lax.dynamic_slice_in_dim(gate_table, levels[0], 1, axis=0)
    near = beside(after(out_weight, kv_send))

    first = to_frame(own, outward)
    second = to_frame(own, inward)
    queries = exchange(after(q_send, own))
    swapped = to_frame(own, partner)
    mine = beside(lax.dynamic_slice_in_dim(near, core * half, half, axis=1))
    far_first = to_frame(first, outward)
    far_second = to_frame(second, inward)
    swapped_first = to_frame(first, partner)
    far = to_frame(near, partner)
    other = to_frame(mine, partner)

    state = attend(((0, 0), (2, 1)), place, mask, queries, [own, swapped], None, False)
    slots = ((4, 3), (1, 2), (3, 4))
    arrived = [first, swapped_first, second]
    state = attend(slots, place, mask, queries, arrived, state, False)
    state = attend(((6, 5),), place, mask, queries, [far_first], state, False)
    attention = attend(((5, 6),), place, mask, queries, [far_second], state, True)
    gathered = exchange(attention)
    return call(
        project_kernel,
        (place, gathered, out_weight, near, far, mine, other, gate, residual),
        jax.ShapeDtypeStruct(residual.shape, jnp.bfloat16),
    )


def solution(mesh):
    return jax.shard_map(
        body,
        mesh=mesh,
        in_specs=(
            P(("ctx", "head"), None),
            P(("ctx", "head"), None),
            P(("ctx", "head"), None),
            P(("ctx", "head"), None),
            P("ctx"),
            P(),
            P("ctx", None, None, None),
            P("head", None),
        ),
        out_specs=P(("ctx", "head"), None),
        check_vma=False,
    )
```

time: 129 us -> 106 us (0.82)
  the two profiles are of different devices: /device:TPU:256 before, /device:TPU:248 now
where the time goes in v2:
time: 106 us; the launch traced here: 105 us
  starting transfers between devices  46.1 us (43%)
  blocking collectives  22.3 us (21%)
  Pallas kernels  20.3 us (19%)
  waiting for transfers between devices  12 us (11%)
  local copies, waits for them, and re-layouts  3.16 us (3%)
    ppermute x8, starting transfers between devices, to_frame(): return lax.ppermute(x, 'ctx', pairs)  26.3 us
    all_to_all x1, blocking collectives, exchange(): return lax.all_to_all(pieces, 'head', 0, 0, tiled=True)  22.3 us
    pallas_call x7, Pallas kernels, call(): pl.pallas_call(kernel, in_specs=specs, out_specs=jax.tree.map(lambda _: V...  20.3 us
    all_to_all x2, waiting for transfers between devices, exchange(): return lax.all_to_all(pieces, 'head', 0, 0, tiled=True)  11.8 us
    ppermute x2, starting transfers between devices, beside(): return lax.ppermute(x, ('ctx', 'head'), pairs)  10.4 us
    all_to_all x2, starting transfers between devices, exchange(): return lax.all_to_all(pieces, 'head', 0, 0, tiled=True)  9.38 us
    unnamed x13, local copies, waits for them, and re-layouts  2.17 us
  transfers between devices with their start and end apart: 12, of which 3 were waited for; matrix products, arithmetic and copies ran while one was open for 1% of the time, Pallas kernels for 16%

profile of v2, /device:TPU:248, one launch (start us, length us, event | category | flops | bytes accessed | tf_op | source)
XLA Modules:
  0.0 104.9 jit_solution(9119209871035213005)
XLA Ops:
  0.0 1.0 copy-done.3
  1.1 1.0 copy-done.4
  2.0 0.2 shard_map.82
  2.2 0.0 copy-start.2
  2.2 4.8 %collective-permute-start.6 = (bf16[384,1536]{1,0:T(8,128)(2,1)}, bf16[384,1536]{1,0:T(8,128)(2,1)S(1)}, u32[]{:S(2)}, u32[]{:S(2)}) collective-permute-start(bf16[384,1536]{1,0:T(8,128)(2,1)} %own_ref.1), channel_id=1, source_target_pairs={{1,0},{2,1},{3,2},{0,3},{7,4},{4,5},{5,6},{6,7},{9,8},{10,9},{11,1... | collective-permute-start | bytes 3538952 | tf_op jit(solution)/shard_map/ppermute | solution.py:43
  7.0 22.3 %all_to_all.15.refs_3_ = bf16[4,2,3,128,128]{4,3,2,1,0:T(8,128)(2,1)S(1)} all-to-all(bf16[4,2,3,128,128]{4,3,2,1,0:T(8,128)(2,1)S(1)} %shard_map.82), channel_id=1, replica_groups=mesh['ctx'=128,'head'=4] {'head'}, dimensions={0} | all-to-all | bytes 1572864 | tf_op jit(solution)/shard_map/all_to_all | solution.py:47
  29.4 3.2 %collective-permute-start.2 = (bf16[4,2,3,128,128]{4,3,2,1,0:T(8,128)(2,1)S(1)}, bf16[4,2,3,128,128]{4,3,2,1,0:T(8,128)(2,1)}, u32[]{:S(2)}, u32[]{:S(2)}) collective-permute-start(bf16[4,2,3,128,128]{4,3,2,1,0:T(8,128)(2,1)S(1)} %all_to_all.15.refs_3_), channel_id=1, source_target_pairs={{8,0},{16,8},{4,12},{24,16},{12,20},{32,24},{20,28},{40,32},{28,36... | collective-permute-start | bytes 2359304 | tf_op jit(solution)/shard_map/ppermute | solution.py:21
  32.6 3.7 %collective-permute-start.5 = (bf16[4,2,3,128,128]{4,3,2,1,0:T(8,128)(2,1)S(1)}, bf16[4,2,3,128,128]{4,3,2,1,0:T(8,128)(2,1)S(1)}, u32[]{:S(2)}, u32[]{:S(2)}) collective-permute-start(bf16[4,2,3,128,128]{4,3,2,1,0:T(8,128)(2,1)S(1)} %all_to_all.15.refs_3_), channel_id=1, source_target_pairs={{4,0},{0,4},{12,8},{8,12},{20,16},{16,20},{28,24},{24,28},{36,32},... | collective-permute-start | bytes 2359304 | tf_op jit(solution)/shard_map/ppermute | solution.py:21
  36.3 4.2 %collective-permute-start = (bf16[4,2,3,128,128]{4,3,2,1,0:T(8,128)(2,1)S(1)}, bf16[4,2,3,128,128]{4,3,2,1,0:T(8,128)(2,1)}, u32[]{:S(2)}, u32[]{:S(2)}) collective-permute-start(bf16[4,2,3,128,128]{4,3,2,1,0:T(8,128)(2,1)S(1)} %all_to_all.15.refs_3_), channel_id=1, source_target_pairs={{12,4},{0,8},{20,12},{8,16},{28,20},{16,24},{36,28},{24,32},{44,36... | collective-permute-start | bytes 2359304 | tf_op jit(solution)/shard_map/ppermute | solution.py:21
  40.5 0.0 copy-start.5
  40.5 0.9 constant_dynamic-slice_fusion.1
  41.4 5.6 %collective-permute-start.8 = (bf16[384,768]{1,0:T(8,128)(2,1)}, bf16[384,768]{1,0:T(8,128)(2,1)}, u32[]{:S(2)}, u32[]{:S(2)}) collective-permute-start(bf16[384,768]{1,0:T(8,128)(2,1)} %constant_dynamic-slice_fusion.1), channel_id=1, source_target_pairs={{1,0},{2,1},{3,2},{0,3},{7,4},{4,5},{5,6},{6,7},{9,8},{10,9},{11,1... | collective-permute-start | bytes 1769480 | tf_op jit(solution)/shard_map/ppermute | solution.py:43
  47.0 1.9 %collective-permute-start.7 = (bf16[384,1536]{1,0:T(8,128)(2,1)S(1)}, bf16[384,1536]{1,0:T(8,128)(2,1)}, u32[]{:S(2)}, u32[]{:S(2)}) collective-permute-start(bf16[384,1536]{1,0:T(8,128)(2,1)S(1)} %collective-permute-done.6.near_ref), channel_id=1, source_target_pairs={{4,0},{0,4},{12,8},{8,12},{20,16},{16,20},{28,24},{24,28},{36,32},... | collective-permute-start | bytes 3538952 | tf_op jit(solution)/shard_map/ppermute | solution.py:21
  48.9 0.2 collective-permute-done.2.refs_3_
  49.1 2.2 %collective-permute-start.4 = (bf16[4,2,3,128,128]{4,3,2,1,0:T(8,128)(2,1)}, bf16[4,2,3,128,128]{4,3,2,1,0:T(8,128)(2,1)}, u32[]{:S(2)}, u32[]{:S(2)}) collective-permute-start(bf16[4,2,3,128,128]{4,3,2,1,0:T(8,128)(2,1)} %collective-permute-done.2.refs_3_), channel_id=1, source_target_pairs={{4,0},{0,4},{12,8},{8,12},{20,16},{16,20},{28,24},{24,28},{36,32},... | collective-permute-start | bytes 2359304 | tf_op jit(solution)/shard_map/ppermute | solution.py:21
  51.4 1.9 %collective-permute-start.3 = (bf16[4,2,3,128,128]{4,3,2,1,0:T(8,128)(2,1)}, bf16[4,2,3,128,128]{4,3,2,1,0:T(8,128)(2,1)}, u32[]{:S(2)}, u32[]{:S(2)}) collective-permute-start(bf16[4,2,3,128,128]{4,3,2,1,0:T(8,128)(2,1)} %collective-permute-done.2.refs_3_), channel_id=1, source_target_pairs={{8,0},{16,8},{4,12},{24,16},{12,20},{32,24},{20,28},{40,32},{28,36... | collective-permute-start | bytes 2359304 | tf_op jit(solution)/shard_map/ppermute | solution.py:21
  53.3 7.2 %collective-permute-start.1 = (bf16[4,2,3,128,128]{4,3,2,1,0:T(8,128)(2,1)}, bf16[4,2,3,128,128]{4,3,2,1,0:T(8,128)(2,1)}, u32[]{:S(2)}, u32[]{:S(2)}) collective-permute-start(bf16[4,2,3,128,128]{4,3,2,1,0:T(8,128)(2,1)} %collective-permute-done.refs_5_), channel_id=1, source_target_pairs={{12,4},{0,8},{20,12},{8,16},{28,20},{16,24},{36,28},{24,32},{44,36... | collective-permute-start | bytes 2359304 | tf_op jit(solution)/shard_map/ppermute | solution.py:21
  60.6 0.8 shard_map.83
  61.4 5.9 %all-to-all-start.1 = ((bf16[4,3,128,128]{3,2,1,0:T(8,128)(2,1)}), bf16[4,3,128,128]{3,2,1,0:T(8,128)(2,1)S(1)}, u32[]{:S(2)}, u32[]{:S(2)}) async-start(bf16[4,3,128,128]{3,2,1,0:T(8,128)(2,1)} %shard_map.83), calls=%async_computation.1 | async-start | bytes 786432 | tf_op jit(solution)/shard_map/all_to_all | solution.py:47
  67.3 1.9 %collective-permute-start.9 = (bf16[384,768]{1,0:T(8,128)(2,1)}, bf16[384,768]{1,0:T(8,128)(2,1)}, u32[]{:S(2)}, u32[]{:S(2)}) collective-permute-start(bf16[384,768]{1,0:T(8,128)(2,1)} %collective-permute-done.8.mine_ref), channel_id=1, source_target_pairs={{4,0},{0,4},{12,8},{8,12},{20,16},{16,20},{28,24},{24,28},{36,32},... | collective-permute-start | bytes 1769480 | tf_op jit(solution)/shard_map/ppermute | solution.py:21
  69.2 0.1 copy.10
  69.3 0.1 reshape.3.refs_1_
  69.4 0.1 pad_add_fusion.refs_0_.place_ref
  69.5 5.1 %all-to-all-done.1.refs_2_ = bf16[4,3,128,128]{3,2,1,0:T(8,128)(2,1)S(1)} async-done(((bf16[4,3,128,128]{3,2,1,0:T(8,128)(2,1)}), bf16[4,3,128,128]{3,2,1,0:T(8,128)(2,1)S(1)}, u32[]{:S(2)}, u32[]{:S(2)}) %all-to-all-start.1) | async-done | bytes 393248 | tf_op jit(solution)/shard_map/all_to_all | solution.py:47
  74.7 3.4 %shard_map.84 = (f32[3,8,512]{2,1,0:T(8,128)S(1)}, f32[3,8,512]{2,1,0:T(8,128)S(1)}, f32[3,128,512]{2,1,0:T(8,128)S(1)}) custom-call(s32[2]{0:T(128)S(1)} %pad_add_fusion.refs_0_.place_ref, s32[112]{0:T(128)S(1)} %reshape.3.refs_1_, bf16[4,3,128,128]{3,2,1,0:T(8,128)(2,1)S(1)} %all-to-all-done.1.refs_2_, ...), custom_call_target="tpu_custom_call" | custom-call | tf_op jit(solution)/shard_map/pallas_call | solution.py:56
  78.1 5.8 %shard_map.85 = (f32[3,8,512]{2,1,0:T(8,128)S(1)}, f32[3,8,512]{2,1,0:T(8,128)S(1)}, f32[3,128,512]{2,1,0:T(8,128)S(1)}) custom-call(s32[2]{0:T(128)S(1)} %pad_add_fusion.refs_0_.place_ref, s32[112]{0:T(128)S(1)} %reshape.3.refs_1_, bf16[4,3,128,128]{3,2,1,0:T(8,128)(2,1)S(1)} %all-to-all-done.1.refs_2_, ...), custom_call_target="tpu_custom_call" | custom-call | tf_op jit(solution)/shard_map/pallas_call | solution.py:56
  83.9 2.9 %shard_map.86 = (f32[3,8,512]{2,1,0:T(8,128)S(1)}, f32[3,8,512]{2,1,0:T(8,128)S(1)}, f32[3,128,512]{2,1,0:T(8,128)S(1)}) custom-call(s32[2]{0:T(128)S(1)} %pad_add_fusion.refs_0_.place_ref, s32[112]{0:T(128)S(1)} %reshape.3.refs_1_, bf16[4,3,128,128]{3,2,1,0:T(8,128)(2,1)S(1)} %all-to-all-done.1.refs_2_, ...), custom_call_target="tpu_custom_call" | custom-call | tf_op jit(solution)/shard_map/pallas_call | solution.py:56
  86.8 0.0 copy-start.1
  86.8 3.6 %shard_map.87 = bf16[4,3,128,128]{3,2,1,0:T(8,128)(2,1)} custom-call(s32[2]{0:T(128)S(1)} %pad_add_fusion.refs_0_.place_ref, s32[112]{0:T(128)S(1)} %reshape.3.refs_1_, bf16[4,3,128,128]{3,2,1,0:T(8,128)(2,1)S(1)} %all-to-all-done.1.refs_2_, bf16[4,2,3,128,128]{4,3,2,1,0:T(8,128)(2,1)} %collective-permute-done.1.refs_3_, ...), custom_call_target="tpu_custom_call" | custom-call | tf_op jit(solution)/shard_map/pallas_call | solution.py:56
  90.4 3.5 %all-to-all-start.2 = ((bf16[4,3,128,128]{3,2,1,0:T(8,128)(2,1)}), bf16[4,3,128,128]{3,2,1,0:T(8,128)(2,1)S(1)}, u32[]{:S(2)}, u32[]{:S(2)}) async-start(bf16[4,3,128,128]{3,2,1,0:T(8,128)(2,1)} %shard_map.87), calls=%async_computation.2 | async-start | bytes 786432 | tf_op jit(solution)/shard_map/all_to_all | solution.py:47
  94.6 6.6 %all-to-all-done.2.o_ref = bf16[4,3,128,128]{3,2,1,0:T(8,128)(2,1)S(1)} async-done(((bf16[4,3,128,128]{3,2,1,0:T(8,128)(2,1)}), bf16[4,3,128,128]{3,2,1,0:T(8,128)(2,1)S(1)}, u32[]{:S(2)}, u32[]{:S(2)}) %all-to-all-start.2) | async-done | bytes 393248 | tf_op jit(solution)/shard_map/all_to_all | solution.py:47
  101.2 3.7 %shard_map.88 = bf16[128,1536]{1,0:T(8,128)(2,1)} custom-call(s32[2]{0:T(128)S(1)} %pad_add_fusion.refs_0_.place_ref, bf16[4,3,128,128]{3,2,1,0:T(8,128)(2,1)S(1)} %all-to-all-done.2.o_ref, bf16[384,1536]{1,0:T(8,128)(2,1)} %own_ref.1, bf16[384,1536]{1,0:T(8,128)(2,1)S(1)} %collective-permute-done.6.near_ref, ...), custom_call_target="tpu_custom_call" | custom-call | tf_op jit(solution)/shard_map/pallas_call | solution.py:56
  (17 shorter events, 0.1 us)
Async XLA Ops:
  0.0 94.5 %copy-start = (f32[50,1536]{1,0:T(8,128)S(1)}, f32[50,1536]{1,0:T(8,128)}, u32[]{:S(2)}) copy-start(f32[50,1536]{1,0:T(8,128)} %param.13) | copy-start | bytes 921604
  0.0 1.0 copy-start.3
  1.0 1.0 copy-start.4
  2.2 58.3 %copy-start.2 = (bf16[128,1536]{1,0:T(8,128)(2,1)S(1)}, bf16[128,1536]{1,0:T(8,128)(2,1)}, u32[]{:S(2)}) copy-start(bf16[128,1536]{1,0:T(8,128)(2,1)} %query_ref) | copy-start | bytes 1179652
  2.2 38.3 %collective-permute-start.6 = (bf16[384,1536]{1,0:T(8,128)(2,1)}, bf16[384,1536]{1,0:T(8,128)(2,1)S(1)}, u32[]{:S(2)}, u32[]{:S(2)}) collective-permute-start(bf16[384,1536]{1,0:T(8,128)(2,1)} %own_ref.1), channel_id=1, source_target_pairs={{1,0},{2,1},{3,2},{0,3},{7,4},{4,5},{5,6},{6,7},{9,8},{10,9},{11,1... | collective-permute-start | bytes 3538952 | tf_op jit(solution)/shard_map/ppermute | solution.py:43
  29.4 19.7 %collective-permute-start.2 = (bf16[4,2,3,128,128]{4,3,2,1,0:T(8,128)(2,1)S(1)}, bf16[4,2,3,128,128]{4,3,2,1,0:T(8,128)(2,1)}, u32[]{:S(2)}, u32[]{:S(2)}) collective-permute-start(bf16[4,2,3,128,128]{4,3,2,1,0:T(8,128)(2,1)S(1)} %all_to_all.15.refs_3_), channel_id=1, source_target_pairs={{8,0},{16,8},{4,12},{24,16},{12,20},{32,24},{20,28},{40,32},{28,36... | collective-permute-start | bytes 2359304 | tf_op jit(solution)/shard_map/ppermute | solution.py:21
  32.6 18.7 %collective-permute-start.5 = (bf16[4,2,3,128,128]{4,3,2,1,0:T(8,128)(2,1)S(1)}, bf16[4,2,3,128,128]{4,3,2,1,0:T(8,128)(2,1)S(1)}, u32[]{:S(2)}, u32[]{:S(2)}) collective-permute-start(bf16[4,2,3,128,128]{4,3,2,1,0:T(8,128)(2,1)S(1)} %all_to_all.15.refs_3_), channel_id=1, source_target_pairs={{4,0},{0,4},{12,8},{8,12},{20,16},{16,20},{28,24},{24,28},{36,32},... | collective-permute-start | bytes 2359304 | tf_op jit(solution)/shard_map/ppermute | solution.py:21
  36.3 17.0 %collective-permute-start = (bf16[4,2,3,128,128]{4,3,2,1,0:T(8,128)(2,1)S(1)}, bf16[4,2,3,128,128]{4,3,2,1,0:T(8,128)(2,1)}, u32[]{:S(2)}, u32[]{:S(2)}) collective-permute-start(bf16[4,2,3,128,128]{4,3,2,1,0:T(8,128)(2,1)S(1)} %all_to_all.15.refs_3_), channel_id=1, source_target_pairs={{12,4},{0,8},{20,12},{8,16},{28,20},{16,24},{36,28},{24,32},{44,36... | collective-permute-start | bytes 2359304 | tf_op jit(solution)/shard_map/ppermute | solution.py:21
  40.5 28.7 %copy-start.5 = (s32[1,7,4,4]{1,3,2,0:T(4,128)S(1)}, s32[1,7,4,4]{1,3,2,0:T(4,128)}, u32[]{:S(2)}) copy-start(s32[1,7,4,4]{1,3,2,0:T(4,128)} %param.14) | copy-start | bytes 1348
  41.4 25.9 %collective-permute-start.8 = (bf16[384,768]{1,0:T(8,128)(2,1)}, bf16[384,768]{1,0:T(8,128)(2,1)}, u32[]{:S(2)}, u32[]{:S(2)}) collective-permute-start(bf16[384,768]{1,0:T(8,128)(2,1)} %constant_dynamic-slice_fusion.1), channel_id=1, source_target_pairs={{1,0},{2,1},{3,2},{0,3},{7,4},{4,5},{5,6},{6,7},{9,8},{10,9},{11,1... | collective-permute-start | bytes 1769480 | tf_op jit(solution)/shard_map/ppermute | solution.py:43
  47.0 47.6 %collective-permute-start.7 = (bf16[384,1536]{1,0:T(8,128)(2,1)S(1)}, bf16[384,1536]{1,0:T(8,128)(2,1)}, u32[]{:S(2)}, u32[]{:S(2)}) collective-permute-start(bf16[384,1536]{1,0:T(8,128)(2,1)S(1)} %collective-permute-done.6.near_ref), channel_id=1, source_target_pairs={{4,0},{0,4},{12,8},{8,12},{20,16},{16,20},{28,24},{24,28},{36,32},... | collective-permute-start | bytes 3538952 | tf_op jit(solution)/shard_map/ppermute | solution.py:21
  49.1 29.0 %collective-permute-start.4 = (bf16[4,2,3,128,128]{4,3,2,1,0:T(8,128)(2,1)}, bf16[4,2,3,128,128]{4,3,2,1,0:T(8,128)(2,1)}, u32[]{:S(2)}, u32[]{:S(2)}) collective-permute-start(bf16[4,2,3,128,128]{4,3,2,1,0:T(8,128)(2,1)} %collective-permute-done.2.refs_3_), channel_id=1, source_target_pairs={{4,0},{0,4},{12,8},{8,12},{20,16},{16,20},{28,24},{24,28},{36,32},... | collective-permute-start | bytes 2359304 | tf_op jit(solution)/shard_map/ppermute | solution.py:21
  51.4 32.5 %collective-permute-start.3 = (bf16[4,2,3,128,128]{4,3,2,1,0:T(8,128)(2,1)}, bf16[4,2,3,128,128]{4,3,2,1,0:T(8,128)(2,1)}, u32[]{:S(2)}, u32[]{:S(2)}) collective-permute-start(bf16[4,2,3,128,128]{4,3,2,1,0:T(8,128)(2,1)} %collective-permute-done.2.refs_3_), channel_id=1, source_target_pairs={{8,0},{16,8},{4,12},{24,16},{12,20},{32,24},{20,28},{40,32},{28,36... | collective-permute-start | bytes 2359304 | tf_op jit(solution)/shard_map/ppermute | solution.py:21
  53.3 33.5 %collective-permute-start.1 = (bf16[4,2,3,128,128]{4,3,2,1,0:T(8,128)(2,1)}, bf16[4,2,3,128,128]{4,3,2,1,0:T(8,128)(2,1)}, u32[]{:S(2)}, u32[]{:S(2)}) collective-permute-start(bf16[4,2,3,128,128]{4,3,2,1,0:T(8,128)(2,1)} %collective-permute-done.refs_5_), channel_id=1, source_target_pairs={{12,4},{0,8},{20,12},{8,16},{28,20},{16,24},{36,28},{24,32},{44,36... | collective-permute-start | bytes 2359304 | tf_op jit(solution)/shard_map/ppermute | solution.py:21
  61.4 13.3 %all-to-all-start.1 = ((bf16[4,3,128,128]{3,2,1,0:T(8,128)(2,1)}), bf16[4,3,128,128]{3,2,1,0:T(8,128)(2,1)S(1)}, u32[]{:S(2)}, u32[]{:S(2)}) async-start(bf16[4,3,128,128]{3,2,1,0:T(8,128)(2,1)} %shard_map.83), calls=%async_computation.1 | async-start | bytes 786432 | tf_op jit(solution)/shard_map/all_to_all | solution.py:47
  67.3 27.3 %collective-permute-start.9 = (bf16[384,768]{1,0:T(8,128)(2,1)}, bf16[384,768]{1,0:T(8,128)(2,1)}, u32[]{:S(2)}, u32[]{:S(2)}) collective-permute-start(bf16[384,768]{1,0:T(8,128)(2,1)} %collective-permute-done.8.mine_ref), channel_id=1, source_target_pairs={{4,0},{0,4},{12,8},{8,12},{20,16},{16,20},{28,24},{24,28},{36,32},... | collective-permute-start | bytes 1769480 | tf_op jit(solution)/shard_map/ppermute | solution.py:21
  86.8 14.4 %copy-start.1 = (bf16[128,1536]{1,0:T(8,128)(2,1)S(1)}, bf16[128,1536]{1,0:T(8,128)(2,1)}, u32[]{:S(2)}) copy-start(bf16[128,1536]{1,0:T(8,128)(2,1)} %residual_ref.1) | copy-start | bytes 1179652
  90.4 10.8 %all-to-all-start.2 = ((bf16[4,3,128,128]{3,2,1,0:T(8,128)(2,1)}), bf16[4,3,128,128]{3,2,1,0:T(8,128)(2,1)S(1)}, u32[]{:S(2)}, u32[]{:S(2)}) async-start(bf16[4,3,128,128]{3,2,1,0:T(8,128)(2,1)} %shard_map.87), calls=%async_computation.2 | async-start | bytes 786432 | tf_op jit(solution)/shard_map/all_to_all | solution.py:47

commit v3 on v2

v3 whole, which is shorter than its diff:
```python
import math

import jax
import jax.numpy as jnp
from jax import lax
from jax.experimental import pallas as pl
from jax.experimental.pallas import tpu as pltpu
from jax.sharding import PartitionSpec as P


HEAD_DIM = 128
BLOCK = 128
EXP2_SCALE = math.log2(math.e) / math.sqrt(HEAD_DIM)
SMEM = pl.BlockSpec(memory_space=pltpu.SMEM)
VMEM = pl.BlockSpec(memory_space=pltpu.VMEM)


def to_frame(x, source_of):
    count = lax.axis_size("ctx")
    pairs = [(source_of(f), f) for f in range(count) if 0 <= source_of(f) < count]
    return lax.ppermute(x, "ctx", pairs)


def partner(f):
    return f ^ 1


def outward(f):
    return f + 2 if f % 2 == 0 else f - 2


def inward(f):
    return f - 2 if f % 2 == 0 else f + 2


def beside(x):
    frames, size = lax.axis_size("ctx"), lax.axis_size("head")
    pairs = [
        (f * size + (i + 1 - 2 * (f % 2)) % size, f * size + i)
        for f in range(frames)
        for i in range(size)
    ]
    return lax.ppermute(x, ("ctx", "head"), pairs)


def exchange(pieces):
    return lax.all_to_all(pieces, "head", 0, 0, tiled=True)


def call(kernel, args, out_shape):
    specs = [SMEM if a.dtype == jnp.int32 else VMEM for a in args]
    args = [
        a if a.dtype == jnp.int32 else pltpu.with_memory_space_constraint(a, pltpu.VMEM)
        for a in args
    ]
    return pl.pallas_call(
        kernel,
        in_specs=specs,
        out_specs=jax.tree.map(lambda _: VMEM, out_shape),
        out_shape=out_shape,
        compiler_params=pltpu.CompilerParams(vmem_limit_bytes=8 << 20),
    )(*args)


def pack_kv_kernel(key_hbm, value_hbm, out_ref, key_ref, value_ref, sems):
    groups, _, heads = out_ref.shape[:3]
    fetch_value = pltpu.make_async_copy(value_hbm, value_ref, sems.at[0])
    fetch_key = pltpu.make_async_copy(key_hbm, key_ref, sems.at[1])
    fetch_value.start()
    fetch_key.start()
    places = [(g, h) for g in range(groups) for h in range(heads)]
    fetch_value.wait()
    for g, h in places:
        at = slice((g * heads + h) * HEAD_DIM, (g * heads + h + 1) * HEAD_DIM)
        out_ref[g, 1, h] = jnp.transpose(value_ref[:, at])
    fetch_key.wait()
    for g, h in places:
        at = slice((g * heads + h) * HEAD_DIM, (g * heads + h + 1) * HEAD_DIM)
        out_ref[g, 0, h] = key_ref[:, at]


def pack_kv(key_rows, value_rows, shape):
    hbm = pl.BlockSpec(memory_space=pltpu.HBM)
    args = [pltpu.with_memory_space_constraint(a, pltpu.HBM) for a in (key_rows, value_rows)]
    return pl.pallas_call(
        pack_kv_kernel,
        in_specs=[hbm, hbm],
        out_specs=VMEM,
        out_shape=jax.ShapeDtypeStruct(shape, jnp.bfloat16),
        scratch_shapes=[pltpu.VMEM(a.shape, a.dtype) for a in args]
        + [pltpu.SemaphoreType.DMA((2,))],
        name="pack_kv",
        compiler_params=pltpu.CompilerParams(vmem_limit_bytes=8 << 20),
    )(*args)


def pack_q_kernel(query_ref, out_ref):
    groups, heads = out_ref.shape[:2]
    for g in range(groups):
        for h in range(heads):
            out_ref[g, h] = query_ref[:, (g * heads + h) * HEAD_DIM : (g * heads + h + 1) * HEAD_DIM]


def half_kernel(place_ref, weight_ref, out_ref):
    width = out_ref.shape[1]
    out_ref[...] = weight_ref[:, pl.ds(pl.multiple_of(place_ref[0] * width, 128), width)]


def attend_kernel(slots, first, last, place_ref, mask_ref, q_ref, *refs):
    count = len(slots)
    kv_refs, refs = refs[:count], refs[count:]
    groups, heads = q_ref.shape[:2]
    rows = groups * BLOCK
    core = place_ref[0]
    if first:
        outs = refs
    else:
        peak_in, total_in, acc_in = refs[:3]
        outs = refs[3:]
    slot_at = [jnp.where(core == 0, even, odd) * groups * groups for even, odd in slots]
    keep = [
        [[mask_ref[slot_at[s] + a * groups + b] > 0 for a in range(groups)] for b in range(groups)]
        for s in range(count)
    ]
    ones = jnp.ones((16, count * rows), jnp.bfloat16)

    def score(h):
        keys = jnp.concatenate([kv[:, 0, h].reshape(rows, HEAD_DIM) for kv in kv_refs], axis=0)
        return lax.dot_general(
            keys,
            q_ref[:, h].reshape(rows, HEAD_DIM),
            (((1,), (1,)), ((), ())),
            preferred_element_type=jnp.float32,
        )

    def soften(h, scores):
        tiles, peak = [], None
        for i in range(count * groups):
            tile = jnp.concatenate(
                [
                    jnp.where(
                        keep[i // groups][i % groups][a],
                        scores[i * BLOCK : (i + 1) * BLOCK, a * BLOCK : (a + 1) * BLOCK],
                        -jnp.inf,
                    )
                    for a in range(groups)
                ],
                axis=1,
            )
            top = jnp.max(tile.reshape(BLOCK // 8, 8, rows), axis=0)
            peak = top if peak is None else jnp.maximum(peak, top)
            tiles.append(tile)
        peak = jnp.max(peak, axis=0, keepdims=True)
        if not first:
            peak = jnp.maximum(peak, peak_in[h, 0:1])
        weights = [jnp.exp2((tile - peak) * EXP2_SCALE).astype(jnp.bfloat16) for tile in tiles]
        return peak, jnp.concatenate(weights, axis=0)

    def gather(h, peak, weights):
        values = jnp.concatenate(
            [kv[b, 1, h] for kv in kv_refs for b in range(groups)], axis=1
        )
        weighted = jnp.dot(
            jnp.concatenate([values, ones], axis=0), weights, preferred_element_type=jnp.float32
        )
        total, weighted = weighted[HEAD_DIM : HEAD_DIM + 8], weighted[:HEAD_DIM]
        if not first:
            rescale = jnp.exp2((peak_in[h, 0:1] - peak) * EXP2_SCALE)
            total = total + total_in[h] * rescale
            weighted = weighted + acc_in[h] * rescale
        if last:
            attention = (weighted / total[0:1]).astype(jnp.bfloat16)
            for a in range(groups):
                outs[0][a, h] = jnp.transpose(attention[:, a * BLOCK : (a + 1) * BLOCK])
        else:
            outs[0][h] = jnp.broadcast_to(peak, (8, rows))
            outs[1][h] = total
            outs[2][h] = weighted

    scores = score(0)
    for h in range(heads):
        ahead = score(h + 1) if h + 1 < heads else None
        gather(h, *soften(h, scores))
        scores = ahead


def attend(slots, place, mask, queries, kvs, state, last):
    groups, heads, tokens = queries.shape[:3]
    rows = groups * tokens
    if last:
        out_shape = jax.ShapeDtypeStruct(queries.shape, jnp.bfloat16)
    else:
        stat = jax.ShapeDtypeStruct((heads, 8, rows), jnp.float32)
        out_shape = [stat, stat, jax.ShapeDtypeStruct((heads, HEAD_DIM, rows), jnp.float32)]

    def kernel(*refs):
        attend_kernel(slots, state is None, last, *refs)

    return call(kernel, (place, mask, queries, *kvs, *(state or ())), out_shape)


def project_kernel(
    place_ref, level_ref, o_ref, near_ref, mine_ref, other_ref, own_hbm, far_hbm, gate_hbm,
    residual_hbm, out_ref, own_ref, far_ref, gate_ref, residual_ref, sems,
):
    pairs = (
        (own_hbm, own_ref), (far_hbm, far_ref), (gate_hbm, gate_ref), (residual_hbm, residual_ref)
    )
    copies = [pltpu.make_async_copy(*pair, sems.at[i]) for i, pair in enumerate(pairs)]
    for copy in copies:
        copy.start()
    groups, heads = o_ref.shape[:2]
    core, x = place_ref[0], place_ref[1]
    half = mine_ref.shape[1]

    def features(up):
        group = (x + up) % groups
        return jnp.concatenate([o_ref[group, h] for h in range(heads)], axis=1)

    step = 1 + 2 * core
    own, near, far, opposite = features(0), features(step), features(4 - step), features(2)
    ats = [pl.ds(pl.multiple_of(c * half, 128), half) for c in (core, 1 - core)]
    sums = [
        jnp.dot(near, near_ref[:, at], preferred_element_type=jnp.float32)
        + jnp.dot(opposite, opposite_ref[...], preferred_element_type=jnp.float32)
        for at, opposite_ref in zip(ats, (mine_ref, other_ref), strict=True)
    ]
    for copy, rows, weight_ref in zip(copies, (own, far), (own_ref, far_ref)):
        copy.wait()
        sums = [
            total + jnp.dot(rows, weight_ref[:, at], preferred_element_type=jnp.float32)
            for at, total in zip(ats, sums, strict=True)
        ]
    for copy in copies[2:]:
        copy.wait()
    for at, total in zip(ats, sums, strict=True):
        gate = gate_ref[pl.ds(level_ref[0], 1), at]
        mixed = residual_ref[:, at].astype(jnp.float32) + gate * total
        out_ref[:, at] = mixed.astype(jnp.bfloat16)


def project(scalars, resident, fetched):
    hbm = pl.BlockSpec(memory_space=pltpu.HBM)
    residual = fetched[-1]
    return pl.pallas_call(
        project_kernel,
        in_specs=[SMEM] * len(scalars) + [VMEM] * len(resident) + [hbm] * len(fetched),
        out_specs=VMEM,
        out_shape=jax.ShapeDtypeStruct(residual.shape, residual.dtype),
        scratch_shapes=[pltpu.VMEM(a.shape, a.dtype) for a in fetched]
        + [pltpu.SemaphoreType.DMA((len(fetched),))],
        name="project",
        compiler_params=pltpu.CompilerParams(vmem_limit_bytes=16 << 20),
    )(
        *scalars,
        *(pltpu.with_memory_space_constraint(a, pltpu.VMEM) for a in resident),
        *(pltpu.with_memory_space_constraint(a, pltpu.HBM) for a in fetched),
    )


def after(value, *others):
    return lax.optimization_barrier((value, *others))[0]


def body(query_rows, key_rows, value_rows, residual, levels, gate_table, block_mask, out_weight):
    groups = lax.axis_size("head")
    tokens, width = query_rows.shape
    heads = width // HEAD_DIM // groups
    core = lax.axis_index("ctx") % 2
    place = jnp.stack([core, lax.axis_index("head")])
    mask = block_mask.reshape(-1)

    q_shape = jax.ShapeDtypeStruct((groups, heads, tokens, HEAD_DIM), jnp.bfloat16)
    kv_send = pack_kv(key_rows, value_rows, (groups, 2, heads, tokens, HEAD_DIM))
    own = exchange(kv_send)
    q_send = call(pack_q_kernel, (after(query_rows, kv_send, place, mask),), q_shape)
    near = beside(after(out_weight, kv_send))

    first = to_frame(own, outward)
    second = to_frame(own, inward)
    queries = exchange(after(q_send, own))
    swapped = to_frame(own, partner)
    half_shape = jax.ShapeDtypeStruct((near.shape[0], width // 2), jnp.bfloat16)
    near_half = call(half_kernel, (place, near), half_shape)
    mine = beside(near_half)
    far_first = to_frame(first, outward)
    far_second = to_frame(second, inward)
    swapped_first = to_frame(first, partner)
    far = to_frame(near, partner)
    other = to_frame(mine, partner)

    state = attend(((0, 0), (2, 1)), place, mask, queries, [own, swapped], None, False)
    slots, arrived = ((4, 3), (1, 2), (3, 4)), [first, swapped_first, second]
    state = attend(slots, place, mask, queries, arrived, state, False)
    state = attend(((6, 5),), place, mask, queries, [far_first], state, False)
    attention = attend(((5, 6),), place, mask, queries, [far_second], state, True)
    gathered = exchange(attention)
    return project(
        (place, levels), (gathered, near, mine, other), (out_weight, far, gate_table, residual)
    )


def solution(mesh):
    return jax.shard_map(
        body,
        mesh=mesh,
        in_specs=(
            P(("ctx", "head"), None),
            P(("ctx", "head"), None),
            P(("ctx", "head"), None),
            P(("ctx", "head"), None),
            P("ctx"),
            P(),
            P("ctx", None, None, None),
            P("head", None),
        ),
        out_specs=P(("ctx", "head"), None),
        check_vma=False,
    )
```

time: 106 us -> 93.5 us (0.88)
  blocking collectives: 22.3 us -> 0 us
  waiting for transfers between devices: 12 us -> 24.2 us
  local copies, waits for them, and re-layouts: 3.16 us -> 0.23 us
  Pallas kernels: 20.3 us -> 22.1 us
    all_to_all x1 -> x0, blocking collectives: 22.3 us -> none  [exchange(): return lax.all_to_all(pieces, 'head', 0, 0, tiled=True)]
    all_to_all x2 -> x3, waiting for transfers between devices: 11.8 us -> 20.5 us  [exchange(): return lax.all_to_all(pieces, 'head', 0, 0, tiled=True)]
    pallas_call x0 -> x2, Pallas kernels: none -> 6.37 us  [the longest x1 4.25 us: project(): pl.pallas_call(project_kernel, in_specs=[SMEM] * len(scalars) + [VMEM] *...]
    pallas_call x7 -> x6, Pallas kernels: 20.3 us -> 15.7 us  [call(): pl.pallas_call(kernel, in_specs=specs, out_specs=jax.tree.map(lambda _: V...]
    ppermute x8, waiting for transfers between devices: 0.22 us -> 3.64 us  [to_frame(): return lax.ppermute(x, 'ctx', pairs)]
    ppermute x2, starting transfers between devices: 10.4 us -> 8.12 us  [beside(): return lax.ppermute(x, ('ctx', 'head'), pairs)]
    unnamed x13 -> x5, local copies, waits for them, and re-layouts: 2.17 us -> 0.12 us
    all_to_all x2 -> x3, starting transfers between devices: 9.38 us -> 11.2 us  [exchange(): return lax.all_to_all(pieces, 'head', 0, 0, tiled=True)]
  transfers between devices with their start and end apart: 12 -> 13, of which waited for: 3 -> 4; matrix products, arithmetic and copies ran while one was open for 1% -> 0% of each run, Pallas kernels for 16% -> 17%
where the time goes in v3:
time: 93.5 us; the launch traced here: 92.8 us
  starting transfers between devices  45.3 us (48%)
  waiting for transfers between devices  24.2 us (26%)
  Pallas kernels  22.1 us (24%)
    ppermute x8, starting transfers between devices, to_frame(): return lax.ppermute(x, 'ctx', pairs)  26 us
    all_to_all x3, waiting for transfers between devices, exchange(): return lax.all_to_all(pieces, 'head', 0, 0, tiled=True)  20.5 us
    pallas_call x6, Pallas kernels, call(): pl.pallas_call(kernel, in_specs=specs, out_specs=jax.tree.map(lambda _: V...  15.7 us
    all_to_all x3, starting transfers between devices, exchange(): return lax.all_to_all(pieces, 'head', 0, 0, tiled=True)  11.2 us
    ppermute x2, starting transfers between devices, beside(): return lax.ppermute(x, ('ctx', 'head'), pairs)  8.12 us
    pallas_call x1, Pallas kernels, project(): pl.pallas_call(project_kernel, in_specs=[SMEM] * len(scalars) + [VMEM] *...  4.25 us
    ppermute x8, waiting for transfers between devices, to_frame(): return lax.ppermute(x, 'ctx', pairs)  3.64 us
    pallas_call x1, Pallas kernels, pack_kv(): pl.pallas_call(pack_kv_kernel, in_specs=[hbm, hbm], out_specs=VMEM, out_s...  2.12 us
  transfers between devices with their start and end apart: 13, of which 4 were waited for; matrix products, arithmetic and copies ran while one was open for 0% of the time, Pallas kernels for 17%

profile of v3, /device:TPU:248, one launch (start us, length us, event | category | flops | bytes accessed | tf_op | source)
XLA Modules:
  0.0 92.8 jit_solution(12355680281009521642)
XLA Ops:
  0.0 2.1 %pack_kv.1 = bf16[4,2,3,128,128]{4,3,2,1,0:T(8,128)(2,1)} custom-call(bf16[128,1536]{1,0:T(8,128)(2,1)} %key_hbm.1, bf16[128,1536]{1,0:T(8,128)(2,1)} %value_hbm.1), custom_call_target="tpu_custom_call" | custom-call | tf_op jit(solution)/shard_map/pack_kv/pallas_call | solution.py:85
  2.1 4.3 %all-to-all-start = ((bf16[4,2,3,128,128]{4,3,2,1,0:T(8,128)(2,1)}), bf16[4,2,3,128,128]{4,3,2,1,0:T(8,128)(2,1)S(1)}, u32[]{:S(2)}, u32[]{:S(2)}) async-start(bf16[4,2,3,128,128]{4,3,2,1,0:T(8,128)(2,1)} %pack_kv.1), calls=%async_computation | async-start | bytes 1572864 | tf_op jit(solution)/shard_map/all_to_all | solution.py:47
  6.4 5.3 %collective-permute-start.6 = (bf16[384,1536]{1,0:T(8,128)(2,1)}, bf16[384,1536]{1,0:T(8,128)(2,1)S(1)}, u32[]{:S(2)}, u32[]{:S(2)}) collective-permute-start(bf16[384,1536]{1,0:T(8,128)(2,1)} %own_hbm.1), channel_id=1, source_target_pairs={{1,0},{2,1},{3,2},{0,3},{7,4},{4,5},{5,6},{6,7},{9,8},{10,9},{11,1... | collective-permute-start | bytes 3538952 | tf_op jit(solution)/shard_map/ppermute | solution.py:43
  11.7 8.5 %all-to-all-done.refs_3_ = bf16[4,2,3,128,128]{4,3,2,1,0:T(8,128)(2,1)S(1)} async-done(((bf16[4,2,3,128,128]{4,3,2,1,0:T(8,128)(2,1)}), bf16[4,2,3,128,128]{4,3,2,1,0:T(8,128)(2,1)S(1)}, u32[]{:S(2)}, u32[]{:S(2)}) %all-to-all-start) | async-done | bytes 786464 | tf_op jit(solution)/shard_map/all_to_all | solution.py:47
  20.2 3.2 %collective-permute-start.2 = (bf16[4,2,3,128,128]{4,3,2,1,0:T(8,128)(2,1)S(1)}, bf16[4,2,3,128,128]{4,3,2,1,0:T(8,128)(2,1)}, u32[]{:S(2)}, u32[]{:S(2)}) collective-permute-start(bf16[4,2,3,128,128]{4,3,2,1,0:T(8,128)(2,1)S(1)} %all-to-all-done.refs_3_), channel_id=1, source_target_pairs={{8,0},{16,8},{4,12},{24,16},{12,20},{32,24},{20,28},{40,32},{28,36... | collective-permute-start | bytes 2359304 | tf_op jit(solution)/shard_map/ppermute | solution.py:21
  23.4 1.9 %collective-permute-start.5 = (bf16[4,2,3,128,128]{4,3,2,1,0:T(8,128)(2,1)S(1)}, bf16[4,2,3,128,128]{4,3,2,1,0:T(8,128)(2,1)S(1)}, u32[]{:S(2)}, u32[]{:S(2)}) collective-permute-start(bf16[4,2,3,128,128]{4,3,2,1,0:T(8,128)(2,1)S(1)} %all-to-all-done.refs_3_), channel_id=1, source_target_pairs={{4,0},{0,4},{12,8},{8,12},{20,16},{16,20},{28,24},{24,28},{36,32},... | collective-permute-start | bytes 2359304 | tf_op jit(solution)/shard_map/ppermute | solution.py:21
  25.4 5.9 %collective-permute-start = (bf16[4,2,3,128,128]{4,3,2,1,0:T(8,128)(2,1)S(1)}, bf16[4,2,3,128,128]{4,3,2,1,0:T(8,128)(2,1)}, u32[]{:S(2)}, u32[]{:S(2)}) collective-permute-start(bf16[4,2,3,128,128]{4,3,2,1,0:T(8,128)(2,1)S(1)} %all-to-all-done.refs_3_), channel_id=1, source_target_pairs={{12,4},{0,8},{20,12},{8,16},{28,20},{16,24},{36,28},{24,32},{44,36... | collective-permute-start | bytes 2359304 | tf_op jit(solution)/shard_map/ppermute | solution.py:21
  31.3 0.1 pad_add_fusion.refs_0_.place_ref
  31.4 0.0 collective-permute-done.6.weight_ref.near_ref
  31.4 1.4 %shard_map.87 = bf16[384,768]{1,0:T(8,128)(2,1)} custom-call(s32[2]{0:T(128)S(1)} %pad_add_fusion.refs_0_.place_ref, bf16[384,1536]{1,0:T(8,128)(2,1)S(1)} %collective-permute-done.6.weight_ref.near_ref), custom_call_target="tpu_custom_call" | custom-call | tf_op jit(solution)/shard_map/pallas_call | solution.py:56
  32.8 2.9 %collective-permute-start.7 = (bf16[384,768]{1,0:T(8,128)(2,1)}, bf16[384,768]{1,0:T(8,128)(2,1)}, u32[]{:S(2)}, u32[]{:S(2)}) collective-permute-start(bf16[384,768]{1,0:T(8,128)(2,1)} %shard_map.87), channel_id=1, source_target_pairs={{1,0},{2,1},{3,2},{0,3},{7,4},{4,5},{5,6},{6,7},{9,8},{10,9},{11,1... | collective-permute-start | bytes 1769480 | tf_op jit(solution)/shard_map/ppermute | solution.py:43
  35.6 1.9 %collective-permute-start.9 = (bf16[384,1536]{1,0:T(8,128)(2,1)S(1)}, bf16[384,1536]{1,0:T(8,128)(2,1)}, u32[]{:S(2)}, u32[]{:S(2)}) collective-permute-start(bf16[384,1536]{1,0:T(8,128)(2,1)S(1)} %collective-permute-done.6.weight_ref.near_ref), channel_id=1, source_target_pairs={{4,0},{0,4},{12,8},{8,12},{20,16},{16,20},{28,24},{24,28},{36,32},... | collective-permute-start | bytes 3538952 | tf_op jit(solution)/shard_map/ppermute | solution.py:21
  37.6 3.6 %collective-permute-done.2.refs_3_ = bf16[4,2,3,128,128]{4,3,2,1,0:T(8,128)(2,1)} collective-permute-done((bf16[4,2,3,128,128]{4,3,2,1,0:T(8,128)(2,1)S(1)}, bf16[4,2,3,128,128]{4,3,2,1,0:T(8,128)(2,1)}, u32[]{:S(2)}, u32[]{:S(2)}) %collective-permute-start.2) | collective-permute-done | bytes 786464 | tf_op jit(solution)/shard_map/ppermute | solution.py:21
  41.2 1.9 %collective-permute-start.4 = (bf16[4,2,3,128,128]{4,3,2,1,0:T(8,128)(2,1)}, bf16[4,2,3,128,128]{4,3,2,1,0:T(8,128)(2,1)}, u32[]{:S(2)}, u32[]{:S(2)}) collective-permute-start(bf16[4,2,3,128,128]{4,3,2,1,0:T(8,128)(2,1)} %collective-permute-done.2.refs_3_), channel_id=1, source_target_pairs={{4,0},{0,4},{12,8},{8,12},{20,16},{16,20},{28,24},{24,28},{36,32},... | collective-permute-start | bytes 2359304 | tf_op jit(solution)/shard_map/ppermute | solution.py:21
  43.1 1.9 %collective-permute-start.3 = (bf16[4,2,3,128,128]{4,3,2,1,0:T(8,128)(2,1)}, bf16[4,2,3,128,128]{4,3,2,1,0:T(8,128)(2,1)}, u32[]{:S(2)}, u32[]{:S(2)}) collective-permute-start(bf16[4,2,3,128,128]{4,3,2,1,0:T(8,128)(2,1)} %collective-permute-done.2.refs_3_), channel_id=1, source_target_pairs={{8,0},{16,8},{4,12},{24,16},{12,20},{32,24},{20,28},{40,32},{28,36... | collective-permute-start | bytes 2359304 | tf_op jit(solution)/shard_map/ppermute | solution.py:21
  45.0 7.2 %collective-permute-start.1 = (bf16[4,2,3,128,128]{4,3,2,1,0:T(8,128)(2,1)}, bf16[4,2,3,128,128]{4,3,2,1,0:T(8,128)(2,1)}, u32[]{:S(2)}, u32[]{:S(2)}) collective-permute-start(bf16[4,2,3,128,128]{4,3,2,1,0:T(8,128)(2,1)} %collective-permute-done.refs_5_), channel_id=1, source_target_pairs={{12,4},{0,8},{20,12},{8,16},{28,20},{16,24},{36,28},{24,32},{44,36... | collective-permute-start | bytes 2359304 | tf_op jit(solution)/shard_map/ppermute | solution.py:21
  52.3 0.1 copy.10
  52.4 0.1 reshape.3.refs_1_
  52.5 0.8 shard_map.82
  53.4 3.5 %all-to-all-start.1 = ((bf16[4,3,128,128]{3,2,1,0:T(8,128)(2,1)}), bf16[4,3,128,128]{3,2,1,0:T(8,128)(2,1)S(1)}, u32[]{:S(2)}, u32[]{:S(2)}) async-start(bf16[4,3,128,128]{3,2,1,0:T(8,128)(2,1)} %shard_map.82), calls=%async_computation.1 | async-start | bytes 786432 | tf_op jit(solution)/shard_map/all_to_all | solution.py:47
  56.8 1.9 %collective-permute-start.8 = (bf16[384,768]{1,0:T(8,128)(2,1)}, bf16[384,768]{1,0:T(8,128)(2,1)}, u32[]{:S(2)}, u32[]{:S(2)}) collective-permute-start(bf16[384,768]{1,0:T(8,128)(2,1)} %collective-permute-done.7.mine_ref), channel_id=1, source_target_pairs={{4,0},{0,4},{12,8},{8,12},{20,16},{16,20},{28,24},{24,28},{36,32},... | collective-permute-start | bytes 1769480 | tf_op jit(solution)/shard_map/ppermute | solution.py:21
  58.8 5.4 %all-to-all-done.1.refs_2_ = bf16[4,3,128,128]{3,2,1,0:T(8,128)(2,1)S(1)} async-done(((bf16[4,3,128,128]{3,2,1,0:T(8,128)(2,1)}), bf16[4,3,128,128]{3,2,1,0:T(8,128)(2,1)S(1)}, u32[]{:S(2)}, u32[]{:S(2)}) %all-to-all-start.1) | async-done | bytes 393248 | tf_op jit(solution)/shard_map/all_to_all | solution.py:47
  64.2 2.8 %shard_map.83 = (f32[3,8,512]{2,1,0:T(8,128)S(1)}, f32[3,8,512]{2,1,0:T(8,128)S(1)}, f32[3,128,512]{2,1,0:T(8,128)S(1)}) custom-call(s32[2]{0:T(128)S(1)} %pad_add_fusion.refs_0_.place_ref, s32[112]{0:T(128)S(1)} %reshape.3.refs_1_, bf16[4,3,128,128]{3,2,1,0:T(8,128)(2,1)S(1)} %all-to-all-done.1.refs_2_, ...), custom_call_target="tpu_custom_call" | custom-call | tf_op jit(solution)/shard_map/pallas_call | solution.py:56
  67.0 0.0 collective-permute-done.4.refs_4_
  67.0 4.9 %shard_map.84 = (f32[3,8,512]{2,1,0:T(8,128)S(1)}, f32[3,8,512]{2,1,0:T(8,128)S(1)}, f32[3,128,512]{2,1,0:T(8,128)S(1)}) custom-call(s32[2]{0:T(128)S(1)} %pad_add_fusion.refs_0_.place_ref, s32[112]{0:T(128)S(1)} %reshape.3.refs_1_, bf16[4,3,128,128]{3,2,1,0:T(8,128)(2,1)S(1)} %all-to-all-done.1.refs_2_, ...), custom_call_target="tpu_custom_call" | custom-call | tf_op jit(solution)/shard_map/pallas_call | solution.py:56
  71.9 2.5 %shard_map.85 = (f32[3,8,512]{2,1,0:T(8,128)S(1)}, f32[3,8,512]{2,1,0:T(8,128)S(1)}, f32[3,128,512]{2,1,0:T(8,128)S(1)}) custom-call(s32[2]{0:T(128)S(1)} %pad_add_fusion.refs_0_.place_ref, s32[112]{0:T(128)S(1)} %reshape.3.refs_1_, bf16[4,3,128,128]{3,2,1,0:T(8,128)(2,1)S(1)} %all-to-all-done.1.refs_2_, ...), custom_call_target="tpu_custom_call" | custom-call | tf_op jit(solution)/shard_map/pallas_call | solution.py:56
  74.4 0.0 collective-permute-done.1.refs_3_
  74.4 3.3 %shard_map.86 = bf16[4,3,128,128]{3,2,1,0:T(8,128)(2,1)} custom-call(s32[2]{0:T(128)S(1)} %pad_add_fusion.refs_0_.place_ref, s32[112]{0:T(128)S(1)} %reshape.3.refs_1_, bf16[4,3,128,128]{3,2,1,0:T(8,128)(2,1)S(1)} %all-to-all-done.1.refs_2_, bf16[4,2,3,128,128]{4,3,2,1,0:T(8,128)(2,1)} %collective-permute-done.1.refs_3_, ...), custom_call_target="tpu_custom_call" | custom-call | tf_op jit(solution)/shard_map/pallas_call | solution.py:56
  77.7 3.5 %all-to-all-start.2 = ((bf16[4,3,128,128]{3,2,1,0:T(8,128)(2,1)}), bf16[4,3,128,128]{3,2,1,0:T(8,128)(2,1)S(1)}, u32[]{:S(2)}, u32[]{:S(2)}) async-start(bf16[4,3,128,128]{3,2,1,0:T(8,128)(2,1)} %shard_map.86), calls=%async_computation.2 | async-start | bytes 786432 | tf_op jit(solution)/shard_map/all_to_all | solution.py:47
  81.8 0.0 collective-permute-done.9.far_hbm
  81.9 6.7 %all-to-all-done.2.o_ref = bf16[4,3,128,128]{3,2,1,0:T(8,128)(2,1)S(1)} async-done(((bf16[4,3,128,128]{3,2,1,0:T(8,128)(2,1)}), bf16[4,3,128,128]{3,2,1,0:T(8,128)(2,1)S(1)}, u32[]{:S(2)}, u32[]{:S(2)}) %all-to-all-start.2) | async-done | bytes 393248 | tf_op jit(solution)/shard_map/all_to_all | solution.py:47
  88.5 4.3 %project.1 = bf16[128,1536]{1,0:T(8,128)(2,1)} custom-call(s32[2]{0:T(128)S(1)} %pad_add_fusion.refs_0_.place_ref, s32[1]{0:T(128)S(6)} %copy.11.level_ref, bf16[4,3,128,128]{3,2,1,0:T(8,128)(2,1)S(1)} %all-to-all-done.2.o_ref, bf16[384,1536]{1,0:T(8,128)(2,1)S(1)} %collective-permute-done.6.weight_ref.near_ref, ...), custom_call_target="tpu_custom_call" | custom-call | tf_op jit(solution)/shard_map/project/pallas_call | solution.py:245
  (9 shorter events, 0.0 us)
Async XLA Ops:
  2.1 18.0 %all-to-all-start = ((bf16[4,2,3,128,128]{4,3,2,1,0:T(8,128)(2,1)}), bf16[4,2,3,128,128]{4,3,2,1,0:T(8,128)(2,1)S(1)}, u32[]{:S(2)}, u32[]{:S(2)}) async-start(bf16[4,2,3,128,128]{4,3,2,1,0:T(8,128)(2,1)} %pack_kv.1), calls=%async_computation | async-start | bytes 1572864 | tf_op jit(solution)/shard_map/all_to_all | solution.py:47
  6.4 45.9 %copy-start.1 = (s32[1,7,4,4]{1,3,2,0:T(4,128)S(1)}, s32[1,7,4,4]{1,3,2,0:T(4,128)}, u32[]{:S(2)}) copy-start(s32[1,7,4,4]{1,3,2,0:T(4,128)} %param.14) | copy-start | bytes 1348
  6.4 46.1 %copy-start = (bf16[128,1536]{1,0:T(8,128)(2,1)S(1)}, bf16[128,1536]{1,0:T(8,128)(2,1)}, u32[]{:S(2)}) copy-start(bf16[128,1536]{1,0:T(8,128)(2,1)} %query_ref) | copy-start | bytes 1179652
  6.4 24.9 %collective-permute-start.6 = (bf16[384,1536]{1,0:T(8,128)(2,1)}, bf16[384,1536]{1,0:T(8,128)(2,1)S(1)}, u32[]{:S(2)}, u32[]{:S(2)}) collective-permute-start(bf16[384,1536]{1,0:T(8,128)(2,1)} %own_hbm.1), channel_id=1, source_target_pairs={{1,0},{2,1},{3,2},{0,3},{7,4},{4,5},{5,6},{6,7},{9,8},{10,9},{11,1... | collective-permute-start | bytes 3538952 | tf_op jit(solution)/shard_map/ppermute | solution.py:43
  20.2 21.0 %collective-permute-start.2 = (bf16[4,2,3,128,128]{4,3,2,1,0:T(8,128)(2,1)S(1)}, bf16[4,2,3,128,128]{4,3,2,1,0:T(8,128)(2,1)}, u32[]{:S(2)}, u32[]{:S(2)}) collective-permute-start(bf16[4,2,3,128,128]{4,3,2,1,0:T(8,128)(2,1)S(1)} %all-to-all-done.refs_3_), channel_id=1, source_target_pairs={{8,0},{16,8},{4,12},{24,16},{12,20},{32,24},{20,28},{40,32},{28,36... | collective-permute-start | bytes 2359304 | tf_op jit(solution)/shard_map/ppermute | solution.py:21
  23.4 19.7 %collective-permute-start.5 = (bf16[4,2,3,128,128]{4,3,2,1,0:T(8,128)(2,1)S(1)}, bf16[4,2,3,128,128]{4,3,2,1,0:T(8,128)(2,1)S(1)}, u32[]{:S(2)}, u32[]{:S(2)}) collective-permute-start(bf16[4,2,3,128,128]{4,3,2,1,0:T(8,128)(2,1)S(1)} %all-to-all-done.refs_3_), channel_id=1, source_target_pairs={{4,0},{0,4},{12,8},{8,12},{20,16},{16,20},{28,24},{24,28},{36,32},... | collective-permute-start | bytes 2359304 | tf_op jit(solution)/shard_map/ppermute | solution.py:21
  25.4 19.7 %collective-permute-start = (bf16[4,2,3,128,128]{4,3,2,1,0:T(8,128)(2,1)S(1)}, bf16[4,2,3,128,128]{4,3,2,1,0:T(8,128)(2,1)}, u32[]{:S(2)}, u32[]{:S(2)}) collective-permute-start(bf16[4,2,3,128,128]{4,3,2,1,0:T(8,128)(2,1)S(1)} %all-to-all-done.refs_3_), channel_id=1, source_target_pairs={{12,4},{0,8},{20,12},{8,16},{28,20},{16,24},{36,28},{24,32},{44,36... | collective-permute-start | bytes 2359304 | tf_op jit(solution)/shard_map/ppermute | solution.py:21
  32.8 24.1 %collective-permute-start.7 = (bf16[384,768]{1,0:T(8,128)(2,1)}, bf16[384,768]{1,0:T(8,128)(2,1)}, u32[]{:S(2)}, u32[]{:S(2)}) collective-permute-start(bf16[384,768]{1,0:T(8,128)(2,1)} %shard_map.87), channel_id=1, source_target_pairs={{1,0},{2,1},{3,2},{0,3},{7,4},{4,5},{5,6},{6,7},{9,8},{10,9},{11,1... | collective-permute-start | bytes 1769480 | tf_op jit(solution)/shard_map/ppermute | solution.py:43
  35.6 46.2 %collective-permute-start.9 = (bf16[384,1536]{1,0:T(8,128)(2,1)S(1)}, bf16[384,1536]{1,0:T(8,128)(2,1)}, u32[]{:S(2)}, u32[]{:S(2)}) collective-permute-start(bf16[384,1536]{1,0:T(8,128)(2,1)S(1)} %collective-permute-done.6.weight_ref.near_ref), channel_id=1, source_target_pairs={{4,0},{0,4},{12,8},{8,12},{20,16},{16,20},{28,24},{24,28},{36,32},... | collective-permute-start | bytes 3538952 | tf_op jit(solution)/shard_map/ppermute | solution.py:21
  41.2 25.8 %collective-permute-start.4 = (bf16[4,2,3,128,128]{4,3,2,1,0:T(8,128)(2,1)}, bf16[4,2,3,128,128]{4,3,2,1,0:T(8,128)(2,1)}, u32[]{:S(2)}, u32[]{:S(2)}) collective-permute-start(bf16[4,2,3,128,128]{4,3,2,1,0:T(8,128)(2,1)} %collective-permute-done.2.refs_3_), channel_id=1, source_target_pairs={{4,0},{0,4},{12,8},{8,12},{20,16},{16,20},{28,24},{24,28},{36,32},... | collective-permute-start | bytes 2359304 | tf_op jit(solution)/shard_map/ppermute | solution.py:21
  43.1 28.8 %collective-permute-start.3 = (bf16[4,2,3,128,128]{4,3,2,1,0:T(8,128)(2,1)}, bf16[4,2,3,128,128]{4,3,2,1,0:T(8,128)(2,1)}, u32[]{:S(2)}, u32[]{:S(2)}) collective-permute-start(bf16[4,2,3,128,128]{4,3,2,1,0:T(8,128)(2,1)} %collective-permute-done.2.refs_3_), channel_id=1, source_target_pairs={{8,0},{16,8},{4,12},{24,16},{12,20},{32,24},{20,28},{40,32},{28,36... | collective-permute-start | bytes 2359304 | tf_op jit(solution)/shard_map/ppermute | solution.py:21
  45.0 29.3 %collective-permute-start.1 = (bf16[4,2,3,128,128]{4,3,2,1,0:T(8,128)(2,1)}, bf16[4,2,3,128,128]{4,3,2,1,0:T(8,128)(2,1)}, u32[]{:S(2)}, u32[]{:S(2)}) collective-permute-start(bf16[4,2,3,128,128]{4,3,2,1,0:T(8,128)(2,1)} %collective-permute-done.refs_5_), channel_id=1, source_target_pairs={{12,4},{0,8},{20,12},{8,16},{28,20},{16,24},{36,28},{24,32},{44,36... | collective-permute-start | bytes 2359304 | tf_op jit(solution)/shard_map/ppermute | solution.py:21
  53.4 10.8 %all-to-all-start.1 = ((bf16[4,3,128,128]{3,2,1,0:T(8,128)(2,1)}), bf16[4,3,128,128]{3,2,1,0:T(8,128)(2,1)S(1)}, u32[]{:S(2)}, u32[]{:S(2)}) async-start(bf16[4,3,128,128]{3,2,1,0:T(8,128)(2,1)} %shard_map.82), calls=%async_computation.1 | async-start | bytes 786432 | tf_op jit(solution)/shard_map/all_to_all | solution.py:47
  56.8 25.0 %collective-permute-start.8 = (bf16[384,768]{1,0:T(8,128)(2,1)}, bf16[384,768]{1,0:T(8,128)(2,1)}, u32[]{:S(2)}, u32[]{:S(2)}) collective-permute-start(bf16[384,768]{1,0:T(8,128)(2,1)} %collective-permute-done.7.mine_ref), channel_id=1, source_target_pairs={{4,0},{0,4},{12,8},{8,12},{20,16},{16,20},{28,24},{24,28},{36,32},... | collective-permute-start | bytes 1769480 | tf_op jit(solution)/shard_map/ppermute | solution.py:21
  77.7 10.8 %all-to-all-start.2 = ((bf16[4,3,128,128]{3,2,1,0:T(8,128)(2,1)}), bf16[4,3,128,128]{3,2,1,0:T(8,128)(2,1)S(1)}, u32[]{:S(2)}, u32[]{:S(2)}) async-start(bf16[4,3,128,128]{3,2,1,0:T(8,128)(2,1)} %shard_map.86), calls=%async_computation.2 | async-start | bytes 786432 | tf_op jit(solution)/shard_map/all_to_all | solution.py:47

commit v4 on v3

--- a/solution.py
+++ b/solution.py
@@ -200,11 +200,12 @@
 
 
 def project_kernel(
-    place_ref, level_ref, o_ref, near_ref, mine_ref, other_ref, own_hbm, far_hbm, gate_hbm,
-    residual_hbm, out_ref, own_ref, far_ref, gate_ref, residual_ref, sems,
+    place_ref, level_ref, o_ref, near_ref, other_ref, mine_hbm, own_hbm, far_hbm, gate_hbm,
+    residual_hbm, out_ref, mine_ref, own_ref, far_ref, gate_ref, residual_ref, sems,
 ):
     pairs = (
-        (own_hbm, own_ref), (far_hbm, far_ref), (gate_hbm, gate_ref), (residual_hbm, residual_ref)
+        (mine_hbm, mine_ref), (own_hbm, own_ref), (far_hbm, far_ref), (gate_hbm, gate_ref),
+        (residual_hbm, residual_ref),
     )
     copies = [pltpu.make_async_copy(*pair, sems.at[i]) for i, pair in enumerate(pairs)]
     for copy in copies:
@@ -220,18 +221,19 @@
     step = 1 + 2 * core
     own, near, far, opposite = features(0), features(step), features(4 - step), features(2)
     ats = [pl.ds(pl.multiple_of(c * half, 128), half) for c in (core, 1 - core)]
+    sums = [jnp.dot(near, near_ref[:, at], preferred_element_type=jnp.float32) for at in ats]
+    copies[0].wait()
     sums = [
-        jnp.dot(near, near_ref[:, at], preferred_element_type=jnp.float32)
-        + jnp.dot(opposite, opposite_ref[...], preferred_element_type=jnp.float32)
-        for at, opposite_ref in zip(ats, (mine_ref, other_ref), strict=True)
+        total + jnp.dot(opposite, opposite_ref[...], preferred_element_type=jnp.float32)
+        for total, opposite_ref in zip(sums, (mine_ref, other_ref), strict=True)
     ]
-    for copy, rows, weight_ref in zip(copies, (own, far), (own_ref, far_ref)):
+    for copy, rows, weight_ref in zip(copies[1:], (own, far), (own_ref, far_ref)):
         copy.wait()
         sums = [
             total + jnp.dot(rows, weight_ref[:, at], preferred_element_type=jnp.float32)
             for at, total in zip(ats, sums, strict=True)
         ]
-    for copy in copies[2:]:
+    for copy in copies[3:]:
         copy.wait()
     for at, total in zip(ats, sums, strict=True):
         gate = gate_ref[pl.ds(level_ref[0], 1), at]
@@ -296,7 +298,7 @@
     attention = attend(((5, 6),), place, mask, queries, [far_second], state, True)
     gathered = exchange(attention)
     return project(
-        (place, levels), (gathered, near, mine, other), (out_weight, far, gate_table, residual)
+        (place, levels), (gathered, near, other), (mine, out_weight, far, gate_table, residual)
     )
 
 

time: 93.5 us -> 93.5 us (level)
  no operation moved by 1% of the time
where the time goes in v4:
time: 93.5 us; the launch traced here: 92.7 us
  starting transfers between devices  45.3 us (48%)
  waiting for transfers between devices  24.2 us (26%)
  Pallas kernels  22 us (24%)
    ppermute x8, starting transfers between devices, to_frame(): return lax.ppermute(x, 'ctx', pairs)  26 us
    all_to_all x3, waiting for transfers between devices, exchange(): return lax.all_to_all(pieces, 'head', 0, 0, tiled=True)  20.5 us
    pallas_call x6, Pallas kernels, call(): pl.pallas_call(kernel, in_specs=specs, out_specs=jax.tree.map(lambda _: V...  15.7 us
    all_to_all x3, starting transfers between devices, exchange(): return lax.all_to_all(pieces, 'head', 0, 0, tiled=True)  11.2 us
    ppermute x2, starting transfers between devices, beside(): return lax.ppermute(x, ('ctx', 'head'), pairs)  8.12 us
    pallas_call x1, Pallas kernels, project(): pl.pallas_call(project_kernel, in_specs=[SMEM] * len(scalars) + [VMEM] *...  4.19 us
    ppermute x8, waiting for transfers between devices, to_frame(): return lax.ppermute(x, 'ctx', pairs)  3.64 us
    pallas_call x1, Pallas kernels, pack_kv(): pl.pallas_call(pack_kv_kernel, in_specs=[hbm, hbm], out_specs=VMEM, out_s...  2.12 us
  transfers between devices with their start and end apart: 13, of which 4 were waited for; matrix products, arithmetic and copies ran while one was open for 0% of the time, Pallas kernels for 17%

profile of v4, /device:TPU:248, one launch (start us, length us, event | category | flops | bytes accessed | tf_op | source)
XLA Modules:
  0.0 92.7 jit_solution(12410652066392395777)
XLA Ops:
  0.0 2.1 %pack_kv.1 = bf16[4,2,3,128,128]{4,3,2,1,0:T(8,128)(2,1)} custom-call(bf16[128,1536]{1,0:T(8,128)(2,1)} %key_hbm.1, bf16[128,1536]{1,0:T(8,128)(2,1)} %value_hbm.1), custom_call_target="tpu_custom_call" | custom-call | tf_op jit(solution)/shard_map/pack_kv/pallas_call | solution.py:85
  2.1 4.3 %all-to-all-start = ((bf16[4,2,3,128,128]{4,3,2,1,0:T(8,128)(2,1)}), bf16[4,2,3,128,128]{4,3,2,1,0:T(8,128)(2,1)S(1)}, u32[]{:S(2)}, u32[]{:S(2)}) async-start(bf16[4,2,3,128,128]{4,3,2,1,0:T(8,128)(2,1)} %pack_kv.1), calls=%async_computation | async-start | bytes 1572864 | tf_op jit(solution)/shard_map/all_to_all | solution.py:47
  6.4 5.3 %collective-permute-start.6 = (bf16[384,1536]{1,0:T(8,128)(2,1)}, bf16[384,1536]{1,0:T(8,128)(2,1)S(1)}, u32[]{:S(2)}, u32[]{:S(2)}) collective-permute-start(bf16[384,1536]{1,0:T(8,128)(2,1)} %own_hbm.1), channel_id=1, source_target_pairs={{1,0},{2,1},{3,2},{0,3},{7,4},{4,5},{5,6},{6,7},{9,8},{10,9},{11,1... | collective-permute-start | bytes 3538952 | tf_op jit(solution)/shard_map/ppermute | solution.py:43
  11.7 8.5 %all-to-all-done.refs_3_ = bf16[4,2,3,128,128]{4,3,2,1,0:T(8,128)(2,1)S(1)} async-done(((bf16[4,2,3,128,128]{4,3,2,1,0:T(8,128)(2,1)}), bf16[4,2,3,128,128]{4,3,2,1,0:T(8,128)(2,1)S(1)}, u32[]{:S(2)}, u32[]{:S(2)}) %all-to-all-start) | async-done | bytes 786464 | tf_op jit(solution)/shard_map/all_to_all | solution.py:47
  20.2 3.2 %collective-permute-start.2 = (bf16[4,2,3,128,128]{4,3,2,1,0:T(8,128)(2,1)S(1)}, bf16[4,2,3,128,128]{4,3,2,1,0:T(8,128)(2,1)}, u32[]{:S(2)}, u32[]{:S(2)}) collective-permute-start(bf16[4,2,3,128,128]{4,3,2,1,0:T(8,128)(2,1)S(1)} %all-to-all-done.refs_3_), channel_id=1, source_target_pairs={{8,0},{16,8},{4,12},{24,16},{12,20},{32,24},{20,28},{40,32},{28,36... | collective-permute-start | bytes 2359304 | tf_op jit(solution)/shard_map/ppermute | solution.py:21
  23.4 1.9 %collective-permute-start.5 = (bf16[4,2,3,128,128]{4,3,2,1,0:T(8,128)(2,1)S(1)}, bf16[4,2,3,128,128]{4,3,2,1,0:T(8,128)(2,1)S(1)}, u32[]{:S(2)}, u32[]{:S(2)}) collective-permute-start(bf16[4,2,3,128,128]{4,3,2,1,0:T(8,128)(2,1)S(1)} %all-to-all-done.refs_3_), channel_id=1, source_target_pairs={{4,0},{0,4},{12,8},{8,12},{20,16},{16,20},{28,24},{24,28},{36,32},... | collective-permute-start | bytes 2359304 | tf_op jit(solution)/shard_map/ppermute | solution.py:21
  25.4 5.9 %collective-permute-start = (bf16[4,2,3,128,128]{4,3,2,1,0:T(8,128)(2,1)S(1)}, bf16[4,2,3,128,128]{4,3,2,1,0:T(8,128)(2,1)}, u32[]{:S(2)}, u32[]{:S(2)}) collective-permute-start(bf16[4,2,3,128,128]{4,3,2,1,0:T(8,128)(2,1)S(1)} %all-to-all-done.refs_3_), channel_id=1, source_target_pairs={{12,4},{0,8},{20,12},{8,16},{28,20},{16,24},{36,28},{24,32},{44,36... | collective-permute-start | bytes 2359304 | tf_op jit(solution)/shard_map/ppermute | solution.py:21
  31.3 0.1 pad_add_fusion.refs_0_.place_ref
  31.4 0.0 collective-permute-done.6.weight_ref.near_ref
  31.4 1.4 %shard_map.87 = bf16[384,768]{1,0:T(8,128)(2,1)} custom-call(s32[2]{0:T(128)S(1)} %pad_add_fusion.refs_0_.place_ref, bf16[384,1536]{1,0:T(8,128)(2,1)S(1)} %collective-permute-done.6.weight_ref.near_ref), custom_call_target="tpu_custom_call" | custom-call | tf_op jit(solution)/shard_map/pallas_call | solution.py:56
  32.8 2.9 %collective-permute-start.7 = (bf16[384,768]{1,0:T(8,128)(2,1)}, bf16[384,768]{1,0:T(8,128)(2,1)}, u32[]{:S(2)}, u32[]{:S(2)}) collective-permute-start(bf16[384,768]{1,0:T(8,128)(2,1)} %shard_map.87), channel_id=1, source_target_pairs={{1,0},{2,1},{3,2},{0,3},{7,4},{4,5},{5,6},{6,7},{9,8},{10,9},{11,1... | collective-permute-start | bytes 1769480 | tf_op jit(solution)/shard_map/ppermute | solution.py:43
  35.6 1.9 %collective-permute-start.9 = (bf16[384,1536]{1,0:T(8,128)(2,1)S(1)}, bf16[384,1536]{1,0:T(8,128)(2,1)}, u32[]{:S(2)}, u32[]{:S(2)}) collective-permute-start(bf16[384,1536]{1,0:T(8,128)(2,1)S(1)} %collective-permute-done.6.weight_ref.near_ref), channel_id=1, source_target_pairs={{4,0},{0,4},{12,8},{8,12},{20,16},{16,20},{28,24},{24,28},{36,32},... | collective-permute-start | bytes 3538952 | tf_op jit(solution)/shard_map/ppermute | solution.py:21
  37.6 3.6 %collective-permute-done.2.refs_3_ = bf16[4,2,3,128,128]{4,3,2,1,0:T(8,128)(2,1)} collective-permute-done((bf16[4,2,3,128,128]{4,3,2,1,0:T(8,128)(2,1)S(1)}, bf16[4,2,3,128,128]{4,3,2,1,0:T(8,128)(2,1)}, u32[]{:S(2)}, u32[]{:S(2)}) %collective-permute-start.2) | collective-permute-done | bytes 786464 | tf_op jit(solution)/shard_map/ppermute | solution.py:21
  41.2 1.9 %collective-permute-start.4 = (bf16[4,2,3,128,128]{4,3,2,1,0:T(8,128)(2,1)}, bf16[4,2,3,128,128]{4,3,2,1,0:T(8,128)(2,1)}, u32[]{:S(2)}, u32[]{:S(2)}) collective-permute-start(bf16[4,2,3,128,128]{4,3,2,1,0:T(8,128)(2,1)} %collective-permute-done.2.refs_3_), channel_id=1, source_target_pairs={{4,0},{0,4},{12,8},{8,12},{20,16},{16,20},{28,24},{24,28},{36,32},... | collective-permute-start | bytes 2359304 | tf_op jit(solution)/shard_map/ppermute | solution.py:21
  43.1 1.9 %collective-permute-start.3 = (bf16[4,2,3,128,128]{4,3,2,1,0:T(8,128)(2,1)}, bf16[4,2,3,128,128]{4,3,2,1,0:T(8,128)(2,1)}, u32[]{:S(2)}, u32[]{:S(2)}) collective-permute-start(bf16[4,2,3,128,128]{4,3,2,1,0:T(8,128)(2,1)} %collective-permute-done.2.refs_3_), channel_id=1, source_target_pairs={{8,0},{16,8},{4,12},{24,16},{12,20},{32,24},{20,28},{40,32},{28,36... | collective-permute-start | bytes 2359304 | tf_op jit(solution)/shard_map/ppermute | solution.py:21
  45.0 7.2 %collective-permute-start.1 = (bf16[4,2,3,128,128]{4,3,2,1,0:T(8,128)(2,1)}, bf16[4,2,3,128,128]{4,3,2,1,0:T(8,128)(2,1)}, u32[]{:S(2)}, u32[]{:S(2)}) collective-permute-start(bf16[4,2,3,128,128]{4,3,2,1,0:T(8,128)(2,1)} %collective-permute-done.refs_5_), channel_id=1, source_target_pairs={{12,4},{0,8},{20,12},{8,16},{28,20},{16,24},{36,28},{24,32},{44,36... | collective-permute-start | bytes 2359304 | tf_op jit(solution)/shard_map/ppermute | solution.py:21
  52.3 0.1 copy.10
  52.4 0.1 reshape.3.refs_1_
  52.5 0.8 shard_map.82
  53.4 3.5 %all-to-all-start.1 = ((bf16[4,3,128,128]{3,2,1,0:T(8,128)(2,1)}), bf16[4,3,128,128]{3,2,1,0:T(8,128)(2,1)S(1)}, u32[]{:S(2)}, u32[]{:S(2)}) async-start(bf16[4,3,128,128]{3,2,1,0:T(8,128)(2,1)} %shard_map.82), calls=%async_computation.1 | async-start | bytes 786432 | tf_op jit(solution)/shard_map/all_to_all | solution.py:47
  56.8 1.9 %collective-permute-start.8 = (bf16[384,768]{1,0:T(8,128)(2,1)}, bf16[384,768]{1,0:T(8,128)(2,1)}, u32[]{:S(2)}, u32[]{:S(2)}) collective-permute-start(bf16[384,768]{1,0:T(8,128)(2,1)} %collective-permute-done.7.mine_hbm), channel_id=1, source_target_pairs={{4,0},{0,4},{12,8},{8,12},{20,16},{16,20},{28,24},{24,28},{36,32},... | collective-permute-start | bytes 1769480 | tf_op jit(solution)/shard_map/ppermute | solution.py:21
  58.8 5.4 %all-to-all-done.1.refs_2_ = bf16[4,3,128,128]{3,2,1,0:T(8,128)(2,1)S(1)} async-done(((bf16[4,3,128,128]{3,2,1,0:T(8,128)(2,1)}), bf16[4,3,128,128]{3,2,1,0:T(8,128)(2,1)S(1)}, u32[]{:S(2)}, u32[]{:S(2)}) %all-to-all-start.1) | async-done | bytes 393248 | tf_op jit(solution)/shard_map/all_to_all | solution.py:47
  64.2 2.8 %shard_map.83 = (f32[3,8,512]{2,1,0:T(8,128)S(1)}, f32[3,8,512]{2,1,0:T(8,128)S(1)}, f32[3,128,512]{2,1,0:T(8,128)S(1)}) custom-call(s32[2]{0:T(128)S(1)} %pad_add_fusion.refs_0_.place_ref, s32[112]{0:T(128)S(1)} %reshape.3.refs_1_, bf16[4,3,128,128]{3,2,1,0:T(8,128)(2,1)S(1)} %all-to-all-done.1.refs_2_, ...), custom_call_target="tpu_custom_call" | custom-call | tf_op jit(solution)/shard_map/pallas_call | solution.py:56
  67.0 0.0 collective-permute-done.4.refs_4_
  67.0 4.9 %shard_map.84 = (f32[3,8,512]{2,1,0:T(8,128)S(1)}, f32[3,8,512]{2,1,0:T(8,128)S(1)}, f32[3,128,512]{2,1,0:T(8,128)S(1)}) custom-call(s32[2]{0:T(128)S(1)} %pad_add_fusion.refs_0_.place_ref, s32[112]{0:T(128)S(1)} %reshape.3.refs_1_, bf16[4,3,128,128]{3,2,1,0:T(8,128)(2,1)S(1)} %all-to-all-done.1.refs_2_, ...), custom_call_target="tpu_custom_call" | custom-call | tf_op jit(solution)/shard_map/pallas_call | solution.py:56
  71.9 2.5 %shard_map.85 = (f32[3,8,512]{2,1,0:T(8,128)S(1)}, f32[3,8,512]{2,1,0:T(8,128)S(1)}, f32[3,128,512]{2,1,0:T(8,128)S(1)}) custom-call(s32[2]{0:T(128)S(1)} %pad_add_fusion.refs_0_.place_ref, s32[112]{0:T(128)S(1)} %reshape.3.refs_1_, bf16[4,3,128,128]{3,2,1,0:T(8,128)(2,1)S(1)} %all-to-all-done.1.refs_2_, ...), custom_call_target="tpu_custom_call" | custom-call | tf_op jit(solution)/shard_map/pallas_call | solution.py:56
  74.4 0.0 collective-permute-done.1.refs_3_
  74.4 3.3 %shard_map.86 = bf16[4,3,128,128]{3,2,1,0:T(8,128)(2,1)} custom-call(s32[2]{0:T(128)S(1)} %pad_add_fusion.refs_0_.place_ref, s32[112]{0:T(128)S(1)} %reshape.3.refs_1_, bf16[4,3,128,128]{3,2,1,0:T(8,128)(2,1)S(1)} %all-to-all-done.1.refs_2_, bf16[4,2,3,128,128]{4,3,2,1,0:T(8,128)(2,1)} %collective-permute-done.1.refs_3_, ...), custom_call_target="tpu_custom_call" | custom-call | tf_op jit(solution)/shard_map/pallas_call | solution.py:56
  77.7 3.5 %all-to-all-start.2 = ((bf16[4,3,128,128]{3,2,1,0:T(8,128)(2,1)}), bf16[4,3,128,128]{3,2,1,0:T(8,128)(2,1)S(1)}, u32[]{:S(2)}, u32[]{:S(2)}) async-start(bf16[4,3,128,128]{3,2,1,0:T(8,128)(2,1)} %shard_map.86), calls=%async_computation.2 | async-start | bytes 786432 | tf_op jit(solution)/shard_map/all_to_all | solution.py:47
  81.8 0.0 collective-permute-done.9.far_hbm
  81.9 6.7 %all-to-all-done.2.o_ref = bf16[4,3,128,128]{3,2,1,0:T(8,128)(2,1)S(1)} async-done(((bf16[4,3,128,128]{3,2,1,0:T(8,128)(2,1)}), bf16[4,3,128,128]{3,2,1,0:T(8,128)(2,1)S(1)}, u32[]{:S(2)}, u32[]{:S(2)}) %all-to-all-start.2) | async-done | bytes 393248 | tf_op jit(solution)/shard_map/all_to_all | solution.py:47
  88.5 4.2 %project.1 = bf16[128,1536]{1,0:T(8,128)(2,1)} custom-call(s32[2]{0:T(128)S(1)} %pad_add_fusion.refs_0_.place_ref, s32[1]{0:T(128)S(6)} %copy.11.level_ref, bf16[4,3,128,128]{3,2,1,0:T(8,128)(2,1)S(1)} %all-to-all-done.2.o_ref, bf16[384,1536]{1,0:T(8,128)(2,1)S(1)} %collective-permute-done.6.weight_ref.near_ref, ...), custom_call_target="tpu_custom_call" | custom-call | tf_op jit(solution)/shard_map/project/pallas_call | solution.py:247
  (9 shorter events, 0.0 us)
Async XLA Ops:
  2.1 18.0 %all-to-all-start = ((bf16[4,2,3,128,128]{4,3,2,1,0:T(8,128)(2,1)}), bf16[4,2,3,128,128]{4,3,2,1,0:T(8,128)(2,1)S(1)}, u32[]{:S(2)}, u32[]{:S(2)}) async-start(bf16[4,2,3,128,128]{4,3,2,1,0:T(8,128)(2,1)} %pack_kv.1), calls=%async_computation | async-start | bytes 1572864 | tf_op jit(solution)/shard_map/all_to_all | solution.py:47
  6.4 45.9 %copy-start.1 = (s32[1,7,4,4]{1,3,2,0:T(4,128)S(1)}, s32[1,7,4,4]{1,3,2,0:T(4,128)}, u32[]{:S(2)}) copy-start(s32[1,7,4,4]{1,3,2,0:T(4,128)} %param.14) | copy-start | bytes 1348
  6.4 46.1 %copy-start = (bf16[128,1536]{1,0:T(8,128)(2,1)S(1)}, bf16[128,1536]{1,0:T(8,128)(2,1)}, u32[]{:S(2)}) copy-start(bf16[128,1536]{1,0:T(8,128)(2,1)} %query_ref) | copy-start | bytes 1179652
  6.4 24.9 %collective-permute-start.6 = (bf16[384,1536]{1,0:T(8,128)(2,1)}, bf16[384,1536]{1,0:T(8,128)(2,1)S(1)}, u32[]{:S(2)}, u32[]{:S(2)}) collective-permute-start(bf16[384,1536]{1,0:T(8,128)(2,1)} %own_hbm.1), channel_id=1, source_target_pairs={{1,0},{2,1},{3,2},{0,3},{7,4},{4,5},{5,6},{6,7},{9,8},{10,9},{11,1... | collective-permute-start | bytes 3538952 | tf_op jit(solution)/shard_map/ppermute | solution.py:43
  20.2 21.0 %collective-permute-start.2 = (bf16[4,2,3,128,128]{4,3,2,1,0:T(8,128)(2,1)S(1)}, bf16[4,2,3,128,128]{4,3,2,1,0:T(8,128)(2,1)}, u32[]{:S(2)}, u32[]{:S(2)}) collective-permute-start(bf16[4,2,3,128,128]{4,3,2,1,0:T(8,128)(2,1)S(1)} %all-to-all-done.refs_3_), channel_id=1, source_target_pairs={{8,0},{16,8},{4,12},{24,16},{12,20},{32,24},{20,28},{40,32},{28,36... | collective-permute-start | bytes 2359304 | tf_op jit(solution)/shard_map/ppermute | solution.py:21
  23.4 19.7 %collective-permute-start.5 = (bf16[4,2,3,128,128]{4,3,2,1,0:T(8,128)(2,1)S(1)}, bf16[4,2,3,128,128]{4,3,2,1,0:T(8,128)(2,1)S(1)}, u32[]{:S(2)}, u32[]{:S(2)}) collective-permute-start(bf16[4,2,3,128,128]{4,3,2,1,0:T(8,128)(2,1)S(1)} %all-to-all-done.refs_3_), channel_id=1, source_target_pairs={{4,0},{0,4},{12,8},{8,12},{20,16},{16,20},{28,24},{24,28},{36,32},... | collective-permute-start | bytes 2359304 | tf_op jit(solution)/shard_map/ppermute | solution.py:21
  25.4 19.7 %collective-permute-start = (bf16[4,2,3,128,128]{4,3,2,1,0:T(8,128)(2,1)S(1)}, bf16[4,2,3,128,128]{4,3,2,1,0:T(8,128)(2,1)}, u32[]{:S(2)}, u32[]{:S(2)}) collective-permute-start(bf16[4,2,3,128,128]{4,3,2,1,0:T(8,128)(2,1)S(1)} %all-to-all-done.refs_3_), channel_id=1, source_target_pairs={{12,4},{0,8},{20,12},{8,16},{28,20},{16,24},{36,28},{24,32},{44,36... | collective-permute-start | bytes 2359304 | tf_op jit(solution)/shard_map/ppermute | solution.py:21
  32.8 24.1 %collective-permute-start.7 = (bf16[384,768]{1,0:T(8,128)(2,1)}, bf16[384,768]{1,0:T(8,128)(2,1)}, u32[]{:S(2)}, u32[]{:S(2)}) collective-permute-start(bf16[384,768]{1,0:T(8,128)(2,1)} %shard_map.87), channel_id=1, source_target_pairs={{1,0},{2,1},{3,2},{0,3},{7,4},{4,5},{5,6},{6,7},{9,8},{10,9},{11,1... | collective-permute-start | bytes 1769480 | tf_op jit(solution)/shard_map/ppermute | solution.py:43
  35.6 46.2 %collective-permute-start.9 = (bf16[384,1536]{1,0:T(8,128)(2,1)S(1)}, bf16[384,1536]{1,0:T(8,128)(2,1)}, u32[]{:S(2)}, u32[]{:S(2)}) collective-permute-start(bf16[384,1536]{1,0:T(8,128)(2,1)S(1)} %collective-permute-done.6.weight_ref.near_ref), channel_id=1, source_target_pairs={{4,0},{0,4},{12,8},{8,12},{20,16},{16,20},{28,24},{24,28},{36,32},... | collective-permute-start | bytes 3538952 | tf_op jit(solution)/shard_map/ppermute | solution.py:21
  41.2 25.8 %collective-permute-start.4 = (bf16[4,2,3,128,128]{4,3,2,1,0:T(8,128)(2,1)}, bf16[4,2,3,128,128]{4,3,2,1,0:T(8,128)(2,1)}, u32[]{:S(2)}, u32[]{:S(2)}) collective-permute-start(bf16[4,2,3,128,128]{4,3,2,1,0:T(8,128)(2,1)} %collective-permute-done.2.refs_3_), channel_id=1, source_target_pairs={{4,0},{0,4},{12,8},{8,12},{20,16},{16,20},{28,24},{24,28},{36,32},... | collective-permute-start | bytes 2359304 | tf_op jit(solution)/shard_map/ppermute | solution.py:21
  43.1 28.8 %collective-permute-start.3 = (bf16[4,2,3,128,128]{4,3,2,1,0:T(8,128)(2,1)}, bf16[4,2,3,128,128]{4,3,2,1,0:T(8,128)(2,1)}, u32[]{:S(2)}, u32[]{:S(2)}) collective-permute-start(bf16[4,2,3,128,128]{4,3,2,1,0:T(8,128)(2,1)} %collective-permute-done.2.refs_3_), channel_id=1, source_target_pairs={{8,0},{16,8},{4,12},{24,16},{12,20},{32,24},{20,28},{40,32},{28,36... | collective-permute-start | bytes 2359304 | tf_op jit(solution)/shard_map/ppermute | solution.py:21
  45.0 29.3 %collective-permute-start.1 = (bf16[4,2,3,128,128]{4,3,2,1,0:T(8,128)(2,1)}, bf16[4,2,3,128,128]{4,3,2,1,0:T(8,128)(2,1)}, u32[]{:S(2)}, u32[]{:S(2)}) collective-permute-start(bf16[4,2,3,128,128]{4,3,2,1,0:T(8,128)(2,1)} %collective-permute-done.refs_5_), channel_id=1, source_target_pairs={{12,4},{0,8},{20,12},{8,16},{28,20},{16,24},{36,28},{24,32},{44,36... | collective-permute-start | bytes 2359304 | tf_op jit(solution)/shard_map/ppermute | solution.py:21
  53.4 10.8 %all-to-all-start.1 = ((bf16[4,3,128,128]{3,2,1,0:T(8,128)(2,1)}), bf16[4,3,128,128]{3,2,1,0:T(8,128)(2,1)S(1)}, u32[]{:S(2)}, u32[]{:S(2)}) async-start(bf16[4,3,128,128]{3,2,1,0:T(8,128)(2,1)} %shard_map.82), calls=%async_computation.1 | async-start | bytes 786432 | tf_op jit(solution)/shard_map/all_to_all | solution.py:47
  56.8 25.0 %collective-permute-start.8 = (bf16[384,768]{1,0:T(8,128)(2,1)}, bf16[384,768]{1,0:T(8,128)(2,1)}, u32[]{:S(2)}, u32[]{:S(2)}) collective-permute-start(bf16[384,768]{1,0:T(8,128)(2,1)} %collective-permute-done.7.mine_hbm), channel_id=1, source_target_pairs={{4,0},{0,4},{12,8},{8,12},{20,16},{16,20},{28,24},{24,28},{36,32},... | collective-permute-start | bytes 1769480 | tf_op jit(solution)/shard_map/ppermute | solution.py:21
  77.7 10.8 %all-to-all-start.2 = ((bf16[4,3,128,128]{3,2,1,0:T(8,128)(2,1)}), bf16[4,3,128,128]{3,2,1,0:T(8,128)(2,1)S(1)}, u32[]{:S(2)}, u32[]{:S(2)}) async-start(bf16[4,3,128,128]{3,2,1,0:T(8,128)(2,1)} %shard_map.86), calls=%async_computation.2 | async-start | bytes 786432 | tf_op jit(solution)/shard_map/all_to_all | solution.py:47

commit v5 on v4

--- a/solution.py
+++ b/solution.py
@@ -47,7 +47,7 @@
     return lax.all_to_all(pieces, "head", 0, 0, tiled=True)
 
 
-def call(kernel, args, out_shape):
+def call(kernel, args, out_shape, out_specs=None, scratch_shapes=()):
     specs = [SMEM if a.dtype == jnp.int32 else VMEM for a in args]
     args = [
         a if a.dtype == jnp.int32 else pltpu.with_memory_space_constraint(a, pltpu.VMEM)
@@ -56,27 +56,39 @@
     return pl.pallas_call(
         kernel,
         in_specs=specs,
-        out_specs=jax.tree.map(lambda _: VMEM, out_shape),
+        out_specs=out_specs or jax.tree.map(lambda _: VMEM, out_shape),
+        scratch_shapes=scratch_shapes,
         out_shape=out_shape,
         compiler_params=pltpu.CompilerParams(vmem_limit_bytes=8 << 20),
     )(*args)
 
 
-def pack_kv_kernel(key_hbm, value_hbm, out_ref, key_ref, value_ref, sems):
+def pack_kv_kernel(key_hbm, value_hbm, out_hbm, key_ref, value_ref, out_ref, sems):
     groups, _, heads = out_ref.shape[:3]
-    fetch_value = pltpu.make_async_copy(value_hbm, value_ref, sems.at[0])
-    fetch_key = pltpu.make_async_copy(key_hbm, key_ref, sems.at[1])
-    fetch_value.start()
-    fetch_key.start()
-    places = [(g, h) for g in range(groups) for h in range(heads)]
-    fetch_value.wait()
-    for g, h in places:
-        at = slice((g * heads + h) * HEAD_DIM, (g * heads + h + 1) * HEAD_DIM)
-        out_ref[g, 1, h] = jnp.transpose(value_ref[:, at])
-    fetch_key.wait()
-    for g, h in places:
-        at = slice((g * heads + h) * HEAD_DIM, (g * heads + h + 1) * HEAD_DIM)
-        out_ref[g, 0, h] = key_ref[:, at]
+    width = heads * HEAD_DIM
+    fetches = [
+        [
+            pltpu.make_async_copy(hbm.at[:, columns], ref.at[:, columns], sems.at[i, g])
+            for i, (hbm, ref) in enumerate(((key_hbm, key_ref), (value_hbm, value_ref)))
+        ]
+        for g, columns in ((g, pl.ds(g * width, width)) for g in range(groups))
+    ]
+    sends = [
+        pltpu.make_async_copy(out_ref.at[g], out_hbm.at[g], sems.at[2, g]) for g in range(groups)
+    ]
+    for pair in fetches:
+        for fetch in pair:
+            fetch.start()
+    for g in range(groups):
+        for fetch in fetches[g]:
+            fetch.wait()
+        for h in range(heads):
+            at = slice((g * heads + h) * HEAD_DIM, (g * heads + h + 1) * HEAD_DIM)
+            out_ref[g, 0, h] = key_ref[:, at]
+            out_ref[g, 1, h] = jnp.transpose(value_ref[:, at])
+        sends[g].start()
+    for send in sends:
+        send.wait()
 
 
 def pack_kv(key_rows, value_rows, shape):
@@ -85,10 +97,10 @@
     return pl.pallas_call(
         pack_kv_kernel,
         in_specs=[hbm, hbm],
-        out_specs=VMEM,
+        out_specs=hbm,
         out_shape=jax.ShapeDtypeStruct(shape, jnp.bfloat16),
         scratch_shapes=[pltpu.VMEM(a.shape, a.dtype) for a in args]
-        + [pltpu.SemaphoreType.DMA((2,))],
+        + [pltpu.VMEM(shape, jnp.bfloat16), pltpu.SemaphoreType.DMA((3, shape[0]))],
         name="pack_kv",
         compiler_params=pltpu.CompilerParams(vmem_limit_bytes=8 << 20),
     )(*args)
@@ -171,7 +183,8 @@
         if last:
             attention = (weighted / total[0:1]).astype(jnp.bfloat16)
             for a in range(groups):
-                outs[0][a, h] = jnp.transpose(attention[:, a * BLOCK : (a + 1) * BLOCK])
+                outs[1][a, h] = jnp.transpose(attention[:, a * BLOCK : (a + 1) * BLOCK])
+            pltpu.make_async_copy(outs[1].at[:, h], outs[0].at[:, h], outs[2].at[h]).start()
         else:
             outs[0][h] = jnp.broadcast_to(peak, (8, rows))
             outs[1][h] = total
@@ -182,13 +195,21 @@
         ahead = score(h + 1) if h + 1 < heads else None
         gather(h, *soften(h, scores))
         scores = ahead
+    if last:
+        for h in range(heads):
+            pltpu.make_async_copy(outs[1].at[:, h], outs[0].at[:, h], outs[2].at[h]).wait()
 
 
 def attend(slots, place, mask, queries, kvs, state, last):
     groups, heads, tokens = queries.shape[:3]
     rows = groups * tokens
+    out_specs, scratch_shapes = None, ()
     if last:
         out_shape = jax.ShapeDtypeStruct(queries.shape, jnp.bfloat16)
+        out_specs = pl.BlockSpec(memory_space=pltpu.HBM)
+        scratch_shapes = [
+            pltpu.VMEM(queries.shape, jnp.bfloat16), pltpu.SemaphoreType.DMA((heads,))
+        ]
     else:
         stat = jax.ShapeDtypeStruct((heads, 8, rows), jnp.float32)
         out_shape = [stat, stat, jax.ShapeDtypeStruct((heads, HEAD_DIM, rows), jnp.float32)]
@@ -196,15 +217,16 @@
     def kernel(*refs):
         attend_kernel(slots, state is None, last, *refs)
 
-    return call(kernel, (place, mask, queries, *kvs, *(state or ())), out_shape)
+    args = (place, mask, queries, *kvs, *(state or ()))
+    return call(kernel, args, out_shape, out_specs, scratch_shapes)
 
 
 def project_kernel(
-    place_ref, level_ref, o_ref, near_ref, other_ref, mine_hbm, own_hbm, far_hbm, gate_hbm,
-    residual_hbm, out_ref, mine_ref, own_ref, far_ref, gate_ref, residual_ref, sems,
+    place_ref, level_ref, o_ref, near_ref, far_ref, other_ref, mine_hbm, own_hbm, gate_hbm,
+    residual_hbm, out_ref, mine_ref, own_ref, gate_ref, residual_ref, sems,
 ):
     pairs = (
-        (mine_hbm, mine_ref), (own_hbm, own_ref), (far_hbm, far_ref), (gate_hbm, gate_ref),
+        (mine_hbm, mine_ref), (own_hbm, own_ref), (gate_hbm, gate_ref),
         (residual_hbm, residual_ref),
     )
     copies = [pltpu.make_async_copy(*pair, sems.at[i]) for i, pair in enumerate(pairs)]
@@ -221,19 +243,22 @@
     step = 1 + 2 * core
     own, near, far, opposite = features(0), features(step), features(4 - step), features(2)
     ats = [pl.ds(pl.multiple_of(c * half, 128), half) for c in (core, 1 - core)]
-    sums = [jnp.dot(near, near_ref[:, at], preferred_element_type=jnp.float32) for at in ats]
+    sums = [
+        jnp.dot(near, near_ref[:, at], preferred_element_type=jnp.float32)
+        + jnp.dot(far, far_ref[:, at], preferred_element_type=jnp.float32)
+        for at in ats
+    ]
     copies[0].wait()
     sums = [
         total + jnp.dot(opposite, opposite_ref[...], preferred_element_type=jnp.float32)
         for total, opposite_ref in zip(sums, (mine_ref, other_ref), strict=True)
     ]
-    for copy, rows, weight_ref in zip(copies[1:], (own, far), (own_ref, far_ref)):
-        copy.wait()
-        sums = [
-            total + jnp.dot(rows, weight_ref[:, at], preferred_element_type=jnp.float32)
-            for at, total in zip(ats, sums, strict=True)
-        ]
-    for copy in copies[3:]:
+    copies[1].wait()
+    sums = [
+        total + jnp.dot(own, own_ref[:, at], preferred_element_type=jnp.float32)
+        for total, at in zip(sums, ats, strict=True)
+    ]
+    for copy in copies[2:]:
         copy.wait()
     for at, total in zip(ats, sums, strict=True):
         gate = gate_ref[pl.ds(level_ref[0], 1), at]
@@ -281,7 +306,7 @@
     first = to_frame(own, outward)
     second = to_frame(own, inward)
     queries = exchange(after(q_send, own))
-    swapped = to_frame(own, partner)
+    swapped = to_frame(after(own, queries), partner)
     half_shape = jax.ShapeDtypeStruct((near.shape[0], width // 2), jnp.bfloat16)
     near_half = call(half_kernel, (place, near), half_shape)
     mine = beside(near_half)
@@ -298,7 +323,7 @@
     attention = attend(((5, 6),), place, mask, queries, [far_second], state, True)
     gathered = exchange(attention)
     return project(
-        (place, levels), (gathered, near, other), (mine, out_weight, far, gate_table, residual)
+        (place, levels), (gathered, near, far, other), (mine, out_weight, gate_table, residual)
     )
 
 

time: 93.5 us -> 97.4 us (1.042)
  starting transfers between devices: 45.3 us -> 49.7 us
  Pallas kernels: 22 us -> 19.8 us
  local copies, waits for them, and re-layouts: 0.23 us -> 1.53 us
    ppermute x8, waiting for transfers between devices: 3.64 us -> 11.2 us  [to_frame(): return lax.ppermute(x, 'ctx', pairs)]
    all_to_all x3, waiting for transfers between devices: 20.5 us -> 13.4 us  [exchange(): return lax.all_to_all(pieces, 'head', 0, 0, tiled=True)]
    ppermute x8, starting transfers between devices: 26 us -> 28.7 us  [to_frame(): return lax.ppermute(x, 'ctx', pairs)]
    pallas_call x7, Pallas kernels: 17.8 us -> 15.6 us  [the longest x6 13.4 us: call(): pl.pallas_call(kernel, in_specs=specs, out_specs=out_specs or jax.tree.ma...]
    all_to_all x3, starting transfers between devices: 11.2 us -> 12.9 us  [exchange(): return lax.all_to_all(pieces, 'head', 0, 0, tiled=True)]
  transfers between devices with their start and end apart: 13 -> 13, of which waited for: 4 -> 5; matrix products, arithmetic and copies ran while one was open for 0% -> 2% of each run, Pallas kernels for 17% -> 14%
where the time goes in v5:
time: 97.4 us; the launch traced here: 96.6 us
  starting transfers between devices  49.7 us (51%)
  waiting for transfers between devices  24.6 us (25%)
  Pallas kernels  19.8 us (20%)
  local copies, waits for them, and re-layouts  1.53 us (2%)
    ppermute x8, starting transfers between devices, to_frame(): return lax.ppermute(x, 'ctx', pairs)  28.7 us
    pallas_call x6, Pallas kernels, call(): pl.pallas_call(kernel, in_specs=specs, out_specs=out_specs or jax.tree.ma...  13.4 us
    all_to_all x3, waiting for transfers between devices, exchange(): return lax.all_to_all(pieces, 'head', 0, 0, tiled=True)  13.4 us
    all_to_all x3, starting transfers between devices, exchange(): return lax.all_to_all(pieces, 'head', 0, 0, tiled=True)  12.9 us
    ppermute x8, waiting for transfers between devices, to_frame(): return lax.ppermute(x, 'ctx', pairs)  11.2 us
    ppermute x2, starting transfers between devices, beside(): return lax.ppermute(x, ('ctx', 'head'), pairs)  8 us
    pallas_call x1, Pallas kernels, project(): pl.pallas_call(project_kernel, in_specs=[SMEM] * len(scalars) + [VMEM] *...  4.21 us
    pallas_call x1, Pallas kernels, pack_kv(): pl.pallas_call(pack_kv_kernel, in_specs=[hbm, hbm], out_specs=hbm, out_sh...  2.19 us
  transfers between devices with their start and end apart: 13, of which 5 were waited for; matrix products, arithmetic and copies ran while one was open for 2% of the time, Pallas kernels for 14%

profile of v5, /device:TPU:248, one launch (start us, length us, event | category | flops | bytes accessed | tf_op | source)
XLA Modules:
  0.0 96.6 jit_solution(6307876866984893779)
XLA Ops:
  0.0 2.2 %pack_kv.1 = bf16[4,2,3,128,128]{4,3,2,1,0:T(8,128)(2,1)} custom-call(bf16[128,1536]{1,0:T(8,128)(2,1)} %key_hbm.1, bf16[128,1536]{1,0:T(8,128)(2,1)} %value_hbm.1), custom_call_target="tpu_custom_call" | custom-call | tf_op jit(solution)/shard_map/pack_kv/pallas_call | solution.py:97
  2.2 0.0 copy-start.2
  2.2 0.0 copy-start
  2.2 4.4 %all-to-all-start = ((bf16[4,2,3,128,128]{4,3,2,1,0:T(8,128)(2,1)}), bf16[4,2,3,128,128]{4,3,2,1,0:T(8,128)(2,1)S(1)}, u32[]{:S(2)}, u32[]{:S(2)}) async-start(bf16[4,2,3,128,128]{4,3,2,1,0:T(8,128)(2,1)} %pack_kv.1), calls=%async_computation | async-start | bytes 1572864 | tf_op jit(solution)/shard_map/all_to_all | solution.py:47
  6.7 5.1 %collective-permute-start.6 = (bf16[384,1536]{1,0:T(8,128)(2,1)S(1)}, bf16[384,1536]{1,0:T(8,128)(2,1)S(1)}, u32[]{:S(2)}, u32[]{:S(2)}) collective-permute-start(bf16[384,1536]{1,0:T(8,128)(2,1)S(1)} %copy-done.1), channel_id=1, source_target_pairs={{1,0},{2,1},{3,2},{0,3},{7,4},{4,5},{5,6},{6,7},{9,8},{10,9},{11,1... | collective-permute-start | bytes 3538952 | tf_op jit(solution)/shard_map/ppermute | solution.py:43
  11.8 0.7 copy.10
  12.5 0.8 reshape.3.refs_1_
  13.4 0.1 pad_add_fusion.refs_0_.place_ref
  13.4 0.8 shard_map.82
  14.2 6.2 %all-to-all-done.refs_3_ = bf16[4,2,3,128,128]{4,3,2,1,0:T(8,128)(2,1)S(1)} async-done(((bf16[4,2,3,128,128]{4,3,2,1,0:T(8,128)(2,1)}), bf16[4,2,3,128,128]{4,3,2,1,0:T(8,128)(2,1)S(1)}, u32[]{:S(2)}, u32[]{:S(2)}) %all-to-all-start) | async-done | bytes 786464 | tf_op jit(solution)/shard_map/all_to_all | solution.py:47
  20.4 3.5 %all-to-all-start.1 = ((bf16[4,3,128,128]{3,2,1,0:T(8,128)(2,1)}), bf16[4,3,128,128]{3,2,1,0:T(8,128)(2,1)S(1)}, u32[]{:S(2)}, u32[]{:S(2)}) async-start(bf16[4,3,128,128]{3,2,1,0:T(8,128)(2,1)} %shard_map.82), calls=%async_computation.1 | async-start | bytes 786432 | tf_op jit(solution)/shard_map/all_to_all | solution.py:47
  23.9 3.3 %collective-permute-start.2 = (bf16[4,2,3,128,128]{4,3,2,1,0:T(8,128)(2,1)S(1)}, bf16[4,2,3,128,128]{4,3,2,1,0:T(8,128)(2,1)}, u32[]{:S(2)}, u32[]{:S(2)}) collective-permute-start(bf16[4,2,3,128,128]{4,3,2,1,0:T(8,128)(2,1)S(1)} %all-to-all-done.refs_3_), channel_id=1, source_target_pairs={{8,0},{16,8},{4,12},{24,16},{12,20},{32,24},{20,28},{40,32},{28,36... | collective-permute-start | bytes 2359304 | tf_op jit(solution)/shard_map/ppermute | solution.py:21
  27.1 5.9 %collective-permute-start = (bf16[4,2,3,128,128]{4,3,2,1,0:T(8,128)(2,1)S(1)}, bf16[4,2,3,128,128]{4,3,2,1,0:T(8,128)(2,1)}, u32[]{:S(2)}, u32[]{:S(2)}) collective-permute-start(bf16[4,2,3,128,128]{4,3,2,1,0:T(8,128)(2,1)S(1)} %all-to-all-done.refs_3_), channel_id=1, source_target_pairs={{12,4},{0,8},{20,12},{8,16},{28,20},{16,24},{36,28},{24,32},{44,36... | collective-permute-start | bytes 2359304 | tf_op jit(solution)/shard_map/ppermute | solution.py:21
  33.1 0.3 all-to-all-done.1.refs_2_
  33.3 4.6 %collective-permute-start.5 = (bf16[4,2,3,128,128]{4,3,2,1,0:T(8,128)(2,1)S(1)}, bf16[4,2,3,128,128]{4,3,2,1,0:T(8,128)(2,1)S(1)}, u32[]{:S(2)}, u32[]{:S(2)}) collective-permute-start(bf16[4,2,3,128,128]{4,3,2,1,0:T(8,128)(2,1)S(1)} %all-to-all-done.refs_3_), channel_id=1, source_target_pairs={{4,0},{0,4},{12,8},{8,12},{20,16},{16,20},{28,24},{24,28},{36,32},... | collective-permute-start | bytes 2359304 | tf_op jit(solution)/shard_map/ppermute | solution.py:21
  38.0 0.6 shard_map.87
  38.6 2.9 %collective-permute-start.8 = (bf16[384,768]{1,0:T(8,128)(2,1)S(1)}, bf16[384,768]{1,0:T(8,128)(2,1)}, u32[]{:S(2)}, u32[]{:S(2)}) collective-permute-start(bf16[384,768]{1,0:T(8,128)(2,1)S(1)} %shard_map.87), channel_id=1, source_target_pairs={{1,0},{2,1},{3,2},{0,3},{7,4},{4,5},{5,6},{6,7},{9,8},{10,9},{11,1... | collective-permute-start | bytes 1769480 | tf_op jit(solution)/shard_map/ppermute | solution.py:43
  41.5 1.9 %collective-permute-start.7 = (bf16[384,1536]{1,0:T(8,128)(2,1)S(1)}, bf16[384,1536]{1,0:T(8,128)(2,1)S(1)}, u32[]{:S(2)}, u32[]{:S(2)}) collective-permute-start(bf16[384,1536]{1,0:T(8,128)(2,1)S(1)} %collective-permute-done.6.weight_ref.near_ref), channel_id=1, source_target_pairs={{4,0},{0,4},{12,8},{8,12},{20,16},{16,20},{28,24},{24,28},{36,32},... | collective-permute-start | bytes 3538952 | tf_op jit(solution)/shard_map/ppermute | solution.py:21
  43.4 5.5 %collective-permute-done.2.refs_3_ = bf16[4,2,3,128,128]{4,3,2,1,0:T(8,128)(2,1)} collective-permute-done((bf16[4,2,3,128,128]{4,3,2,1,0:T(8,128)(2,1)S(1)}, bf16[4,2,3,128,128]{4,3,2,1,0:T(8,128)(2,1)}, u32[]{:S(2)}, u32[]{:S(2)}) %collective-permute-start.2) | collective-permute-done | bytes 786464 | tf_op jit(solution)/shard_map/ppermute | solution.py:21
  48.9 1.9 %collective-permute-start.4 = (bf16[4,2,3,128,128]{4,3,2,1,0:T(8,128)(2,1)}, bf16[4,2,3,128,128]{4,3,2,1,0:T(8,128)(2,1)S(1)}, u32[]{:S(2)}, u32[]{:S(2)}) collective-permute-start(bf16[4,2,3,128,128]{4,3,2,1,0:T(8,128)(2,1)} %collective-permute-done.2.refs_3_), channel_id=1, source_target_pairs={{4,0},{0,4},{12,8},{8,12},{20,16},{16,20},{28,24},{24,28},{36,32},... | collective-permute-start | bytes 2359304 | tf_op jit(solution)/shard_map/ppermute | solution.py:21
  50.8 0.0 collective-permute-done.refs_5_
  50.8 1.9 %collective-permute-start.3 = (bf16[4,2,3,128,128]{4,3,2,1,0:T(8,128)(2,1)}, bf16[4,2,3,128,128]{4,3,2,1,0:T(8,128)(2,1)S(1)}, u32[]{:S(2)}, u32[]{:S(2)}) collective-permute-start(bf16[4,2,3,128,128]{4,3,2,1,0:T(8,128)(2,1)} %collective-permute-done.2.refs_3_), channel_id=1, source_target_pairs={{8,0},{16,8},{4,12},{24,16},{12,20},{32,24},{20,28},{40,32},{28,36... | collective-permute-start | bytes 2359304 | tf_op jit(solution)/shard_map/ppermute | solution.py:21
  52.7 7.2 %collective-permute-start.1 = (bf16[4,2,3,128,128]{4,3,2,1,0:T(8,128)(2,1)}, bf16[4,2,3,128,128]{4,3,2,1,0:T(8,128)(2,1)S(1)}, u32[]{:S(2)}, u32[]{:S(2)}) collective-permute-start(bf16[4,2,3,128,128]{4,3,2,1,0:T(8,128)(2,1)} %collective-permute-done.refs_5_), channel_id=1, source_target_pairs={{12,4},{0,8},{20,12},{8,16},{28,20},{16,24},{36,28},{24,32},{44,36... | collective-permute-start | bytes 2359304 | tf_op jit(solution)/shard_map/ppermute | solution.py:21
  60.0 1.9 %collective-permute-start.9 = (bf16[384,768]{1,0:T(8,128)(2,1)}, bf16[384,768]{1,0:T(8,128)(2,1)}, u32[]{:S(2)}, u32[]{:S(2)}) collective-permute-start(bf16[384,768]{1,0:T(8,128)(2,1)} %collective-permute-done.8.mine_hbm), channel_id=1, source_target_pairs={{4,0},{0,4},{12,8},{8,12},{20,16},{16,20},{28,24},{24,28},{36,32},... | collective-permute-start | bytes 1769480 | tf_op jit(solution)/shard_map/ppermute | solution.py:21
  61.9 2.8 %shard_map.83 = (f32[3,8,512]{2,1,0:T(8,128)S(1)}, f32[3,8,512]{2,1,0:T(8,128)S(1)}, f32[3,128,512]{2,1,0:T(8,128)S(1)}) custom-call(s32[2]{0:T(128)S(1)} %pad_add_fusion.refs_0_.place_ref, s32[112]{0:T(128)S(1)} %reshape.3.refs_1_, bf16[4,3,128,128]{3,2,1,0:T(8,128)(2,1)S(1)} %all-to-all-done.1.refs_2_, ...), custom_call_target="tpu_custom_call" | custom-call | tf_op jit(solution)/shard_map/pallas_call | solution.py:56
  64.7 4.7 %shard_map.84 = (f32[3,8,512]{2,1,0:T(8,128)S(1)}, f32[3,8,512]{2,1,0:T(8,128)S(1)}, f32[3,128,512]{2,1,0:T(8,128)S(1)}) custom-call(s32[2]{0:T(128)S(1)} %pad_add_fusion.refs_0_.place_ref, s32[112]{0:T(128)S(1)} %reshape.3.refs_1_, bf16[4,3,128,128]{3,2,1,0:T(8,128)(2,1)S(1)} %all-to-all-done.1.refs_2_, ...), custom_call_target="tpu_custom_call" | custom-call | tf_op jit(solution)/shard_map/pallas_call | solution.py:56
  69.4 5.7 %collective-permute-done.3.refs_3_ = bf16[4,2,3,128,128]{4,3,2,1,0:T(8,128)(2,1)S(1)} collective-permute-done((bf16[4,2,3,128,128]{4,3,2,1,0:T(8,128)(2,1)}, bf16[4,2,3,128,128]{4,3,2,1,0:T(8,128)(2,1)S(1)}, u32[]{:S(2)}, u32[]{:S(2)}) %collective-permute-start.3) | collective-permute-done | bytes 786464 | tf_op jit(solution)/shard_map/ppermute | solution.py:21
  75.2 1.9 %shard_map.85 = (f32[3,8,512]{2,1,0:T(8,128)S(1)}, f32[3,8,512]{2,1,0:T(8,128)S(1)}, f32[3,128,512]{2,1,0:T(8,128)S(1)}) custom-call(s32[2]{0:T(128)S(1)} %pad_add_fusion.refs_0_.place_ref, s32[112]{0:T(128)S(1)} %reshape.3.refs_1_, bf16[4,3,128,128]{3,2,1,0:T(8,128)(2,1)S(1)} %all-to-all-done.1.refs_2_, ...), custom_call_target="tpu_custom_call" | custom-call | tf_op jit(solution)/shard_map/pallas_call | solution.py:56
  77.0 2.7 %shard_map.86 = bf16[4,3,128,128]{3,2,1,0:T(8,128)(2,1)} custom-call(s32[2]{0:T(128)S(1)} %pad_add_fusion.refs_0_.place_ref, s32[112]{0:T(128)S(1)} %reshape.3.refs_1_, bf16[4,3,128,128]{3,2,1,0:T(8,128)(2,1)S(1)} %all-to-all-done.1.refs_2_, bf16[4,2,3,128,128]{4,3,2,1,0:T(8,128)(2,1)S(1)} %collective-permute-done.1.refs_3_, ...), custom_call_target="tpu_custom_call" | custom-call | tf_op jit(solution)/shard_map/pallas_call | solution.py:56
  79.7 5.0 %all-to-all-start.2 = ((bf16[4,3,128,128]{3,2,1,0:T(8,128)(2,1)}), bf16[4,3,128,128]{3,2,1,0:T(8,128)(2,1)S(1)}, u32[]{:S(2)}, u32[]{:S(2)}) async-start(bf16[4,3,128,128]{3,2,1,0:T(8,128)(2,1)} %shard_map.86), calls=%async_computation.2 | async-start | bytes 786432 | tf_op jit(solution)/shard_map/all_to_all | solution.py:47
  85.4 7.0 %all-to-all-done.2.o_ref = bf16[4,3,128,128]{3,2,1,0:T(8,128)(2,1)S(1)} async-done(((bf16[4,3,128,128]{3,2,1,0:T(8,128)(2,1)}), bf16[4,3,128,128]{3,2,1,0:T(8,128)(2,1)S(1)}, u32[]{:S(2)}, u32[]{:S(2)}) %all-to-all-start.2) | async-done | bytes 393248 | tf_op jit(solution)/shard_map/all_to_all | solution.py:47
  92.4 4.2 %project.1 = bf16[128,1536]{1,0:T(8,128)(2,1)} custom-call(s32[2]{0:T(128)S(1)} %pad_add_fusion.refs_0_.place_ref, s32[1]{0:T(128)S(6)} %copy.11.level_ref, bf16[4,3,128,128]{3,2,1,0:T(8,128)(2,1)S(1)} %all-to-all-done.2.o_ref, bf16[384,1536]{1,0:T(8,128)(2,1)S(1)} %collective-permute-done.6.weight_ref.near_ref, ...), custom_call_target="tpu_custom_call" | custom-call | tf_op jit(solution)/shard_map/project/pallas_call | solution.py:272
  (11 shorter events, 0.0 us)
Async XLA Ops:
  0.0 6.7 %copy-start.1 = (bf16[384,1536]{1,0:T(8,128)(2,1)S(1)}, bf16[384,1536]{1,0:T(8,128)(2,1)}, u32[]{:S(2)}) copy-start(bf16[384,1536]{1,0:T(8,128)(2,1)} %own_hbm.1) | copy-start | bytes 3538948
  2.2 9.6 %copy-start.2 = (s32[1,7,4,4]{1,3,2,0:T(4,128)S(1)}, s32[1,7,4,4]{1,3,2,0:T(4,128)}, u32[]{:S(2)}) copy-start(s32[1,7,4,4]{1,3,2,0:T(4,128)} %param.14) | copy-start | bytes 1348
  2.2 11.2 %copy-start = (bf16[128,1536]{1,0:T(8,128)(2,1)S(1)}, bf16[128,1536]{1,0:T(8,128)(2,1)}, u32[]{:S(2)}) copy-start(bf16[128,1536]{1,0:T(8,128)(2,1)} %query_ref) | copy-start | bytes 1179652
  2.2 18.2 %all-to-all-start = ((bf16[4,2,3,128,128]{4,3,2,1,0:T(8,128)(2,1)}), bf16[4,2,3,128,128]{4,3,2,1,0:T(8,128)(2,1)S(1)}, u32[]{:S(2)}, u32[]{:S(2)}) async-start(bf16[4,2,3,128,128]{4,3,2,1,0:T(8,128)(2,1)} %pack_kv.1), calls=%async_computation | async-start | bytes 1572864 | tf_op jit(solution)/shard_map/all_to_all | solution.py:47
  6.7 31.3 %collective-permute-start.6 = (bf16[384,1536]{1,0:T(8,128)(2,1)S(1)}, bf16[384,1536]{1,0:T(8,128)(2,1)S(1)}, u32[]{:S(2)}, u32[]{:S(2)}) collective-permute-start(bf16[384,1536]{1,0:T(8,128)(2,1)S(1)} %copy-done.1), channel_id=1, source_target_pairs={{1,0},{2,1},{3,2},{0,3},{7,4},{4,5},{5,6},{6,7},{9,8},{10,9},{11,1... | collective-permute-start | bytes 3538952 | tf_op jit(solution)/shard_map/ppermute | solution.py:43
  20.4 12.9 %all-to-all-start.1 = ((bf16[4,3,128,128]{3,2,1,0:T(8,128)(2,1)}), bf16[4,3,128,128]{3,2,1,0:T(8,128)(2,1)S(1)}, u32[]{:S(2)}, u32[]{:S(2)}) async-start(bf16[4,3,128,128]{3,2,1,0:T(8,128)(2,1)} %shard_map.82), calls=%async_computation.1 | async-start | bytes 786432 | tf_op jit(solution)/shard_map/all_to_all | solution.py:47
  23.9 25.0 %collective-permute-start.2 = (bf16[4,2,3,128,128]{4,3,2,1,0:T(8,128)(2,1)S(1)}, bf16[4,2,3,128,128]{4,3,2,1,0:T(8,128)(2,1)}, u32[]{:S(2)}, u32[]{:S(2)}) collective-permute-start(bf16[4,2,3,128,128]{4,3,2,1,0:T(8,128)(2,1)S(1)} %all-to-all-done.refs_3_), channel_id=1, source_target_pairs={{8,0},{16,8},{4,12},{24,16},{12,20},{32,24},{20,28},{40,32},{28,36... | collective-permute-start | bytes 2359304 | tf_op jit(solution)/shard_map/ppermute | solution.py:21
  27.1 23.6 %collective-permute-start = (bf16[4,2,3,128,128]{4,3,2,1,0:T(8,128)(2,1)S(1)}, bf16[4,2,3,128,128]{4,3,2,1,0:T(8,128)(2,1)}, u32[]{:S(2)}, u32[]{:S(2)}) collective-permute-start(bf16[4,2,3,128,128]{4,3,2,1,0:T(8,128)(2,1)S(1)} %all-to-all-done.refs_3_), channel_id=1, source_target_pairs={{12,4},{0,8},{20,12},{8,16},{28,20},{16,24},{36,28},{24,32},{44,36... | collective-permute-start | bytes 2359304 | tf_op jit(solution)/shard_map/ppermute | solution.py:21
  33.3 19.4 %collective-permute-start.5 = (bf16[4,2,3,128,128]{4,3,2,1,0:T(8,128)(2,1)S(1)}, bf16[4,2,3,128,128]{4,3,2,1,0:T(8,128)(2,1)S(1)}, u32[]{:S(2)}, u32[]{:S(2)}) collective-permute-start(bf16[4,2,3,128,128]{4,3,2,1,0:T(8,128)(2,1)S(1)} %all-to-all-done.refs_3_), channel_id=1, source_target_pairs={{4,0},{0,4},{12,8},{8,12},{20,16},{16,20},{28,24},{24,28},{36,32},... | collective-permute-start | bytes 2359304 | tf_op jit(solution)/shard_map/ppermute | solution.py:21
  38.6 21.4 %collective-permute-start.8 = (bf16[384,768]{1,0:T(8,128)(2,1)S(1)}, bf16[384,768]{1,0:T(8,128)(2,1)}, u32[]{:S(2)}, u32[]{:S(2)}) collective-permute-start(bf16[384,768]{1,0:T(8,128)(2,1)S(1)} %shard_map.87), channel_id=1, source_target_pairs={{1,0},{2,1},{3,2},{0,3},{7,4},{4,5},{5,6},{6,7},{9,8},{10,9},{11,1... | collective-permute-start | bytes 1769480 | tf_op jit(solution)/shard_map/ppermute | solution.py:43
  41.5 44.0 %collective-permute-start.7 = (bf16[384,1536]{1,0:T(8,128)(2,1)S(1)}, bf16[384,1536]{1,0:T(8,128)(2,1)S(1)}, u32[]{:S(2)}, u32[]{:S(2)}) collective-permute-start(bf16[384,1536]{1,0:T(8,128)(2,1)S(1)} %collective-permute-done.6.weight_ref.near_ref), channel_id=1, source_target_pairs={{4,0},{0,4},{12,8},{8,12},{20,16},{16,20},{28,24},{24,28},{36,32},... | collective-permute-start | bytes 3538952 | tf_op jit(solution)/shard_map/ppermute | solution.py:21
  48.9 15.9 %collective-permute-start.4 = (bf16[4,2,3,128,128]{4,3,2,1,0:T(8,128)(2,1)}, bf16[4,2,3,128,128]{4,3,2,1,0:T(8,128)(2,1)S(1)}, u32[]{:S(2)}, u32[]{:S(2)}) collective-permute-start(bf16[4,2,3,128,128]{4,3,2,1,0:T(8,128)(2,1)} %collective-permute-done.2.refs_3_), channel_id=1, source_target_pairs={{4,0},{0,4},{12,8},{8,12},{20,16},{16,20},{28,24},{24,28},{36,32},... | collective-permute-start | bytes 2359304 | tf_op jit(solution)/shard_map/ppermute | solution.py:21
  50.8 24.4 %collective-permute-start.3 = (bf16[4,2,3,128,128]{4,3,2,1,0:T(8,128)(2,1)}, bf16[4,2,3,128,128]{4,3,2,1,0:T(8,128)(2,1)S(1)}, u32[]{:S(2)}, u32[]{:S(2)}) collective-permute-start(bf16[4,2,3,128,128]{4,3,2,1,0:T(8,128)(2,1)} %collective-permute-done.2.refs_3_), channel_id=1, source_target_pairs={{8,0},{16,8},{4,12},{24,16},{12,20},{32,24},{20,28},{40,32},{28,36... | collective-permute-start | bytes 2359304 | tf_op jit(solution)/shard_map/ppermute | solution.py:21
  52.7 24.3 %collective-permute-start.1 = (bf16[4,2,3,128,128]{4,3,2,1,0:T(8,128)(2,1)}, bf16[4,2,3,128,128]{4,3,2,1,0:T(8,128)(2,1)S(1)}, u32[]{:S(2)}, u32[]{:S(2)}) collective-permute-start(bf16[4,2,3,128,128]{4,3,2,1,0:T(8,128)(2,1)} %collective-permute-done.refs_5_), channel_id=1, source_target_pairs={{12,4},{0,8},{20,12},{8,16},{28,20},{16,24},{36,28},{24,32},{44,36... | collective-permute-start | bytes 2359304 | tf_op jit(solution)/shard_map/ppermute | solution.py:21
  60.0 25.4 %collective-permute-start.9 = (bf16[384,768]{1,0:T(8,128)(2,1)}, bf16[384,768]{1,0:T(8,128)(2,1)}, u32[]{:S(2)}, u32[]{:S(2)}) collective-permute-start(bf16[384,768]{1,0:T(8,128)(2,1)} %collective-permute-done.8.mine_hbm), channel_id=1, source_target_pairs={{4,0},{0,4},{12,8},{8,12},{20,16},{16,20},{28,24},{24,28},{36,32},... | collective-permute-start | bytes 1769480 | tf_op jit(solution)/shard_map/ppermute | solution.py:21
  79.7 12.7 %all-to-all-start.2 = ((bf16[4,3,128,128]{3,2,1,0:T(8,128)(2,1)}), bf16[4,3,128,128]{3,2,1,0:T(8,128)(2,1)S(1)}, u32[]{:S(2)}, u32[]{:S(2)}) async-start(bf16[4,3,128,128]{3,2,1,0:T(8,128)(2,1)} %shard_map.86), calls=%async_computation.2 | async-start | bytes 786432 | tf_op jit(solution)/shard_map/all_to_all | solution.py:47

commit v6 on v5

--- a/solution.py
+++ b/solution.py
@@ -10,6 +10,7 @@
 
 HEAD_DIM = 128
 BLOCK = 128
+OWN = (0, 0)
 EXP2_SCALE = math.log2(math.e) / math.sqrt(HEAD_DIM)
 SMEM = pl.BlockSpec(memory_space=pltpu.SMEM)
 VMEM = pl.BlockSpec(memory_space=pltpu.VMEM)
@@ -63,32 +64,35 @@
     )(*args)
 
 
-def pack_kv_kernel(key_hbm, value_hbm, out_hbm, key_ref, value_ref, out_ref, sems):
-    groups, _, heads = out_ref.shape[:3]
+def pack_kv_kernel(key_hbm, value_hbm, out_hbm, value_ref, turned_ref, key_sems, sems):
+    groups, _, heads = out_hbm.shape[:3]
     width = heads * HEAD_DIM
     fetches = [
-        [
-            pltpu.make_async_copy(hbm.at[:, columns], ref.at[:, columns], sems.at[i, g])
-            for i, (hbm, ref) in enumerate(((key_hbm, key_ref), (value_hbm, value_ref)))
-        ]
+        pltpu.make_async_copy(value_hbm.at[:, columns], value_ref.at[:, columns], sems.at[0, g])
         for g, columns in ((g, pl.ds(g * width, width)) for g in range(groups))
     ]
+    keys = [
+        pltpu.make_async_copy(
+            key_hbm.at[:, pl.ds(i * HEAD_DIM, HEAD_DIM)],
+            out_hbm.at[i // heads, 0, i % heads],
+            key_sems.at[i],
+        )
+        for i in range(groups * heads)
+    ]
     sends = [
-        pltpu.make_async_copy(out_ref.at[g], out_hbm.at[g], sems.at[2, g]) for g in range(groups)
-    ]
-    for pair in fetches:
-        for fetch in pair:
-            fetch.start()
+        pltpu.make_async_copy(turned_ref.at[g], out_hbm.at[g, 1], sems.at[1, g])
+        for g in range(groups)
+    ]
+    for copy in fetches + keys:
+        copy.start()
     for g in range(groups):
-        for fetch in fetches[g]:
-            fetch.wait()
+        fetches[g].wait()
         for h in range(heads):
             at = slice((g * heads + h) * HEAD_DIM, (g * heads + h + 1) * HEAD_DIM)
-            out_ref[g, 0, h] = key_ref[:, at]
-            out_ref[g, 1, h] = jnp.transpose(value_ref[:, at])
+            turned_ref[g, h] = jnp.transpose(value_ref[:, at])
         sends[g].start()
-    for send in sends:
-        send.wait()
+    for copy in keys + sends:
+        copy.wait()
 
 
 def pack_kv(key_rows, value_rows, shape):
@@ -99,8 +103,12 @@
         in_specs=[hbm, hbm],
         out_specs=hbm,
         out_shape=jax.ShapeDtypeStruct(shape, jnp.bfloat16),
-        scratch_shapes=[pltpu.VMEM(a.shape, a.dtype) for a in args]
-        + [pltpu.VMEM(shape, jnp.bfloat16), pltpu.SemaphoreType.DMA((3, shape[0]))],
+        scratch_shapes=[
+            pltpu.VMEM(value_rows.shape, value_rows.dtype),
+            pltpu.VMEM((shape[0], *shape[2:]), jnp.bfloat16),
+            pltpu.SemaphoreType.DMA((shape[0] * shape[2],)),
+            pltpu.SemaphoreType.DMA((2, shape[0])),
+        ],
         name="pack_kv",
         compiler_params=pltpu.CompilerParams(vmem_limit_bytes=8 << 20),
     )(*args)
@@ -148,17 +156,19 @@
     def soften(h, scores):
         tiles, peak = [], None
         for i in range(count * groups):
-            tile = jnp.concatenate(
-                [
-                    jnp.where(
-                        keep[i // groups][i % groups][a],
-                        scores[i * BLOCK : (i + 1) * BLOCK, a * BLOCK : (a + 1) * BLOCK],
-                        -jnp.inf,
-                    )
-                    for a in range(groups)
-                ],
-                axis=1,
-            )
+            tile = scores[i * BLOCK : (i + 1) * BLOCK]
+            if slots[i // groups] != OWN:
+                tile = jnp.concatenate(
+                    [
+                        jnp.where(
+                            keep[i // groups][i % groups][a],
+                            tile[:, a * BLOCK : (a + 1) * BLOCK],
+                            -jnp.inf,
+                        )
+                        for a in range(groups)
+                    ],
+                    axis=1,
+                )
             top = jnp.max(tile.reshape(BLOCK // 8, 8, rows), axis=0)
             peak = top if peak is None else jnp.maximum(peak, top)
             tiles.append(tile)
@@ -316,7 +326,7 @@
     far = to_frame(near, partner)
     other = to_frame(mine, partner)
 
-    state = attend(((0, 0), (2, 1)), place, mask, queries, [own, swapped], None, False)
+    state = attend((OWN, (2, 1)), place, mask, queries, [own, swapped], None, False)
     slots, arrived = ((4, 3), (1, 2), (3, 4)), [first, swapped_first, second]
     state = attend(slots, place, mask, queries, arrived, state, False)
     state = attend(((6, 5),), place, mask, queries, [far_first], state, False)

time: 97.4 us -> 108 us (1.11)
  Pallas kernels: 19.8 us -> 30.8 us
    pallas_call x1, Pallas kernels: 2.19 us -> 13.2 us  [pack_kv(): pl.pallas_call(pack_kv_kernel, in_specs=[hbm, hbm], out_specs=hbm, out_sh...]
  transfers between devices with their start and end apart: 13 -> 13, of which waited for: 5 -> 5; matrix products, arithmetic and copies ran while one was open for 2% -> 1% of each run, Pallas kernels for 14% -> 12%
where the time goes in v6:
time: 108 us
  starting transfers between devices  49.7 us (46%)
  Pallas kernels  30.8 us (29%)
  waiting for transfers between devices  24.7 us (23%)
  local copies, waits for them, and re-layouts  1.53 us (1%)
    ppermute x8, starting transfers between devices, to_frame(): return lax.ppermute(x, 'ctx', pairs)  28.7 us
    all_to_all x3, waiting for transfers between devices, exchange(): return lax.all_to_all(pieces, 'head', 0, 0, tiled=True)  13.4 us
    pallas_call x6, Pallas kernels, call(): pl.pallas_call(kernel, in_specs=specs, out_specs=out_specs or jax.tree.ma...  13.4 us
    pallas_call x1, Pallas kernels, pack_kv(): pl.pallas_call(pack_kv_kernel, in_specs=[hbm, hbm], out_specs=hbm, out_sh...  13.2 us
    all_to_all x3, starting transfers between devices, exchange(): return lax.all_to_all(pieces, 'head', 0, 0, tiled=True)  12.9 us
    ppermute x8, waiting for transfers between devices, to_frame(): return lax.ppermute(x, 'ctx', pairs)  11.3 us
    ppermute x2, starting transfers between devices, beside(): return lax.ppermute(x, ('ctx', 'head'), pairs)  8 us
    pallas_call x1, Pallas kernels, project(): pl.pallas_call(project_kernel, in_specs=[SMEM] * len(scalars) + [VMEM] *...  4.21 us
  transfers between devices with their start and end apart: 13, of which 5 were waited for; matrix products, arithmetic and copies ran while one was open for 1% of the time, Pallas kernels for 12%

profile of v6, /device:TPU:248, one launch (start us, length us, event | category | flops | bytes accessed | tf_op | source)
XLA Modules:
  0.0 107.6 jit_solution(1468872053291968731)
XLA Ops:
  0.0 13.2 %pack_kv.1 = bf16[4,2,3,128,128]{4,3,2,1,0:T(8,128)(2,1)} custom-call(bf16[128,1536]{1,0:T(8,128)(2,1)} %key_hbm.1, bf16[128,1536]{1,0:T(8,128)(2,1)} %value_hbm.1), custom_call_target="tpu_custom_call" | custom-call | tf_op jit(solution)/shard_map/pack_kv/pallas_call | solution.py:101
  13.2 0.0 copy-start.2
  13.2 0.0 copy-start
  13.2 4.4 %all-to-all-start = ((bf16[4,2,3,128,128]{4,3,2,1,0:T(8,128)(2,1)}), bf16[4,2,3,128,128]{4,3,2,1,0:T(8,128)(2,1)S(1)}, u32[]{:S(2)}, u32[]{:S(2)}) async-start(bf16[4,2,3,128,128]{4,3,2,1,0:T(8,128)(2,1)} %pack_kv.1), calls=%async_computation | async-start | bytes 1572864 | tf_op jit(solution)/shard_map/all_to_all | solution.py:48
  17.7 5.1 %collective-permute-start.6 = (bf16[384,1536]{1,0:T(8,128)(2,1)S(1)}, bf16[384,1536]{1,0:T(8,128)(2,1)S(1)}, u32[]{:S(2)}, u32[]{:S(2)}) collective-permute-start(bf16[384,1536]{1,0:T(8,128)(2,1)S(1)} %copy-done.1), channel_id=1, source_target_pairs={{1,0},{2,1},{3,2},{0,3},{7,4},{4,5},{5,6},{6,7},{9,8},{10,9},{11,1... | collective-permute-start | bytes 3538952 | tf_op jit(solution)/shard_map/ppermute | solution.py:44
  22.8 0.7 copy.10
  23.5 0.8 reshape.3.refs_1_
  24.4 0.1 pad_add_fusion.refs_0_.place_ref
  24.4 0.8 shard_map.82
  25.3 6.2 %all-to-all-done.refs_3_ = bf16[4,2,3,128,128]{4,3,2,1,0:T(8,128)(2,1)S(1)} async-done(((bf16[4,2,3,128,128]{4,3,2,1,0:T(8,128)(2,1)}), bf16[4,2,3,128,128]{4,3,2,1,0:T(8,128)(2,1)S(1)}, u32[]{:S(2)}, u32[]{:S(2)}) %all-to-all-start) | async-done | bytes 786464 | tf_op jit(solution)/shard_map/all_to_all | solution.py:48
  31.4 3.5 %all-to-all-start.1 = ((bf16[4,3,128,128]{3,2,1,0:T(8,128)(2,1)}), bf16[4,3,128,128]{3,2,1,0:T(8,128)(2,1)S(1)}, u32[]{:S(2)}, u32[]{:S(2)}) async-start(bf16[4,3,128,128]{3,2,1,0:T(8,128)(2,1)} %shard_map.82), calls=%async_computation.1 | async-start | bytes 786432 | tf_op jit(solution)/shard_map/all_to_all | solution.py:48
  34.9 3.3 %collective-permute-start.2 = (bf16[4,2,3,128,128]{4,3,2,1,0:T(8,128)(2,1)S(1)}, bf16[4,2,3,128,128]{4,3,2,1,0:T(8,128)(2,1)}, u32[]{:S(2)}, u32[]{:S(2)}) collective-permute-start(bf16[4,2,3,128,128]{4,3,2,1,0:T(8,128)(2,1)S(1)} %all-to-all-done.refs_3_), channel_id=1, source_target_pairs={{8,0},{16,8},{4,12},{24,16},{12,20},{32,24},{20,28},{40,32},{28,36... | collective-permute-start | bytes 2359304 | tf_op jit(solution)/shard_map/ppermute | solution.py:22
  38.1 5.9 %collective-permute-start = (bf16[4,2,3,128,128]{4,3,2,1,0:T(8,128)(2,1)S(1)}, bf16[4,2,3,128,128]{4,3,2,1,0:T(8,128)(2,1)}, u32[]{:S(2)}, u32[]{:S(2)}) collective-permute-start(bf16[4,2,3,128,128]{4,3,2,1,0:T(8,128)(2,1)S(1)} %all-to-all-done.refs_3_), channel_id=1, source_target_pairs={{12,4},{0,8},{20,12},{8,16},{28,20},{16,24},{36,28},{24,32},{44,36... | collective-permute-start | bytes 2359304 | tf_op jit(solution)/shard_map/ppermute | solution.py:22
  44.1 0.3 all-to-all-done.1.refs_2_
  44.3 4.6 %collective-permute-start.5 = (bf16[4,2,3,128,128]{4,3,2,1,0:T(8,128)(2,1)S(1)}, bf16[4,2,3,128,128]{4,3,2,1,0:T(8,128)(2,1)S(1)}, u32[]{:S(2)}, u32[]{:S(2)}) collective-permute-start(bf16[4,2,3,128,128]{4,3,2,1,0:T(8,128)(2,1)S(1)} %all-to-all-done.refs_3_), channel_id=1, source_target_pairs={{4,0},{0,4},{12,8},{8,12},{20,16},{16,20},{28,24},{24,28},{36,32},... | collective-permute-start | bytes 2359304 | tf_op jit(solution)/shard_map/ppermute | solution.py:22
  49.0 0.6 shard_map.87
  49.6 2.9 %collective-permute-start.8 = (bf16[384,768]{1,0:T(8,128)(2,1)S(1)}, bf16[384,768]{1,0:T(8,128)(2,1)}, u32[]{:S(2)}, u32[]{:S(2)}) collective-permute-start(bf16[384,768]{1,0:T(8,128)(2,1)S(1)} %shard_map.87), channel_id=1, source_target_pairs={{1,0},{2,1},{3,2},{0,3},{7,4},{4,5},{5,6},{6,7},{9,8},{10,9},{11,1... | collective-permute-start | bytes 1769480 | tf_op jit(solution)/shard_map/ppermute | solution.py:44
  52.5 1.9 %collective-permute-start.7 = (bf16[384,1536]{1,0:T(8,128)(2,1)S(1)}, bf16[384,1536]{1,0:T(8,128)(2,1)S(1)}, u32[]{:S(2)}, u32[]{:S(2)}) collective-permute-start(bf16[384,1536]{1,0:T(8,128)(2,1)S(1)} %collective-permute-done.6.weight_ref.near_ref), channel_id=1, source_target_pairs={{4,0},{0,4},{12,8},{8,12},{20,16},{16,20},{28,24},{24,28},{36,32},... | collective-permute-start | bytes 3538952 | tf_op jit(solution)/shard_map/ppermute | solution.py:22
  54.4 5.5 %collective-permute-done.2.refs_3_ = bf16[4,2,3,128,128]{4,3,2,1,0:T(8,128)(2,1)} collective-permute-done((bf16[4,2,3,128,128]{4,3,2,1,0:T(8,128)(2,1)S(1)}, bf16[4,2,3,128,128]{4,3,2,1,0:T(8,128)(2,1)}, u32[]{:S(2)}, u32[]{:S(2)}) %collective-permute-start.2) | collective-permute-done | bytes 786464 | tf_op jit(solution)/shard_map/ppermute | solution.py:22
  59.9 1.9 %collective-permute-start.4 = (bf16[4,2,3,128,128]{4,3,2,1,0:T(8,128)(2,1)}, bf16[4,2,3,128,128]{4,3,2,1,0:T(8,128)(2,1)S(1)}, u32[]{:S(2)}, u32[]{:S(2)}) collective-permute-start(bf16[4,2,3,128,128]{4,3,2,1,0:T(8,128)(2,1)} %collective-permute-done.2.refs_3_), channel_id=1, source_target_pairs={{4,0},{0,4},{12,8},{8,12},{20,16},{16,20},{28,24},{24,28},{36,32},... | collective-permute-start | bytes 2359304 | tf_op jit(solution)/shard_map/ppermute | solution.py:22
  61.8 0.0 collective-permute-done.refs_5_
  61.8 1.9 %collective-permute-start.3 = (bf16[4,2,3,128,128]{4,3,2,1,0:T(8,128)(2,1)}, bf16[4,2,3,128,128]{4,3,2,1,0:T(8,128)(2,1)S(1)}, u32[]{:S(2)}, u32[]{:S(2)}) collective-permute-start(bf16[4,2,3,128,128]{4,3,2,1,0:T(8,128)(2,1)} %collective-permute-done.2.refs_3_), channel_id=1, source_target_pairs={{8,0},{16,8},{4,12},{24,16},{12,20},{32,24},{20,28},{40,32},{28,36... | collective-permute-start | bytes 2359304 | tf_op jit(solution)/shard_map/ppermute | solution.py:22
  63.7 7.2 %collective-permute-start.1 = (bf16[4,2,3,128,128]{4,3,2,1,0:T(8,128)(2,1)}, bf16[4,2,3,128,128]{4,3,2,1,0:T(8,128)(2,1)S(1)}, u32[]{:S(2)}, u32[]{:S(2)}) collective-permute-start(bf16[4,2,3,128,128]{4,3,2,1,0:T(8,128)(2,1)} %collective-permute-done.refs_5_), channel_id=1, source_target_pairs={{12,4},{0,8},{20,12},{8,16},{28,20},{16,24},{36,28},{24,32},{44,36... | collective-permute-start | bytes 2359304 | tf_op jit(solution)/shard_map/ppermute | solution.py:22
  71.0 1.9 %collective-permute-start.9 = (bf16[384,768]{1,0:T(8,128)(2,1)}, bf16[384,768]{1,0:T(8,128)(2,1)}, u32[]{:S(2)}, u32[]{:S(2)}) collective-permute-start(bf16[384,768]{1,0:T(8,128)(2,1)} %collective-permute-done.8.mine_hbm), channel_id=1, source_target_pairs={{4,0},{0,4},{12,8},{8,12},{20,16},{16,20},{28,24},{24,28},{36,32},... | collective-permute-start | bytes 1769480 | tf_op jit(solution)/shard_map/ppermute | solution.py:22
  72.9 2.8 %shard_map.83 = (f32[3,8,512]{2,1,0:T(8,128)S(1)}, f32[3,8,512]{2,1,0:T(8,128)S(1)}, f32[3,128,512]{2,1,0:T(8,128)S(1)}) custom-call(s32[2]{0:T(128)S(1)} %pad_add_fusion.refs_0_.place_ref, s32[112]{0:T(128)S(1)} %reshape.3.refs_1_, bf16[4,3,128,128]{3,2,1,0:T(8,128)(2,1)S(1)} %all-to-all-done.1.refs_2_, ...), custom_call_target="tpu_custom_call" | custom-call | tf_op jit(solution)/shard_map/pallas_call | solution.py:57
  75.7 4.7 %shard_map.84 = (f32[3,8,512]{2,1,0:T(8,128)S(1)}, f32[3,8,512]{2,1,0:T(8,128)S(1)}, f32[3,128,512]{2,1,0:T(8,128)S(1)}) custom-call(s32[2]{0:T(128)S(1)} %pad_add_fusion.refs_0_.place_ref, s32[112]{0:T(128)S(1)} %reshape.3.refs_1_, bf16[4,3,128,128]{3,2,1,0:T(8,128)(2,1)S(1)} %all-to-all-done.1.refs_2_, ...), custom_call_target="tpu_custom_call" | custom-call | tf_op jit(solution)/shard_map/pallas_call | solution.py:57
  80.4 5.8 %collective-permute-done.3.refs_3_ = bf16[4,2,3,128,128]{4,3,2,1,0:T(8,128)(2,1)S(1)} collective-permute-done((bf16[4,2,3,128,128]{4,3,2,1,0:T(8,128)(2,1)}, bf16[4,2,3,128,128]{4,3,2,1,0:T(8,128)(2,1)S(1)}, u32[]{:S(2)}, u32[]{:S(2)}) %collective-permute-start.3) | collective-permute-done | bytes 786464 | tf_op jit(solution)/shard_map/ppermute | solution.py:22
  86.2 1.9 %shard_map.85 = (f32[3,8,512]{2,1,0:T(8,128)S(1)}, f32[3,8,512]{2,1,0:T(8,128)S(1)}, f32[3,128,512]{2,1,0:T(8,128)S(1)}) custom-call(s32[2]{0:T(128)S(1)} %pad_add_fusion.refs_0_.place_ref, s32[112]{0:T(128)S(1)} %reshape.3.refs_1_, bf16[4,3,128,128]{3,2,1,0:T(8,128)(2,1)S(1)} %all-to-all-done.1.refs_2_, ...), custom_call_target="tpu_custom_call" | custom-call | tf_op jit(solution)/shard_map/pallas_call | solution.py:57
  88.1 2.7 %shard_map.86 = bf16[4,3,128,128]{3,2,1,0:T(8,128)(2,1)} custom-call(s32[2]{0:T(128)S(1)} %pad_add_fusion.refs_0_.place_ref, s32[112]{0:T(128)S(1)} %reshape.3.refs_1_, bf16[4,3,128,128]{3,2,1,0:T(8,128)(2,1)S(1)} %all-to-all-done.1.refs_2_, bf16[4,2,3,128,128]{4,3,2,1,0:T(8,128)(2,1)S(1)} %collective-permute-done.1.refs_3_, ...), custom_call_target="tpu_custom_call" | custom-call | tf_op jit(solution)/shard_map/pallas_call | solution.py:57
  90.7 5.0 %all-to-all-start.2 = ((bf16[4,3,128,128]{3,2,1,0:T(8,128)(2,1)}), bf16[4,3,128,128]{3,2,1,0:T(8,128)(2,1)S(1)}, u32[]{:S(2)}, u32[]{:S(2)}) async-start(bf16[4,3,128,128]{3,2,1,0:T(8,128)(2,1)} %shard_map.86), calls=%async_computation.2 | async-start | bytes 786432 | tf_op jit(solution)/shard_map/all_to_all | solution.py:48
  96.5 7.0 %all-to-all-done.2.o_ref = bf16[4,3,128,128]{3,2,1,0:T(8,128)(2,1)S(1)} async-done(((bf16[4,3,128,128]{3,2,1,0:T(8,128)(2,1)}), bf16[4,3,128,128]{3,2,1,0:T(8,128)(2,1)S(1)}, u32[]{:S(2)}, u32[]{:S(2)}) %all-to-all-start.2) | async-done | bytes 393248 | tf_op jit(solution)/shard_map/all_to_all | solution.py:48
  103.4 4.2 %project.1 = bf16[128,1536]{1,0:T(8,128)(2,1)} custom-call(s32[2]{0:T(128)S(1)} %pad_add_fusion.refs_0_.place_ref, s32[1]{0:T(128)S(6)} %copy.11.level_ref, bf16[4,3,128,128]{3,2,1,0:T(8,128)(2,1)S(1)} %all-to-all-done.2.o_ref, bf16[384,1536]{1,0:T(8,128)(2,1)S(1)} %collective-permute-done.6.weight_ref.near_ref, ...), custom_call_target="tpu_custom_call" | custom-call | tf_op jit(solution)/shard_map/project/pallas_call | solution.py:282
  (11 shorter events, 0.0 us)
Async XLA Ops:
  0.0 17.7 %copy-start.1 = (bf16[384,1536]{1,0:T(8,128)(2,1)S(1)}, bf16[384,1536]{1,0:T(8,128)(2,1)}, u32[]{:S(2)}) copy-start(bf16[384,1536]{1,0:T(8,128)(2,1)} %own_hbm.1) | copy-start | bytes 3538948
  13.2 9.6 %copy-start.2 = (s32[1,7,4,4]{1,3,2,0:T(4,128)S(1)}, s32[1,7,4,4]{1,3,2,0:T(4,128)}, u32[]{:S(2)}) copy-start(s32[1,7,4,4]{1,3,2,0:T(4,128)} %param.14) | copy-start | bytes 1348
  13.2 11.2 %copy-start = (bf16[128,1536]{1,0:T(8,128)(2,1)S(1)}, bf16[128,1536]{1,0:T(8,128)(2,1)}, u32[]{:S(2)}) copy-start(bf16[128,1536]{1,0:T(8,128)(2,1)} %query_ref) | copy-start | bytes 1179652
  13.2 18.2 %all-to-all-start = ((bf16[4,2,3,128,128]{4,3,2,1,0:T(8,128)(2,1)}), bf16[4,2,3,128,128]{4,3,2,1,0:T(8,128)(2,1)S(1)}, u32[]{:S(2)}, u32[]{:S(2)}) async-start(bf16[4,2,3,128,128]{4,3,2,1,0:T(8,128)(2,1)} %pack_kv.1), calls=%async_computation | async-start | bytes 1572864 | tf_op jit(solution)/shard_map/all_to_all | solution.py:48
  17.7 31.3 %collective-permute-start.6 = (bf16[384,1536]{1,0:T(8,128)(2,1)S(1)}, bf16[384,1536]{1,0:T(8,128)(2,1)S(1)}, u32[]{:S(2)}, u32[]{:S(2)}) collective-permute-start(bf16[384,1536]{1,0:T(8,128)(2,1)S(1)} %copy-done.1), channel_id=1, source_target_pairs={{1,0},{2,1},{3,2},{0,3},{7,4},{4,5},{5,6},{6,7},{9,8},{10,9},{11,1... | collective-permute-start | bytes 3538952 | tf_op jit(solution)/shard_map/ppermute | solution.py:44
  31.4 12.9 %all-to-all-start.1 = ((bf16[4,3,128,128]{3,2,1,0:T(8,128)(2,1)}), bf16[4,3,128,128]{3,2,1,0:T(8,128)(2,1)S(1)}, u32[]{:S(2)}, u32[]{:S(2)}) async-start(bf16[4,3,128,128]{3,2,1,0:T(8,128)(2,1)} %shard_map.82), calls=%async_computation.1 | async-start | bytes 786432 | tf_op jit(solution)/shard_map/all_to_all | solution.py:48
  34.9 25.0 %collective-permute-start.2 = (bf16[4,2,3,128,128]{4,3,2,1,0:T(8,128)(2,1)S(1)}, bf16[4,2,3,128,128]{4,3,2,1,0:T(8,128)(2,1)}, u32[]{:S(2)}, u32[]{:S(2)}) collective-permute-start(bf16[4,2,3,128,128]{4,3,2,1,0:T(8,128)(2,1)S(1)} %all-to-all-done.refs_3_), channel_id=1, source_target_pairs={{8,0},{16,8},{4,12},{24,16},{12,20},{32,24},{20,28},{40,32},{28,36... | collective-permute-start | bytes 2359304 | tf_op jit(solution)/shard_map/ppermute | solution.py:22
  38.1 23.6 %collective-permute-start = (bf16[4,2,3,128,128]{4,3,2,1,0:T(8,128)(2,1)S(1)}, bf16[4,2,3,128,128]{4,3,2,1,0:T(8,128)(2,1)}, u32[]{:S(2)}, u32[]{:S(2)}) collective-permute-start(bf16[4,2,3,128,128]{4,3,2,1,0:T(8,128)(2,1)S(1)} %all-to-all-done.refs_3_), channel_id=1, source_target_pairs={{12,4},{0,8},{20,12},{8,16},{28,20},{16,24},{36,28},{24,32},{44,36... | collective-permute-start | bytes 2359304 | tf_op jit(solution)/shard_map/ppermute | solution.py:22
  44.3 19.4 %collective-permute-start.5 = (bf16[4,2,3,128,128]{4,3,2,1,0:T(8,128)(2,1)S(1)}, bf16[4,2,3,128,128]{4,3,2,1,0:T(8,128)(2,1)S(1)}, u32[]{:S(2)}, u32[]{:S(2)}) collective-permute-start(bf16[4,2,3,128,128]{4,3,2,1,0:T(8,128)(2,1)S(1)} %all-to-all-done.refs_3_), channel_id=1, source_target_pairs={{4,0},{0,4},{12,8},{8,12},{20,16},{16,20},{28,24},{24,28},{36,32},... | collective-permute-start | bytes 2359304 | tf_op jit(solution)/shard_map/ppermute | solution.py:22
  49.6 21.4 %collective-permute-start.8 = (bf16[384,768]{1,0:T(8,128)(2,1)S(1)}, bf16[384,768]{1,0:T(8,128)(2,1)}, u32[]{:S(2)}, u32[]{:S(2)}) collective-permute-start(bf16[384,768]{1,0:T(8,128)(2,1)S(1)} %shard_map.87), channel_id=1, source_target_pairs={{1,0},{2,1},{3,2},{0,3},{7,4},{4,5},{5,6},{6,7},{9,8},{10,9},{11,1... | collective-permute-start | bytes 1769480 | tf_op jit(solution)/shard_map/ppermute | solution.py:44
  52.5 44.0 %collective-permute-start.7 = (bf16[384,1536]{1,0:T(8,128)(2,1)S(1)}, bf16[384,1536]{1,0:T(8,128)(2,1)S(1)}, u32[]{:S(2)}, u32[]{:S(2)}) collective-permute-start(bf16[384,1536]{1,0:T(8,128)(2,1)S(1)} %collective-permute-done.6.weight_ref.near_ref), channel_id=1, source_target_pairs={{4,0},{0,4},{12,8},{8,12},{20,16},{16,20},{28,24},{24,28},{36,32},... | collective-permute-start | bytes 3538952 | tf_op jit(solution)/shard_map/ppermute | solution.py:22
  59.9 15.8 %collective-permute-start.4 = (bf16[4,2,3,128,128]{4,3,2,1,0:T(8,128)(2,1)}, bf16[4,2,3,128,128]{4,3,2,1,0:T(8,128)(2,1)S(1)}, u32[]{:S(2)}, u32[]{:S(2)}) collective-permute-start(bf16[4,2,3,128,128]{4,3,2,1,0:T(8,128)(2,1)} %collective-permute-done.2.refs_3_), channel_id=1, source_target_pairs={{4,0},{0,4},{12,8},{8,12},{20,16},{16,20},{28,24},{24,28},{36,32},... | collective-permute-start | bytes 2359304 | tf_op jit(solution)/shard_map/ppermute | solution.py:22
  61.8 24.4 %collective-permute-start.3 = (bf16[4,2,3,128,128]{4,3,2,1,0:T(8,128)(2,1)}, bf16[4,2,3,128,128]{4,3,2,1,0:T(8,128)(2,1)S(1)}, u32[]{:S(2)}, u32[]{:S(2)}) collective-permute-start(bf16[4,2,3,128,128]{4,3,2,1,0:T(8,128)(2,1)} %collective-permute-done.2.refs_3_), channel_id=1, source_target_pairs={{8,0},{16,8},{4,12},{24,16},{12,20},{32,24},{20,28},{40,32},{28,36... | collective-permute-start | bytes 2359304 | tf_op jit(solution)/shard_map/ppermute | solution.py:22
  63.7 24.3 %collective-permute-start.1 = (bf16[4,2,3,128,128]{4,3,2,1,0:T(8,128)(2,1)}, bf16[4,2,3,128,128]{4,3,2,1,0:T(8,128)(2,1)S(1)}, u32[]{:S(2)}, u32[]{:S(2)}) collective-permute-start(bf16[4,2,3,128,128]{4,3,2,1,0:T(8,128)(2,1)} %collective-permute-done.refs_5_), channel_id=1, source_target_pairs={{12,4},{0,8},{20,12},{8,16},{28,20},{16,24},{36,28},{24,32},{44,36... | collective-permute-start | bytes 2359304 | tf_op jit(solution)/shard_map/ppermute | solution.py:22
  71.0 25.4 %collective-permute-start.9 = (bf16[384,768]{1,0:T(8,128)(2,1)}, bf16[384,768]{1,0:T(8,128)(2,1)}, u32[]{:S(2)}, u32[]{:S(2)}) collective-permute-start(bf16[384,768]{1,0:T(8,128)(2,1)} %collective-permute-done.8.mine_hbm), channel_id=1, source_target_pairs={{4,0},{0,4},{12,8},{8,12},{20,16},{16,20},{28,24},{24,28},{36,32},... | collective-permute-start | bytes 1769480 | tf_op jit(solution)/shard_map/ppermute | solution.py:22
  90.7 12.7 %all-to-all-start.2 = ((bf16[4,3,128,128]{3,2,1,0:T(8,128)(2,1)}), bf16[4,3,128,128]{3,2,1,0:T(8,128)(2,1)S(1)}, u32[]{:S(2)}, u32[]{:S(2)}) async-start(bf16[4,3,128,128]{3,2,1,0:T(8,128)(2,1)} %shard_map.86), calls=%async_computation.2 | async-start | bytes 786432 | tf_op jit(solution)/shard_map/all_to_all | solution.py:48

commit v7 on v5

--- a/solution.py
+++ b/solution.py
@@ -10,6 +10,7 @@
 
 HEAD_DIM = 128
 BLOCK = 128
+OWN = (0, 0)
 EXP2_SCALE = math.log2(math.e) / math.sqrt(HEAD_DIM)
 SMEM = pl.BlockSpec(memory_space=pltpu.SMEM)
 VMEM = pl.BlockSpec(memory_space=pltpu.VMEM)
@@ -148,17 +149,19 @@
     def soften(h, scores):
         tiles, peak = [], None
         for i in range(count * groups):
-            tile = jnp.concatenate(
-                [
-                    jnp.where(
-                        keep[i // groups][i % groups][a],
-                        scores[i * BLOCK : (i + 1) * BLOCK, a * BLOCK : (a + 1) * BLOCK],
-                        -jnp.inf,
-                    )
-                    for a in range(groups)
-                ],
-                axis=1,
-            )
+            tile = scores[i * BLOCK : (i + 1) * BLOCK]
+            if slots[i // groups] != OWN:
+                tile = jnp.concatenate(
+                    [
+                        jnp.where(
+                            keep[i // groups][i % groups][a],
+                            tile[:, a * BLOCK : (a + 1) * BLOCK],
+                            -jnp.inf,
+                        )
+                        for a in range(groups)
+                    ],
+                    axis=1,
+                )
             top = jnp.max(tile.reshape(BLOCK // 8, 8, rows), axis=0)
             peak = top if peak is None else jnp.maximum(peak, top)
             tiles.append(tile)
@@ -316,7 +319,7 @@
     far = to_frame(near, partner)
     other = to_frame(mine, partner)
 
-    state = attend(((0, 0), (2, 1)), place, mask, queries, [own, swapped], None, False)
+    state = attend((OWN, (2, 1)), place, mask, queries, [own, swapped], None, False)
     slots, arrived = ((4, 3), (1, 2), (3, 4)), [first, swapped_first, second]
     state = attend(slots, place, mask, queries, arrived, state, False)
     state = attend(((6, 5),), place, mask, queries, [far_first], state, False)

time: 97.4 us -> 97.4 us (level)
  no operation moved by 1% of the time
where the time goes in v7:
time: 97.4 us; the launch traced here: 96.6 us
  starting transfers between devices  49.7 us (51%)
  waiting for transfers between devices  24.7 us (25%)
  Pallas kernels  19.8 us (20%)
  local copies, waits for them, and re-layouts  1.53 us (2%)
    ppermute x8, starting transfers between devices, to_frame(): return lax.ppermute(x, 'ctx', pairs)  28.7 us
    all_to_all x3, waiting for transfers between devices, exchange(): return lax.all_to_all(pieces, 'head', 0, 0, tiled=True)  13.4 us
    pallas_call x6, Pallas kernels, call(): pl.pallas_call(kernel, in_specs=specs, out_specs=out_specs or jax.tree.ma...  13.4 us
    all_to_all x3, starting transfers between devices, exchange(): return lax.all_to_all(pieces, 'head', 0, 0, tiled=True)  12.9 us
    ppermute x8, waiting for transfers between devices, to_frame(): return lax.ppermute(x, 'ctx', pairs)  11.3 us
    ppermute x2, starting transfers between devices, beside(): return lax.ppermute(x, ('ctx', 'head'), pairs)  8 us
    pallas_call x1, Pallas kernels, project(): pl.pallas_call(project_kernel, in_specs=[SMEM] * len(scalars) + [VMEM] *...  4.21 us
    pallas_call x1, Pallas kernels, pack_kv(): pl.pallas_call(pack_kv_kernel, in_specs=[hbm, hbm], out_specs=hbm, out_sh...  2.19 us
  transfers between devices with their start and end apart: 13, of which 5 were waited for; matrix products, arithmetic and copies ran while one was open for 2% of the time, Pallas kernels for 14%

profile of v7, /device:TPU:248, one launch (start us, length us, event | category | flops | bytes accessed | tf_op | source)
XLA Modules:
  0.0 96.6 jit_solution(7322324151730716304)
XLA Ops:
  0.0 2.2 %pack_kv.1 = bf16[4,2,3,128,128]{4,3,2,1,0:T(8,128)(2,1)} custom-call(bf16[128,1536]{1,0:T(8,128)(2,1)} %key_hbm.1, bf16[128,1536]{1,0:T(8,128)(2,1)} %value_hbm.1), custom_call_target="tpu_custom_call" | custom-call | tf_op jit(solution)/shard_map/pack_kv/pallas_call | solution.py:98
  2.2 0.0 copy-start.2
  2.2 0.0 copy-start
  2.2 4.4 %all-to-all-start = ((bf16[4,2,3,128,128]{4,3,2,1,0:T(8,128)(2,1)}), bf16[4,2,3,128,128]{4,3,2,1,0:T(8,128)(2,1)S(1)}, u32[]{:S(2)}, u32[]{:S(2)}) async-start(bf16[4,2,3,128,128]{4,3,2,1,0:T(8,128)(2,1)} %pack_kv.1), calls=%async_computation | async-start | bytes 1572864 | tf_op jit(solution)/shard_map/all_to_all | solution.py:48
  6.7 5.1 %collective-permute-start.6 = (bf16[384,1536]{1,0:T(8,128)(2,1)S(1)}, bf16[384,1536]{1,0:T(8,128)(2,1)S(1)}, u32[]{:S(2)}, u32[]{:S(2)}) collective-permute-start(bf16[384,1536]{1,0:T(8,128)(2,1)S(1)} %copy-done.1), channel_id=1, source_target_pairs={{1,0},{2,1},{3,2},{0,3},{7,4},{4,5},{5,6},{6,7},{9,8},{10,9},{11,1... | collective-permute-start | bytes 3538952 | tf_op jit(solution)/shard_map/ppermute | solution.py:44
  11.8 0.7 copy.10
  12.5 0.8 reshape.3.refs_1_
  13.4 0.1 pad_add_fusion.refs_0_.place_ref
  13.4 0.8 shard_map.82
  14.2 6.2 %all-to-all-done.refs_3_ = bf16[4,2,3,128,128]{4,3,2,1,0:T(8,128)(2,1)S(1)} async-done(((bf16[4,2,3,128,128]{4,3,2,1,0:T(8,128)(2,1)}), bf16[4,2,3,128,128]{4,3,2,1,0:T(8,128)(2,1)S(1)}, u32[]{:S(2)}, u32[]{:S(2)}) %all-to-all-start) | async-done | bytes 786464 | tf_op jit(solution)/shard_map/all_to_all | solution.py:48
  20.4 3.5 %all-to-all-start.1 = ((bf16[4,3,128,128]{3,2,1,0:T(8,128)(2,1)}), bf16[4,3,128,128]{3,2,1,0:T(8,128)(2,1)S(1)}, u32[]{:S(2)}, u32[]{:S(2)}) async-start(bf16[4,3,128,128]{3,2,1,0:T(8,128)(2,1)} %shard_map.82), calls=%async_computation.1 | async-start | bytes 786432 | tf_op jit(solution)/shard_map/all_to_all | solution.py:48
  23.9 3.3 %collective-permute-start.2 = (bf16[4,2,3,128,128]{4,3,2,1,0:T(8,128)(2,1)S(1)}, bf16[4,2,3,128,128]{4,3,2,1,0:T(8,128)(2,1)}, u32[]{:S(2)}, u32[]{:S(2)}) collective-permute-start(bf16[4,2,3,128,128]{4,3,2,1,0:T(8,128)(2,1)S(1)} %all-to-all-done.refs_3_), channel_id=1, source_target_pairs={{8,0},{16,8},{4,12},{24,16},{12,20},{32,24},{20,28},{40,32},{28,36... | collective-permute-start | bytes 2359304 | tf_op jit(solution)/shard_map/ppermute | solution.py:22
  27.1 5.9 %collective-permute-start = (bf16[4,2,3,128,128]{4,3,2,1,0:T(8,128)(2,1)S(1)}, bf16[4,2,3,128,128]{4,3,2,1,0:T(8,128)(2,1)}, u32[]{:S(2)}, u32[]{:S(2)}) collective-permute-start(bf16[4,2,3,128,128]{4,3,2,1,0:T(8,128)(2,1)S(1)} %all-to-all-done.refs_3_), channel_id=1, source_target_pairs={{12,4},{0,8},{20,12},{8,16},{28,20},{16,24},{36,28},{24,32},{44,36... | collective-permute-start | bytes 2359304 | tf_op jit(solution)/shard_map/ppermute | solution.py:22
  33.1 0.3 all-to-all-done.1.refs_2_
  33.3 4.6 %collective-permute-start.5 = (bf16[4,2,3,128,128]{4,3,2,1,0:T(8,128)(2,1)S(1)}, bf16[4,2,3,128,128]{4,3,2,1,0:T(8,128)(2,1)S(1)}, u32[]{:S(2)}, u32[]{:S(2)}) collective-permute-start(bf16[4,2,3,128,128]{4,3,2,1,0:T(8,128)(2,1)S(1)} %all-to-all-done.refs_3_), channel_id=1, source_target_pairs={{4,0},{0,4},{12,8},{8,12},{20,16},{16,20},{28,24},{24,28},{36,32},... | collective-permute-start | bytes 2359304 | tf_op jit(solution)/shard_map/ppermute | solution.py:22
  38.0 0.6 shard_map.87
  38.6 2.9 %collective-permute-start.8 = (bf16[384,768]{1,0:T(8,128)(2,1)S(1)}, bf16[384,768]{1,0:T(8,128)(2,1)}, u32[]{:S(2)}, u32[]{:S(2)}) collective-permute-start(bf16[384,768]{1,0:T(8,128)(2,1)S(1)} %shard_map.87), channel_id=1, source_target_pairs={{1,0},{2,1},{3,2},{0,3},{7,4},{4,5},{5,6},{6,7},{9,8},{10,9},{11,1... | collective-permute-start | bytes 1769480 | tf_op jit(solution)/shard_map/ppermute | solution.py:44
  41.5 1.9 %collective-permute-start.7 = (bf16[384,1536]{1,0:T(8,128)(2,1)S(1)}, bf16[384,1536]{1,0:T(8,128)(2,1)S(1)}, u32[]{:S(2)}, u32[]{:S(2)}) collective-permute-start(bf16[384,1536]{1,0:T(8,128)(2,1)S(1)} %collective-permute-done.6.weight_ref.near_ref), channel_id=1, source_target_pairs={{4,0},{0,4},{12,8},{8,12},{20,16},{16,20},{28,24},{24,28},{36,32},... | collective-permute-start | bytes 3538952 | tf_op jit(solution)/shard_map/ppermute | solution.py:22
  43.4 5.5 %collective-permute-done.2.refs_3_ = bf16[4,2,3,128,128]{4,3,2,1,0:T(8,128)(2,1)} collective-permute-done((bf16[4,2,3,128,128]{4,3,2,1,0:T(8,128)(2,1)S(1)}, bf16[4,2,3,128,128]{4,3,2,1,0:T(8,128)(2,1)}, u32[]{:S(2)}, u32[]{:S(2)}) %collective-permute-start.2) | collective-permute-done | bytes 786464 | tf_op jit(solution)/shard_map/ppermute | solution.py:22
  48.9 1.9 %collective-permute-start.4 = (bf16[4,2,3,128,128]{4,3,2,1,0:T(8,128)(2,1)}, bf16[4,2,3,128,128]{4,3,2,1,0:T(8,128)(2,1)S(1)}, u32[]{:S(2)}, u32[]{:S(2)}) collective-permute-start(bf16[4,2,3,128,128]{4,3,2,1,0:T(8,128)(2,1)} %collective-permute-done.2.refs_3_), channel_id=1, source_target_pairs={{4,0},{0,4},{12,8},{8,12},{20,16},{16,20},{28,24},{24,28},{36,32},... | collective-permute-start | bytes 2359304 | tf_op jit(solution)/shard_map/ppermute | solution.py:22
  50.8 0.0 collective-permute-done.refs_5_
  50.8 1.9 %collective-permute-start.3 = (bf16[4,2,3,128,128]{4,3,2,1,0:T(8,128)(2,1)}, bf16[4,2,3,128,128]{4,3,2,1,0:T(8,128)(2,1)S(1)}, u32[]{:S(2)}, u32[]{:S(2)}) collective-permute-start(bf16[4,2,3,128,128]{4,3,2,1,0:T(8,128)(2,1)} %collective-permute-done.2.refs_3_), channel_id=1, source_target_pairs={{8,0},{16,8},{4,12},{24,16},{12,20},{32,24},{20,28},{40,32},{28,36... | collective-permute-start | bytes 2359304 | tf_op jit(solution)/shard_map/ppermute | solution.py:22
  52.7 7.2 %collective-permute-start.1 = (bf16[4,2,3,128,128]{4,3,2,1,0:T(8,128)(2,1)}, bf16[4,2,3,128,128]{4,3,2,1,0:T(8,128)(2,1)S(1)}, u32[]{:S(2)}, u32[]{:S(2)}) collective-permute-start(bf16[4,2,3,128,128]{4,3,2,1,0:T(8,128)(2,1)} %collective-permute-done.refs_5_), channel_id=1, source_target_pairs={{12,4},{0,8},{20,12},{8,16},{28,20},{16,24},{36,28},{24,32},{44,36... | collective-permute-start | bytes 2359304 | tf_op jit(solution)/shard_map/ppermute | solution.py:22
  60.0 1.9 %collective-permute-start.9 = (bf16[384,768]{1,0:T(8,128)(2,1)}, bf16[384,768]{1,0:T(8,128)(2,1)}, u32[]{:S(2)}, u32[]{:S(2)}) collective-permute-start(bf16[384,768]{1,0:T(8,128)(2,1)} %collective-permute-done.8.mine_hbm), channel_id=1, source_target_pairs={{4,0},{0,4},{12,8},{8,12},{20,16},{16,20},{28,24},{24,28},{36,32},... | collective-permute-start | bytes 1769480 | tf_op jit(solution)/shard_map/ppermute | solution.py:22
  61.9 2.8 %shard_map.83 = (f32[3,8,512]{2,1,0:T(8,128)S(1)}, f32[3,8,512]{2,1,0:T(8,128)S(1)}, f32[3,128,512]{2,1,0:T(8,128)S(1)}) custom-call(s32[2]{0:T(128)S(1)} %pad_add_fusion.refs_0_.place_ref, s32[112]{0:T(128)S(1)} %reshape.3.refs_1_, bf16[4,3,128,128]{3,2,1,0:T(8,128)(2,1)S(1)} %all-to-all-done.1.refs_2_, ...), custom_call_target="tpu_custom_call" | custom-call | tf_op jit(solution)/shard_map/pallas_call | solution.py:57
  64.7 4.7 %shard_map.84 = (f32[3,8,512]{2,1,0:T(8,128)S(1)}, f32[3,8,512]{2,1,0:T(8,128)S(1)}, f32[3,128,512]{2,1,0:T(8,128)S(1)}) custom-call(s32[2]{0:T(128)S(1)} %pad_add_fusion.refs_0_.place_ref, s32[112]{0:T(128)S(1)} %reshape.3.refs_1_, bf16[4,3,128,128]{3,2,1,0:T(8,128)(2,1)S(1)} %all-to-all-done.1.refs_2_, ...), custom_call_target="tpu_custom_call" | custom-call | tf_op jit(solution)/shard_map/pallas_call | solution.py:57
  69.4 5.8 %collective-permute-done.3.refs_3_ = bf16[4,2,3,128,128]{4,3,2,1,0:T(8,128)(2,1)S(1)} collective-permute-done((bf16[4,2,3,128,128]{4,3,2,1,0:T(8,128)(2,1)}, bf16[4,2,3,128,128]{4,3,2,1,0:T(8,128)(2,1)S(1)}, u32[]{:S(2)}, u32[]{:S(2)}) %collective-permute-start.3) | collective-permute-done | bytes 786464 | tf_op jit(solution)/shard_map/ppermute | solution.py:22
  75.2 1.9 %shard_map.85 = (f32[3,8,512]{2,1,0:T(8,128)S(1)}, f32[3,8,512]{2,1,0:T(8,128)S(1)}, f32[3,128,512]{2,1,0:T(8,128)S(1)}) custom-call(s32[2]{0:T(128)S(1)} %pad_add_fusion.refs_0_.place_ref, s32[112]{0:T(128)S(1)} %reshape.3.refs_1_, bf16[4,3,128,128]{3,2,1,0:T(8,128)(2,1)S(1)} %all-to-all-done.1.refs_2_, ...), custom_call_target="tpu_custom_call" | custom-call | tf_op jit(solution)/shard_map/pallas_call | solution.py:57
  77.0 2.7 %shard_map.86 = bf16[4,3,128,128]{3,2,1,0:T(8,128)(2,1)} custom-call(s32[2]{0:T(128)S(1)} %pad_add_fusion.refs_0_.place_ref, s32[112]{0:T(128)S(1)} %reshape.3.refs_1_, bf16[4,3,128,128]{3,2,1,0:T(8,128)(2,1)S(1)} %all-to-all-done.1.refs_2_, bf16[4,2,3,128,128]{4,3,2,1,0:T(8,128)(2,1)S(1)} %collective-permute-done.1.refs_3_, ...), custom_call_target="tpu_custom_call" | custom-call | tf_op jit(solution)/shard_map/pallas_call | solution.py:57
  79.7 5.0 %all-to-all-start.2 = ((bf16[4,3,128,128]{3,2,1,0:T(8,128)(2,1)}), bf16[4,3,128,128]{3,2,1,0:T(8,128)(2,1)S(1)}, u32[]{:S(2)}, u32[]{:S(2)}) async-start(bf16[4,3,128,128]{3,2,1,0:T(8,128)(2,1)} %shard_map.86), calls=%async_computation.2 | async-start | bytes 786432 | tf_op jit(solution)/shard_map/all_to_all | solution.py:48
  85.4 7.0 %all-to-all-done.2.o_ref = bf16[4,3,128,128]{3,2,1,0:T(8,128)(2,1)S(1)} async-done(((bf16[4,3,128,128]{3,2,1,0:T(8,128)(2,1)}), bf16[4,3,128,128]{3,2,1,0:T(8,128)(2,1)S(1)}, u32[]{:S(2)}, u32[]{:S(2)}) %all-to-all-start.2) | async-done | bytes 393248 | tf_op jit(solution)/shard_map/all_to_all | solution.py:48
  92.4 4.2 %project.1 = bf16[128,1536]{1,0:T(8,128)(2,1)} custom-call(s32[2]{0:T(128)S(1)} %pad_add_fusion.refs_0_.place_ref, s32[1]{0:T(128)S(6)} %copy.11.level_ref, bf16[4,3,128,128]{3,2,1,0:T(8,128)(2,1)S(1)} %all-to-all-done.2.o_ref, bf16[384,1536]{1,0:T(8,128)(2,1)S(1)} %collective-permute-done.6.weight_ref.near_ref, ...), custom_call_target="tpu_custom_call" | custom-call | tf_op jit(solution)/shard_map/project/pallas_call | solution.py:275
  (11 shorter events, 0.0 us)
Async XLA Ops:
  0.0 6.7 %copy-start.1 = (bf16[384,1536]{1,0:T(8,128)(2,1)S(1)}, bf16[384,1536]{1,0:T(8,128)(2,1)}, u32[]{:S(2)}) copy-start(bf16[384,1536]{1,0:T(8,128)(2,1)} %own_hbm.1) | copy-start | bytes 3538948
  2.2 9.6 %copy-start.2 = (s32[1,7,4,4]{1,3,2,0:T(4,128)S(1)}, s32[1,7,4,4]{1,3,2,0:T(4,128)}, u32[]{:S(2)}) copy-start(s32[1,7,4,4]{1,3,2,0:T(4,128)} %param.14) | copy-start | bytes 1348
  2.2 11.2 %copy-start = (bf16[128,1536]{1,0:T(8,128)(2,1)S(1)}, bf16[128,1536]{1,0:T(8,128)(2,1)}, u32[]{:S(2)}) copy-start(bf16[128,1536]{1,0:T(8,128)(2,1)} %query_ref) | copy-start | bytes 1179652
  2.2 18.2 %all-to-all-start = ((bf16[4,2,3,128,128]{4,3,2,1,0:T(8,128)(2,1)}), bf16[4,2,3,128,128]{4,3,2,1,0:T(8,128)(2,1)S(1)}, u32[]{:S(2)}, u32[]{:S(2)}) async-start(bf16[4,2,3,128,128]{4,3,2,1,0:T(8,128)(2,1)} %pack_kv.1), calls=%async_computation | async-start | bytes 1572864 | tf_op jit(solution)/shard_map/all_to_all | solution.py:48
  6.7 31.3 %collective-permute-start.6 = (bf16[384,1536]{1,0:T(8,128)(2,1)S(1)}, bf16[384,1536]{1,0:T(8,128)(2,1)S(1)}, u32[]{:S(2)}, u32[]{:S(2)}) collective-permute-start(bf16[384,1536]{1,0:T(8,128)(2,1)S(1)} %copy-done.1), channel_id=1, source_target_pairs={{1,0},{2,1},{3,2},{0,3},{7,4},{4,5},{5,6},{6,7},{9,8},{10,9},{11,1... | collective-permute-start | bytes 3538952 | tf_op jit(solution)/shard_map/ppermute | solution.py:44
  20.4 12.9 %all-to-all-start.1 = ((bf16[4,3,128,128]{3,2,1,0:T(8,128)(2,1)}), bf16[4,3,128,128]{3,2,1,0:T(8,128)(2,1)S(1)}, u32[]{:S(2)}, u32[]{:S(2)}) async-start(bf16[4,3,128,128]{3,2,1,0:T(8,128)(2,1)} %shard_map.82), calls=%async_computation.1 | async-start | bytes 786432 | tf_op jit(solution)/shard_map/all_to_all | solution.py:48
  23.9 25.0 %collective-permute-start.2 = (bf16[4,2,3,128,128]{4,3,2,1,0:T(8,128)(2,1)S(1)}, bf16[4,2,3,128,128]{4,3,2,1,0:T(8,128)(2,1)}, u32[]{:S(2)}, u32[]{:S(2)}) collective-permute-start(bf16[4,2,3,128,128]{4,3,2,1,0:T(8,128)(2,1)S(1)} %all-to-all-done.refs_3_), channel_id=1, source_target_pairs={{8,0},{16,8},{4,12},{24,16},{12,20},{32,24},{20,28},{40,32},{28,36... | collective-permute-start | bytes 2359304 | tf_op jit(solution)/shard_map/ppermute | solution.py:22
  27.1 23.6 %collective-permute-start = (bf16[4,2,3,128,128]{4,3,2,1,0:T(8,128)(2,1)S(1)}, bf16[4,2,3,128,128]{4,3,2,1,0:T(8,128)(2,1)}, u32[]{:S(2)}, u32[]{:S(2)}) collective-permute-start(bf16[4,2,3,128,128]{4,3,2,1,0:T(8,128)(2,1)S(1)} %all-to-all-done.refs_3_), channel_id=1, source_target_pairs={{12,4},{0,8},{20,12},{8,16},{28,20},{16,24},{36,28},{24,32},{44,36... | collective-permute-start | bytes 2359304 | tf_op jit(solution)/shard_map/ppermute | solution.py:22
  33.3 19.4 %collective-permute-start.5 = (bf16[4,2,3,128,128]{4,3,2,1,0:T(8,128)(2,1)S(1)}, bf16[4,2,3,128,128]{4,3,2,1,0:T(8,128)(2,1)S(1)}, u32[]{:S(2)}, u32[]{:S(2)}) collective-permute-start(bf16[4,2,3,128,128]{4,3,2,1,0:T(8,128)(2,1)S(1)} %all-to-all-done.refs_3_), channel_id=1, source_target_pairs={{4,0},{0,4},{12,8},{8,12},{20,16},{16,20},{28,24},{24,28},{36,32},... | collective-permute-start | bytes 2359304 | tf_op jit(solution)/shard_map/ppermute | solution.py:22
  38.6 21.4 %collective-permute-start.8 = (bf16[384,768]{1,0:T(8,128)(2,1)S(1)}, bf16[384,768]{1,0:T(8,128)(2,1)}, u32[]{:S(2)}, u32[]{:S(2)}) collective-permute-start(bf16[384,768]{1,0:T(8,128)(2,1)S(1)} %shard_map.87), channel_id=1, source_target_pairs={{1,0},{2,1},{3,2},{0,3},{7,4},{4,5},{5,6},{6,7},{9,8},{10,9},{11,1... | collective-permute-start | bytes 1769480 | tf_op jit(solution)/shard_map/ppermute | solution.py:44
  41.5 44.0 %collective-permute-start.7 = (bf16[384,1536]{1,0:T(8,128)(2,1)S(1)}, bf16[384,1536]{1,0:T(8,128)(2,1)S(1)}, u32[]{:S(2)}, u32[]{:S(2)}) collective-permute-start(bf16[384,1536]{1,0:T(8,128)(2,1)S(1)} %collective-permute-done.6.weight_ref.near_ref), channel_id=1, source_target_pairs={{4,0},{0,4},{12,8},{8,12},{20,16},{16,20},{28,24},{24,28},{36,32},... | collective-permute-start | bytes 3538952 | tf_op jit(solution)/shard_map/ppermute | solution.py:22
  48.9 15.8 %collective-permute-start.4 = (bf16[4,2,3,128,128]{4,3,2,1,0:T(8,128)(2,1)}, bf16[4,2,3,128,128]{4,3,2,1,0:T(8,128)(2,1)S(1)}, u32[]{:S(2)}, u32[]{:S(2)}) collective-permute-start(bf16[4,2,3,128,128]{4,3,2,1,0:T(8,128)(2,1)} %collective-permute-done.2.refs_3_), channel_id=1, source_target_pairs={{4,0},{0,4},{12,8},{8,12},{20,16},{16,20},{28,24},{24,28},{36,32},... | collective-permute-start | bytes 2359304 | tf_op jit(solution)/shard_map/ppermute | solution.py:22
  50.8 24.4 %collective-permute-start.3 = (bf16[4,2,3,128,128]{4,3,2,1,0:T(8,128)(2,1)}, bf16[4,2,3,128,128]{4,3,2,1,0:T(8,128)(2,1)S(1)}, u32[]{:S(2)}, u32[]{:S(2)}) collective-permute-start(bf16[4,2,3,128,128]{4,3,2,1,0:T(8,128)(2,1)} %collective-permute-done.2.refs_3_), channel_id=1, source_target_pairs={{8,0},{16,8},{4,12},{24,16},{12,20},{32,24},{20,28},{40,32},{28,36... | collective-permute-start | bytes 2359304 | tf_op jit(solution)/shard_map/ppermute | solution.py:22
  52.7 24.3 %collective-permute-start.1 = (bf16[4,2,3,128,128]{4,3,2,1,0:T(8,128)(2,1)}, bf16[4,2,3,128,128]{4,3,2,1,0:T(8,128)(2,1)S(1)}, u32[]{:S(2)}, u32[]{:S(2)}) collective-permute-start(bf16[4,2,3,128,128]{4,3,2,1,0:T(8,128)(2,1)} %collective-permute-done.refs_5_), channel_id=1, source_target_pairs={{12,4},{0,8},{20,12},{8,16},{28,20},{16,24},{36,28},{24,32},{44,36... | collective-permute-start | bytes 2359304 | tf_op jit(solution)/shard_map/ppermute | solution.py:22
  60.0 25.4 %collective-permute-start.9 = (bf16[384,768]{1,0:T(8,128)(2,1)}, bf16[384,768]{1,0:T(8,128)(2,1)}, u32[]{:S(2)}, u32[]{:S(2)}) collective-permute-start(bf16[384,768]{1,0:T(8,128)(2,1)} %collective-permute-done.8.mine_hbm), channel_id=1, source_target_pairs={{4,0},{0,4},{12,8},{8,12},{20,16},{16,20},{28,24},{24,28},{36,32},... | collective-permute-start | bytes 1769480 | tf_op jit(solution)/shard_map/ppermute | solution.py:22
  79.7 12.7 %all-to-all-start.2 = ((bf16[4,3,128,128]{3,2,1,0:T(8,128)(2,1)}), bf16[4,3,128,128]{3,2,1,0:T(8,128)(2,1)S(1)}, u32[]{:S(2)}, u32[]{:S(2)}) async-start(bf16[4,3,128,128]{3,2,1,0:T(8,128)(2,1)} %shard_map.86), calls=%async_computation.2 | async-start | bytes 786432 | tf_op jit(solution)/shard_map/all_to_all | solution.py:48
